TPU v7x, 256 devices: a whole 4x4x8 slice. The times are simulated.
256 devices in a mesh: row: 8 (over z), col: 16 (over x_hi, y, core), rep: 2 (over x_lo).
Axes of the slice: x: 4 (x_hi: 2, x_lo: 2; x = x_hi * 2 + x_lo), y: 4, z: 8, core: 2. Of those that a mesh axis runs over, the one named last changes fastest.
Arguments:
- amplitudes: bfloat16 [8192, 8192], P('row', 'col'), may hold values from -6 to 6
- intermediate: bfloat16 [8192, 8192], P('row', 'col'), may hold values from -0.0625 to 0.0625
Outputs:
- residual: float32 [16, 16, 32, 8192], P(None, 'col', None, ('row', 'rep'))
All inputs are finite; a program needn't handle non-finite values.
Results may differ from a plain program's by a relative error of at most 0.0029.
Values may be sent and summed in bfloat16 or wider, within the bound.
No kernel may reach another device: no remote copies, remote signals or barrier semaphores. Data moves between devices by JAX's collectives and lax.ppermute only.
A program may use at most 128 MiB of HBM per device.

v0:
```python
import jax
import jax.numpy as jnp
from jax import lax
from jax.sharding import PartitionSpec as P


def local(amplitudes, intermediate):
    rows_axis = lax.axis_size("row")
    cols_axis = lax.axis_size("col")
    depth_axis = lax.axis_size("rep")
    layer_index = lax.axis_index("rep")
    owner_rows = rows_axis * depth_axis
    fold_count = owner_rows // cols_axis
    local_rows = amplitudes.shape[0]
    band_rows = local_rows // depth_axis
    local_cols = intermediate.shape[1]
    slice_width = local_cols // owner_rows
    own_rows = lax.dynamic_slice_in_dim(amplitudes, layer_index * band_rows, band_rows, 0)
    all_weights = lax.all_gather(intermediate, "row", axis=0, tiled=True)
    summed = jnp.dot(
        lax.all_gather(own_rows, "col", axis=1, tiled=True),
        all_weights,
        preferred_element_type=jnp.float32,
    )
    cycle = summed.astype(jnp.bfloat16)
    spread_block = cycle.reshape(band_rows, fold_count, cols_axis, slice_width)
    direct = lax.all_to_all(spread_block, "col", split_axis=2, concat_axis=1, tiled=True).reshape(
        band_rows, owner_rows, slice_width
    )
    stacked = cycle.reshape(cols_axis, slice_width, fold_count, cols_axis * slice_width)
    mirror = lax.all_to_all(
        lax.all_to_all(stacked, "col", split_axis=0, concat_axis=2, tiled=True),
        ("row", "rep"),
        split_axis=2,
        concat_axis=0,
        tiled=True,
    )
    mirror_part = mirror.reshape(owner_rows, slice_width, band_rows).astype(jnp.float32)
    direct_part = jnp.transpose(direct, (1, 2, 0)).astype(jnp.float32)
    return (mirror_part + direct_part).reshape(owner_rows, 1, slice_width, band_rows)


def solution(mesh):
    in_specs = (P("row", "col"), P("row", "col"))
    out_specs = P(None, "col", None, ("row", "rep"))
    return jax.shard_map(local, mesh=mesh, in_specs=in_specs, out_specs=out_specs, check_vma=False)
```

profile of v0, /device:TPU:1, one launch (start us, length us, event | category | flops | bytes accessed | tf_op | source)
XLA Modules:
  0.0 261.0 jit_solution(2352553779667338768)
XLA Ops:
  6.5 0.0 copy-start
  6.5 0.0 all-gather.5.cloned.1.call-start
  6.5 0.7 all-gather.5.cloned.1.call-update
  7.3 0.0 all-gather.3.cloned.1.call-start
  7.3 0.5 copy-done
  7.8 0.8 constant_dynamic-slice_fusion
  8.6 0.0 all-gather.3.cloned.1.call-update
  8.6 98.5 %all-gather.5.cloned.1.call-done = bf16[8192,512]{1,0:T(8,128)(2,1)} async-done(((bf16[1024,512]{1,0:T(8,128)(2,1)}), bf16[8192,512]{1,0:T(8,128)(2,1)}) %all-gather.5.cloned.1.call-update) | async-done | bytes 8388624 | tf_op jit(solution)/shard_map/all_gather | solution.py:19
  107.1 83.7 %all-gather.3.cloned.1.call-done = bf16[512,8192]{1,0:T(8,128)(2,1)} async-done(((bf16[512,512]{1,0:T(8,128)(2,1)}), bf16[512,8192]{1,0:T(8,128)(2,1)}) %all-gather.3.cloned.1.call-update) | async-done | bytes 8388624 | tf_op jit(solution)/shard_map/all_gather | solution.py:21
  190.9 10.2 %convolution_convert_fusion = bf16[512,512]{1,0:T(8,128)(2,1)S(1)} fusion(bf16[512,8192]{1,0:T(8,128)(2,1)} %all-gather.3.cloned.1.call-done, bf16[8192,512]{1,0:T(8,128)(2,1)} %all-gather.5.cloned.1.call-done), kind=kOutput, calls=%fused_computation | convolution fusion | flops 4295229440 | bytes 17301504 | tf_op jit(solution)/shard_map/dot_general | solution.py:20
  201.1 0.2 copy.8
  201.3 14.1 %all_to_all.36 = bf16[512,1,16,32]{0,3,1,2:T(8,128)(2,1)S(1)} all-to-all(bf16[512,1,16,32]{0,3,1,2:T(8,128)(2,1)S(1)} %bitcast.39), channel_id=1, replica_groups=mesh['row'=8,'col'=16,'rep'=2] {'col'}, dimensions={2} | all-to-all | bytes 1048576 | tf_op jit(solution)/shard_map/all_to_all | solution.py:27
  215.4 15.0 %all_to_all.37 = bf16[16,32,1,512]{3,1,2,0:T(8,128)(2,1)S(1)} all-to-all(bf16[16,32,1,512]{3,1,2,0:T(8,128)(2,1)S(1)} %bitcast.37), channel_id=1, replica_groups=mesh['row'=8,'col'=16,'rep'=2] {'col'}, dimensions={0} | all-to-all | bytes 1048576 | tf_op jit(solution)/shard_map/all_to_all | solution.py:32
  230.4 22.7 %all_to_all.38 = bf16[1,32,16,512]{3,1,0,2:T(8,128)(2,1)S(1)} all-to-all(bf16[1,32,16,512]{3,1,0,2:T(8,128)(2,1)S(1)} %bitcast.38), channel_id=1, replica_groups=mesh['row'=8,'col'=16,'rep'=2] {'row','rep'}, dimensions={2} | all-to-all | bytes 1048576 | tf_op jit(solution)/shard_map/all_to_all | solution.py:31
  253.1 1.1 fusion.1
Async XLA Ops:
  6.5 1.2 copy-start
  6.5 100.6 %all-gather.5.cloned.1.call-start = ((), (), s32[]{:S(2)}) async-start(), calls=%async_computation.4 | async-start | bytes 9437184 | tf_op jit(solution)/shard_map/all_gather | solution.py:19
  7.3 183.6 %all-gather.3.cloned.1.call-start = ((), (), s32[]{:S(2)}) async-start(), calls=%async_computation.3 | async-start | bytes 8912896 | tf_op jit(solution)/shard_map/all_gather | solution.py:21
Sparse Core Ops, SparseCore 0:
  9.1 97.9 all-gather.4
  109.7 81.1 all-gather.2
where the time goes:
time: 262 us; the launch traced here: 261 us
  waiting for transfers between devices  183 us (70%)
  blocking collectives  51.7 us (20%)
  between operations  13.4 us (5%)
  matrix products  10.2 us (4%)
    all_gather x1, waiting for transfers between devices, local(): all_weights = lax.all_gather(intermediate, 'row', axis=0, tiled=True)  98.5 us
    all_gather x1, waiting for transfers between devices, local(): lax.all_gather(own_rows, 'col', axis=1, tiled=True)  83.7 us
    all_to_all x1, blocking collectives, local(): lax.all_to_all(lax.all_to_all(stacked, 'col', split_axis=0, concat_axis=2...  22.7 us
    all_to_all x1, blocking collectives, local(): lax.all_to_all(stacked, 'col', split_axis=0, concat_axis=2, tiled=True)  15 us
    all_to_all x1, blocking collectives, local(): lax.all_to_all(spread_block, 'col', split_axis=2, concat_axis=1, tiled=True)  14.1 us
    dot_general x1, matrix products, local(): jnp.dot(lax.all_gather(own_rows, 'col', axis=1, tiled=True), all_weights,...  10.2 us
  transfers between devices with their start and end apart: 2, of which 2 were waited for; matrix products, arithmetic and copies ran while one was open for 0% of the time, Pallas kernels for 0%

commit v1 on v0

v1 whole, which is shorter than its diff:
```python
import functools

import jax
import jax.numpy as jnp
import numpy as np
from jax import lax
from jax.experimental import pallas as pl
from jax.experimental.pallas import tpu as pltpu
from jax.sharding import Mesh, PartitionSpec as P

AXES = ("row", "xh", "y", "core", "rep")
F32, BF16 = jnp.float32, jnp.bfloat16
X_LINE = ("xh", "rep")
PAIR = [(0, 1), (1, 0), (2, 3), (3, 2)]
CROSS = [(0, 3), (3, 0), (1, 2), (2, 1)]
B = 512


def call(body, outs, n_scalar, n_in, flops=0, moved=0, scratch=()):
    vmem = pl.BlockSpec(memory_space=pltpu.VMEM)
    smem = pl.BlockSpec(memory_space=pltpu.SMEM)
    return pl.pallas_call(
        body,
        out_shape=outs,
        in_specs=[smem] * n_scalar + [vmem] * n_in,
        out_specs=[vmem] * len(outs),
        scratch_shapes=list(scratch),
        compiler_params=pltpu.CompilerParams(vmem_limit_bytes=48 << 20),
        cost_estimate=pl.CostEstimate(flops=flops, bytes_accessed=moved, transcendentals=0),
    )


def lane_block(shape):
    return lax.broadcasted_iota(jnp.int32, shape, len(shape) - 1) // 32


def turn(parts):
    block = lane_block(parts[0].shape)
    out = []
    for j in range(4):
        rolled = [pltpu.roll(p, ((i - j) * 32) % 128, 1) if i != j else p for i, p in enumerate(parts)]
        out.append(
            jnp.where(
                block < 2, jnp.where(block == 0, rolled[0], rolled[1]), jnp.where(block == 2, rolled[2], rolled[3])
            )
        )
    return out


def w_pack(rep_ref, w_ref, out_ref):
    rep = rep_ref[0]
    for half in range(2):
        for g in range(4):
            parts = []
            for hi in range(4):
                v = w_ref[half * B + hi * 128 : half * B + (hi + 1) * 128, g * 128 : (g + 1) * 128].astype(F32)
                parts.append(jnp.where(rep == 0, v, pltpu.roll(v, 96, 1)))
            turned = turn(parts)
            for j in (0, 2):
                out_ref[g * 2 + j // 2, half] = turned[j].astype(BF16)


def w_unpack(in_ref, out_ref):
    for g in range(4):
        turned = turn([in_ref[4 * g + j].astype(F32) for j in range(4)])
        for hi in range(4):
            out_ref[hi * 128 : (hi + 1) * 128, g * 128 : (g + 1) * 128] = turned[hi].astype(BF16)


def dot(a, b):
    return jnp.dot(a, b, preferred_element_type=F32)


def product_early(slots, pos_ref, w_ref, *refs):
    pieces, (first_ref, second_ref) = refs[: len(slots)], refs[len(slots) :]
    for which, out_ref in ((0, first_ref), (1, second_ref)):
        total = None
        for (half, p), piece in zip(slots, pieces):
            if half == which:
                term = dot(piece[...], w_ref[pos_ref[p]])
                total = term if total is None else total + term
        out_ref[...] = total


def product_late(early, late, pos_ref, keep_ref, first_in, second_in, w_ref, top_ref, bottom_ref, *refs):
    old, new = refs[: len(early)], refs[len(early) : len(early) + len(late)]
    kept_ref, sent_ref, far_ref, sums = refs[len(early) + len(late) :]
    far_ref[:256] = top_ref[...]
    far_ref[256:] = bottom_ref[...]
    sums[0] = first_in[...]
    sums[1] = second_in[...]
    for (half, p), piece in zip(early, old):

        @pl.when(pos_ref[p] == 4)
        def _(half=half, piece=piece):
            sums[half] += dot(piece[...], far_ref[...])

    for (half, p), piece in zip(late, new):

        @pl.when(pos_ref[p] == 4)
        def _(half=half, piece=piece):
            sums[half] += dot(piece[...], far_ref[...])

        @pl.when(pos_ref[p] != 4)
        def _(half=half, p=p, piece=piece):
            sums[half] += dot(piece[...], w_ref[pos_ref[p]])

    keep = keep_ref[0]
    kept_ref[...] = sums[keep]
    sent_ref[...] = sums[1 - keep]


def spread(kept_ref, got_ref, direct_ref, mirror_ref):
    cycle = (kept_ref[...] + got_ref[...]).astype(BF16).astype(F32)
    direct_ref[...] = cycle.T.astype(BF16)
    split = cycle.reshape(16, 4, 8, B)
    for g in range(4):
        parts = [split[:, hi, :, g * 128 : (g + 1) * 128].reshape(128, 128) for hi in range(4)]
        for j, t in enumerate(turn(parts)):
            mirror_ref[2 * g + j // 2, :, j % 2] = t.reshape(16, 8, 128).astype(BF16)


def finish(direct_ref, mirror_ref, out_ref):
    for owner in range(16):
        z, core = owner // 2, owner % 2
        for g in range(4):
            parts = [mirror_ref[z, 2 * g + j // 2, core, j % 2].astype(F32) for j in range(4)]
            for hi, t in enumerate(turn(parts)):
                rows = slice(owner * 32 + hi * 8, owner * 32 + hi * 8 + 8)
                lanes = slice(g * 128, (g + 1) * 128)
                out_ref[rows, lanes] = t + direct_ref[rows, lanes].astype(F32)


def ring(n, step):
    return [(i, (i + step) % n) for i in range(n)]


def after(x, *others):
    return lax.optimization_barrier((x, *others))[0]


def local(amplitudes, intermediate):
    z, xh, y, core, rep = (lax.axis_index(a) for a in AXES)
    shape = jax.ShapeDtypeStruct
    up = lambda v, axis, n: lax.ppermute(v, axis, ring(n, -1))
    down = lambda v, axis, n: lax.ppermute(v, axis, ring(n, 1))
    pair = lambda v: lax.ppermute(v, X_LINE, PAIR)
    cross = lambda v: lax.ppermute(v, X_LINE, CROSS)

    packed = call(w_pack, [shape((8, 2, 128, 128), BF16)], 1, 1, moved=2 << 20)(
        rep.reshape(1).astype(jnp.int32), intermediate
    )[0]
    arrived = lax.all_to_all(packed.reshape(16, 128, 128), ("xh", "y", "core"), split_axis=0, concat_axis=0, tiled=True)
    w = {0: call(w_unpack, [shape((B, B), BF16)], 0, 1, moved=1 << 20)(arrived)[0]}

    f = {(0, 0): lax.dynamic_slice_in_dim(amplitudes, rep * B, B, 0)}
    g = {(0, 0): lax.dynamic_slice_in_dim(amplitudes, (1 - rep) * B, B, 0)}
    f[0, 1] = up(f[0, 0], "y", 4)
    f[0, 3] = down(f[0, 0], "y", 4)
    f[1, 0] = cross(g[0, 0])
    w[1], w[7] = up(w[0], "row", 8), down(w[0], "row", 8)
    f[0, 2] = up(f[0, 1], "y", 4)
    f[1, 3] = down(f[1, 0], "y", 4)
    g[0, 1] = pair(f[0, 1])
    g[1, 0] = cross(after(f[0, 0], f[1, 0]))
    w[2], w[6] = up(w[1], "row", 8), down(w[7], "row", 8)
    f[1, 1] = up(after(f[1, 0], f[0, 2]), "y", 4)
    f[1, 2] = down(f[1, 3], "y", 4)
    g[0, 3] = pair(after(f[0, 3], g[0, 1]))
    g[1, 1] = cross(after(f[0, 1], g[1, 0]))
    w[3], w[5] = up(w[2], "row", 8), down(w[6], "row", 8)
    g[0, 2] = pair(after(f[0, 2], g[0, 3]))
    g[1, 2] = cross(after(f[0, 2], g[1, 1]))
    g[1, 3] = down(after(g[1, 0], f[1, 2]), "y", 4)
    top, bottom = up(w[3][:256], "row", 8), down(w[5][256:], "row", 8)

    spots = [(i, j) for i in range(2) for j in range(4)]
    position = jnp.stack(
        [(4 * lax.rem(xh + i, 2) + lax.rem(y + j, 4) - z + 8) % 8 for i, j in spots]
    ).astype(jnp.int32)
    late = [(1, spots.index(s)) for s in ((0, 2), (1, 2), (1, 3))]
    early = [(h, p) for h in range(2) for p in range(8) if (h, p) not in late]
    piece = lambda h, p: (f, g)[h][spots[p]]
    stack = jnp.stack([w[0], w[1], w[2], w[3], jnp.zeros((B, B), BF16), w[5], w[6], w[7]])
    old = [piece(*e) for e in early]
    first, second = call(
        functools.partial(product_early, early),
        [shape((B, B), F32)] * 2,
        1,
        1 + len(early),
        flops=2 * B**3 * len(early),
        moved=12 << 20,
    )(position, stack, *old)
    kept, sent = call(
        functools.partial(product_late, early, late),
        [shape((B, B), F32)] * 2,
        2,
        5 + 16,
        flops=2 * B**3 * 5,
        moved=8 << 20,
        scratch=[pltpu.VMEM((B, B), BF16), pltpu.VMEM((2, B, B), F32)],
    )(
        position,
        (core ^ rep).reshape(1).astype(jnp.int32),
        first,
        second,
        stack,
        top,
        bottom,
        *old,
        *[piece(*e) for e in late],
    )
    got = lax.ppermute(sent, "core", [(0, 1), (1, 0)])
    direct, mirror = call(
        spread, [shape((B, B), BF16), shape((8, 16, 2, 8, 128), BF16)], 0, 2, moved=3 << 20
    )(kept, got)
    direct = lax.ppermute(direct, ("core", "rep"), [(0, 0), (1, 2), (2, 1), (3, 3)])
    mirror = lax.all_to_all(mirror.reshape(256, 8, 128), AXES, split_axis=0, concat_axis=0, tiled=True)
    out = call(finish, [shape((B, B), F32)], 0, 2, moved=2 << 20)(direct, mirror.reshape(8, 8, 2, 2, 8, 128))[0]
    return out.reshape(16, 1, 32, B)


def solution(mesh):
    fine = Mesh(np.asarray(mesh.devices).reshape(8, 2, 4, 2, 2), AXES)
    block = P("row", ("xh", "y", "core"))
    out = P(None, ("xh", "y", "core"), None, ("row", "rep"))
    return jax.shard_map(local, mesh=fine, in_specs=(block, block), out_specs=out, check_vma=False)
```

time: 262 us -> 138 us (0.53)
  waiting for transfers between devices: 183 us -> 56.5 us
  blocking collectives: 51.7 us -> 0 us
  starting transfers between devices: 0.04 us -> 49.2 us
  Pallas kernels: 0 us -> 20.9 us
  between operations: 13.4 us -> 0.22 us
  matrix products: 10.2 us -> 0 us
  local copies, waits for them, and re-layouts: 1.49 us -> 10.6 us
    all_gather x2 -> x0, waiting for transfers between devices: 182 us -> none  [the longest x1 98.5 us: local(): all_weights = lax.all_gather(intermediate, 'row', axis=0, tiled=True)]
    all_to_all x3 -> x0, blocking collectives: 51.7 us -> none  [the longest x1 22.7 us: local(): lax.all_to_all(lax.all_to_all(stacked, 'col', split_axis=0, concat_axis=2...]
    ppermute x0 -> x24, waiting for transfers between devices: none -> 46.3 us  [the longest x8 20.5 us: local(): down = lambda v, axis, n: lax.ppermute(v, axis, ring(n, 1))]
    ppermute x0 -> x24, starting transfers between devices: none -> 32 us  [the longest x7 17.4 us: local(): up = lambda v, axis, n: lax.ppermute(v, axis, ring(n, -1))]
    pallas_call x0 -> x6, Pallas kernels: none -> 20.9 us  [the longest x1 8.04 us: local(): call(functools.partial(product_late, early, late), [shape((B, B), F32)] *...]
    all_to_all x0 -> x2, starting transfers between devices: none -> 17.1 us  [the longest x1 8.67 us: local(): lax.all_to_all(mirror.reshape(256, 8, 128), AXES, split_axis=0, concat_ax...]
    dot_general x1 -> x0, matrix products: 10.2 us -> none  [local(): jnp.dot(lax.all_gather(own_rows, 'col', axis=1, tiled=True), all_weights,...]
    all_to_all x0 -> x2, waiting for transfers between devices: none -> 10.2 us  [the longest x1 5.18 us: local(): lax.all_to_all(mirror.reshape(256, 8, 128), AXES, split_axis=0, concat_ax...]
  transfers between devices with their start and end apart: 2 -> 26, of which waited for: 2 -> 13; matrix products, arithmetic and copies ran while one was open for 0% -> 4% of each run, Pallas kernels for 0% -> 6%
where the time goes in v1:
time: 138 us; the launch traced here: 137 us
  waiting for transfers between devices  56.5 us (41%)
  starting transfers between devices  49.2 us (36%)
  Pallas kernels  20.9 us (15%)
  local copies, waits for them, and re-layouts  10.6 us (8%)
    ppermute x8, waiting for transfers between devices, local(): down = lambda v, axis, n: lax.ppermute(v, axis, ring(n, 1))  20.5 us
    ppermute x7, starting transfers between devices, local(): up = lambda v, axis, n: lax.ppermute(v, axis, ring(n, -1))  17.4 us
    ppermute x1, waiting for transfers between devices, local(): lax.ppermute(direct, ('core', 'rep'), [(0, 0), (1, 2), (2, 1), (3, 3)])  11.2 us
    all_to_all x1, starting transfers between devices, local(): lax.all_to_all(mirror.reshape(256, 8, 128), AXES, split_axis=0, concat_ax...  8.67 us
    all_to_all x1, starting transfers between devices, local(): lax.all_to_all(packed.reshape(16, 128, 128), ('xh', 'y', 'core'), split_a...  8.45 us
    unnamed x25, local copies, waits for them, and re-layouts  8.12 us
    pallas_call x1, Pallas kernels, local(): call(functools.partial(product_late, early, late), [shape((B, B), F32)] *...  8.04 us
    pallas_call x1, Pallas kernels, local(): call(functools.partial(product_early, early), [shape((B, B), F32)] * 2, 1...  7.61 us
  transfers between devices with their start and end apart: 26, of which 13 were waited for; matrix products, arithmetic and copies ran while one was open for 4% of the time, Pallas kernels for 6%

profile of v1, /device:TPU:1, one launch (start us, length us, event | category | flops | bytes accessed | tf_op | source)
XLA Modules:
  0.0 137.4 jit_solution(1870003894302777251)
XLA Ops:
  0.0 1.2 copy-done
  1.2 1.9 %shard_map.28 = bf16[8,2,128,128]{3,2,1,0:T(8,128)(2,1)} custom-call(s32[1]{0:T(128)} %bitcast.9.rep_ref, bf16[1024,512]{1,0:T(8,128)(2,1)S(1)} %copy-done), custom_call_target="tpu_custom_call" | custom-call | bytes 2097152 | tf_op jit(solution)/shard_map/pallas_call | solution.py:150
  3.1 8.4 %all-to-all-start = ((bf16[16,128,128]{2,1,0:T(8,128)(2,1)}), bf16[16,128,128]{2,1,0:T(8,128)(2,1)S(1)}, u32[]{:S(2)}, u32[]{:S(2)}) async-start(bf16[16,128,128]{2,1,0:T(8,128)(2,1)} %bitcast.10), calls=%async_computation | async-start | bytes 1048576 | tf_op jit(solution)/shard_map/all_to_all | solution.py:153
  11.6 1.3 constant_dynamic-slice_fusion
  12.9 2.7 %collective-permute-start.9 = (bf16[512,512]{1,0:T(8,128)(2,1)S(1)}, bf16[512,512]{1,0:T(8,128)(2,1)S(1)}, u32[]{:S(2)}, u32[]{:S(2)}) collective-permute-start(bf16[512,512]{1,0:T(8,128)(2,1)S(1)} %get-tuple-element.31.refs_8_), channel_id=1, source_target_pairs={{0,17},{17,0},{1,16},{16,1},{2,19},{19,2},{3,18},{18,3},{4,21},{21... | collective-permute-start | bytes 1572872 | tf_op jit(solution)/shard_map/ppermute | solution.py:148
  15.6 2.4 %collective-permute-start.6 = (bf16[512,512]{1,0:T(8,128)(2,1)S(1)}, bf16[512,512]{1,0:T(8,128)(2,1)S(1)}, u32[]{:S(2)}, u32[]{:S(2)}) collective-permute-start(bf16[512,512]{1,0:T(8,128)(2,1)S(1)} %get-tuple-element.20.refs_0_), channel_id=1, source_target_pairs={{0,12},{4,0},{8,4},{12,8},{1,13},{5,1},{9,5},{13,9},{2,14},{6,2},{... | collective-permute-start | bytes 1572872 | tf_op jit(solution)/shard_map/ppermute | solution.py:145
  18.0 0.0 collective-permute-start.8
  18.0 5.0 %all-to-all-done.in_ref = bf16[16,128,128]{2,1,0:T(8,128)(2,1)S(1)} async-done(((bf16[16,128,128]{2,1,0:T(8,128)(2,1)}), bf16[16,128,128]{2,1,0:T(8,128)(2,1)S(1)}, u32[]{:S(2)}, u32[]{:S(2)}) %all-to-all-start) | async-done | bytes 524320 | tf_op jit(solution)/shard_map/all_to_all | solution.py:153
  23.0 0.5 shard_map.29
  23.5 5.7 %collective-permute-start = (bf16[512,512]{1,0:T(8,128)(2,1)S(1)}, bf16[512,512]{1,0:T(8,128)(2,1)}, u32[]{:S(2)}, u32[]{:S(2)}) collective-permute-start(bf16[512,512]{1,0:T(8,128)(2,1)S(1)} %shard_map.29), channel_id=1, source_target_pairs={{0,224},{32,0},{64,32},{96,64},{128,96},{160,128},{192,160},{224,1... | collective-permute-start | bytes 1572872 | tf_op jit(solution)/shard_map/ppermute | solution.py:145
  29.1 0.0 collective-permute-start.3
  29.1 3.7 %collective-permute-done.9.refs_4_ = bf16[512,512]{1,0:T(8,128)(2,1)S(1)} collective-permute-done((bf16[512,512]{1,0:T(8,128)(2,1)S(1)}, bf16[512,512]{1,0:T(8,128)(2,1)S(1)}, u32[]{:S(2)}, u32[]{:S(2)}) %collective-permute-start.9) | collective-permute-done | bytes 524320 | tf_op jit(solution)/shard_map/ppermute | solution.py:148
  32.8 0.0 collective-permute-start.15
  32.8 0.0 collective-permute-done.6.refs_1_
  32.8 0.3 collective-permute-start.13
  33.2 0.2 collective-permute-done.8.refs_3_
  33.4 2.2 %collective-permute-start.7 = (bf16[512,512]{1,0:T(8,128)(2,1)S(1)}, bf16[512,512]{1,0:T(8,128)(2,1)}, u32[]{:S(2)}, u32[]{:S(2)}) collective-permute-start(bf16[512,512]{1,0:T(8,128)(2,1)S(1)} %collective-permute-done.6.refs_1_), channel_id=1, source_target_pairs={{0,12},{4,0},{8,4},{12,8},{1,13},{5,1},{9,5},{13,9},{2,14},{6,2},{... | collective-permute-start | bytes 1572872 | tf_op jit(solution)/shard_map/ppermute | solution.py:145
  35.6 3.6 %collective-permute-done = bf16[512,512]{1,0:T(8,128)(2,1)} collective-permute-done((bf16[512,512]{1,0:T(8,128)(2,1)S(1)}, bf16[512,512]{1,0:T(8,128)(2,1)}, u32[]{:S(2)}, u32[]{:S(2)}) %collective-permute-start) | collective-permute-done | bytes 524320 | tf_op jit(solution)/shard_map/ppermute | solution.py:145
  39.1 1.1 collective-permute-start.11
  40.2 2.1 %collective-permute-done.3 = bf16[512,512]{1,0:T(8,128)(2,1)} collective-permute-done((bf16[512,512]{1,0:T(8,128)(2,1)S(1)}, bf16[512,512]{1,0:T(8,128)(2,1)}, u32[]{:S(2)}, u32[]{:S(2)}) %collective-permute-start.3) | collective-permute-done | bytes 524320 | tf_op jit(solution)/shard_map/ppermute | solution.py:146
  42.4 1.4 %collective-permute-start.1 = (bf16[512,512]{1,0:T(8,128)(2,1)}, bf16[512,512]{1,0:T(8,128)(2,1)}, u32[]{:S(2)}, u32[]{:S(2)}) collective-permute-start(bf16[512,512]{1,0:T(8,128)(2,1)} %collective-permute-done), channel_id=1, source_target_pairs={{0,224},{32,0},{64,32},{96,64},{128,96},{160,128},{192,160},{224,1... | collective-permute-start | bytes 1572872 | tf_op jit(solution)/shard_map/ppermute | solution.py:145
  43.8 3.6 %collective-permute-done.15.refs_11_ = bf16[512,512]{1,0:T(8,128)(2,1)S(1)} collective-permute-done((bf16[512,512]{1,0:T(8,128)(2,1)S(1)}, bf16[512,512]{1,0:T(8,128)(2,1)S(1)}, u32[]{:S(2)}, u32[]{:S(2)}) %collective-permute-start.15) | collective-permute-done | bytes 524320 | tf_op jit(solution)/shard_map/ppermute | solution.py:148
  47.3 0.8 copy-done.4
  48.1 1.6 %collective-permute-start.4 = (bf16[512,512]{1,0:T(8,128)(2,1)}, bf16[512,512]{1,0:T(8,128)(2,1)}, u32[]{:S(2)}, u32[]{:S(2)}) collective-permute-start(bf16[512,512]{1,0:T(8,128)(2,1)} %collective-permute-done.3), channel_id=1, source_target_pairs={{0,32},{32,64},{64,96},{96,128},{128,160},{160,192},{192,224},{224... | collective-permute-start | bytes 1572872 | tf_op jit(solution)/shard_map/ppermute | solution.py:146
  49.8 0.1 stack.59.pos_ref
  49.8 0.3 collective-permute-start.16
  50.1 0.0 collective-permute-done.7.refs_2_
  50.2 2.4 %collective-permute-done.11.refs_7_ = bf16[512,512]{1,0:T(8,128)(2,1)} collective-permute-done((bf16[512,512]{1,0:T(8,128)(2,1)S(1)}, bf16[512,512]{1,0:T(8,128)(2,1)}, u32[]{:S(2)}, u32[]{:S(2)}) %collective-permute-start.11) | collective-permute-done | bytes 524320 | tf_op jit(solution)/shard_map/ppermute | solution.py:146
  52.6 0.5 collective-permute-start.12
  53.0 1.2 collective-permute-done.1
  54.3 3.4 %collective-permute-start.2 = (bf16[512,512]{1,0:T(8,128)(2,1)}, bf16[512,512]{1,0:T(8,128)(2,1)S(1)}, u32[]{:S(2)}, u32[]{:S(2)}) collective-permute-start(bf16[512,512]{1,0:T(8,128)(2,1)} %collective-permute-done.1), channel_id=1, source_target_pairs={{0,224},{32,0},{64,32},{96,64},{128,96},{160,128},{192,160},{224,1... | collective-permute-start | bytes 1572872 | tf_op jit(solution)/shard_map/ppermute | solution.py:145
  57.7 1.1 bitcast_dynamic-update-slice_fusion.5
  58.8 6.4 %collective-permute-done.4 = bf16[512,512]{1,0:T(8,128)(2,1)} collective-permute-done((bf16[512,512]{1,0:T(8,128)(2,1)}, bf16[512,512]{1,0:T(8,128)(2,1)}, u32[]{:S(2)}, u32[]{:S(2)}) %collective-permute-start.4) | collective-permute-done | bytes 524320 | tf_op jit(solution)/shard_map/ppermute | solution.py:146
  65.2 0.0 collective-permute-start.5
  65.2 1.1 bitcast_dynamic-update-slice_fusion.4
  66.3 2.4 %collective-permute-start.10 = (bf16[512,512]{1,0:T(8,128)(2,1)S(1)}, bf16[512,512]{1,0:T(8,128)(2,1)S(1)}, u32[]{:S(2)}, u32[]{:S(2)}) collective-permute-start(bf16[512,512]{1,0:T(8,128)(2,1)S(1)} %collective-permute-done.9.refs_4_), channel_id=1, source_target_pairs={{0,12},{4,0},{8,4},{12,8},{1,13},{5,1},{9,5},{13,9},{2,14},{6,2},{... | collective-permute-start | bytes 1572872 | tf_op jit(solution)/shard_map/ppermute | solution.py:145
  68.7 0.0 collective-permute-done.14.refs_10_
  68.7 0.0 collective-permute-start.20
  68.7 0.0 collective-permute-done.12.refs_6_
  68.7 0.1 collective-permute-start.19
  68.8 0.0 collective-permute-done.2
  68.8 0.1 collective-permute-start.21
  69.0 9.3 %collective-permute-done.5 = bf16[512,512]{1,0:T(8,128)(2,1)S(1)} collective-permute-done((bf16[512,512]{1,0:T(8,128)(2,1)}, bf16[512,512]{1,0:T(8,128)(2,1)S(1)}, u32[]{:S(2)}, u32[]{:S(2)}) %collective-permute-start.5) | collective-permute-done | bytes 524320 | tf_op jit(solution)/shard_map/ppermute | solution.py:146
  78.4 0.0 collective-permute-start.17
  78.5 1.1 bitcast_dynamic-update-slice_fusion.1
  79.5 1.1 bitcast_dynamic-update-slice_fusion.w_ref
  80.6 0.0 collective-permute-done.10.refs_5_
  80.6 1.5 %collective-permute-start.18 = (bf16[256,512]{1,0:T(8,128)(2,1)S(1)}, bf16[256,512]{1,0:T(8,128)(2,1)S(1)}, u32[]{:S(2)}, u32[]{:S(2)}) collective-permute-start(bf16[256,512]{1,0:T(8,128)(2,1)S(1)} %slice.9), channel_id=1, source_target_pairs={{0,32},{32,64},{64,96},{96,128},{128,160},{160,192},{192,224},{224... | collective-permute-start | bytes 786440 | tf_op jit(solution)/shard_map/ppermute | solution.py:146
  82.2 0.4 copy-done.3
  82.6 7.6 %shard_map.30 = (f32[512,512]{1,0:T(8,128)}, f32[512,512]{1,0:T(8,128)}) custom-call(s32[8]{0:T(128)S(1)} %stack.59.pos_ref, bf16[8,512,512]{2,1,0:T(8,128)(2,1)} %copy-done.3, bf16[512,512]{1,0:T(8,128)(2,1)S(1)} %get-tuple-element.20.refs_0_, bf16[512,512]{1,0:T(8,128)(2,1)S(1)} %collective-permute-done.6.refs_1_, ...), custom_call_target="tpu_custom_call" | custom-call | flops 3489660928 | bytes 12582912 | tf_op jit(solution)/shard_map/pallas_call | solution.py:186
  90.2 0.0 collective-permute-done.19.refs_13_
  90.3 0.7 copy-done.6
  91.0 0.2 copy-done.7
  91.2 0.2 copy-done.8
  91.4 8.0 %shard_map.31 = (f32[512,512]{1,0:T(8,128)}, f32[512,512]{1,0:T(8,128)}) custom-call(s32[8]{0:T(128)S(1)} %stack.59.pos_ref, s32[1]{0:T(128)} %bitcast.8.keep_ref, f32[512,512]{1,0:T(8,128)} %get-tuple-element.22.first_in, f32[512,512]{1,0:T(8,128)} %get-tuple-element.23.second_in, bf16[8,512,512]{2,1,0:T(8,128)(2,1)} %copy-done.3, ...), custom_call_target="tpu_custom_call" | custom-call | flops 1342177280 | bytes 8388608 | tf_op jit(solution)/shard_map/pallas_call | solution.py:194
  99.4 2.8 %collective-permute-start.22 = (f32[512,512]{1,0:T(8,128)}, f32[512,512]{1,0:T(8,128)S(1)}, u32[]{:S(2)}, u32[]{:S(2)}) collective-permute-start(f32[512,512]{1,0:T(8,128)} %get-tuple-element.28), channel_id=1, source_target_pairs={{0,2},{2,0},{1,3},{3,1},{4,6},{6,4},{5,7},{7,5},{8,10},{10,8},{9,1... | collective-permute-start | bytes 3145736 | tf_op jit(solution)/shard_map/ppermute | solution.py:213
  102.2 2.5 %collective-permute-done.22.got_ref = f32[512,512]{1,0:T(8,128)S(1)} collective-permute-done((f32[512,512]{1,0:T(8,128)}, f32[512,512]{1,0:T(8,128)S(1)}, u32[]{:S(2)}, u32[]{:S(2)}) %collective-permute-start.22) | collective-permute-done | bytes 1048608 | tf_op jit(solution)/shard_map/ppermute | solution.py:213
  104.7 1.2 copy-done.1
  105.9 1.4 %shard_map.32 = (bf16[512,512]{1,0:T(8,128)(2,1)S(1)}, bf16[8,16,2,8,128]{4,3,2,1,0:T(8,128)(2,1)}) custom-call(f32[512,512]{1,0:T(8,128)S(1)} %copy-done.1, f32[512,512]{1,0:T(8,128)S(1)} %collective-permute-done.22.got_ref), custom_call_target="tpu_custom_call" | custom-call | bytes 3145728 | tf_op jit(solution)/shard_map/pallas_call | solution.py:214
  107.4 8.7 %all-to-all-start.1 = ((bf16[256,8,128]{2,1,0:T(8,128)(2,1)}), bf16[256,8,128]{2,1,0:T(8,128)(2,1)S(1)}, u32[]{:S(2)}, u32[]{:S(2)}) async-start(bf16[256,8,128]{2,1,0:T(8,128)(2,1)} %bitcast.18), calls=%async_computation.1 | async-start | bytes 1048576 | tf_op jit(solution)/shard_map/all_to_all | solution.py:218
  116.0 3.5 %collective-permute-start.23 = (bf16[512,512]{1,0:T(8,128)(2,1)S(1)}, bf16[512,512]{1,0:T(8,128)(2,1)S(1)}, u32[]{:S(2)}, u32[]{:S(2)}) collective-permute-start(bf16[512,512]{1,0:T(8,128)(2,1)S(1)} %get-tuple-element.29), channel_id=1, source_target_pairs={{0,0},{1,2},{2,1},{3,3},{4,4},{5,6},{6,5},{7,7},{8,8},{9,10},{10,9... | collective-permute-start | bytes 1572872 | tf_op jit(solution)/shard_map/ppermute | solution.py:217
  119.6 11.2 %collective-permute-done.23.direct_ref = bf16[512,512]{1,0:T(8,128)(2,1)S(1)} collective-permute-done((bf16[512,512]{1,0:T(8,128)(2,1)S(1)}, bf16[512,512]{1,0:T(8,128)(2,1)S(1)}, u32[]{:S(2)}, u32[]{:S(2)}) %collective-permute-start.23) | collective-permute-done | bytes 524320 | tf_op jit(solution)/shard_map/ppermute | solution.py:217
  130.8 5.2 %all-to-all-done.1 = bf16[256,8,128]{2,1,0:T(8,128)(2,1)S(1)} async-done(((bf16[256,8,128]{2,1,0:T(8,128)(2,1)}), bf16[256,8,128]{2,1,0:T(8,128)(2,1)S(1)}, u32[]{:S(2)}, u32[]{:S(2)}) %all-to-all-start.1) | async-done | bytes 524320 | tf_op jit(solution)/shard_map/all_to_all | solution.py:218
  135.9 1.4 %shard_map.33 = f32[512,512]{1,0:T(8,128)} custom-call(bf16[512,512]{1,0:T(8,128)(2,1)S(1)} %collective-permute-done.23.direct_ref, bf16[8,8,2,2,8,128]{5,4,3,2,1,0:T(8,128)(2,1)S(1)} %bitcast.30), custom_call_target="tpu_custom_call" | custom-call | bytes 2097152 | tf_op jit(solution)/shard_map/pallas_call | solution.py:219
  (24 shorter events, 0.2 us)
Async XLA Ops:
  0.0 1.2 copy-start
  3.1 19.8 %all-to-all-start = ((bf16[16,128,128]{2,1,0:T(8,128)(2,1)}), bf16[16,128,128]{2,1,0:T(8,128)(2,1)S(1)}, u32[]{:S(2)}, u32[]{:S(2)}) async-start(bf16[16,128,128]{2,1,0:T(8,128)(2,1)} %bitcast.10), calls=%async_computation | async-start | bytes 1048576 | tf_op jit(solution)/shard_map/all_to_all | solution.py:153
  12.9 20.0 %collective-permute-start.9 = (bf16[512,512]{1,0:T(8,128)(2,1)S(1)}, bf16[512,512]{1,0:T(8,128)(2,1)S(1)}, u32[]{:S(2)}, u32[]{:S(2)}) collective-permute-start(bf16[512,512]{1,0:T(8,128)(2,1)S(1)} %get-tuple-element.31.refs_8_), channel_id=1, source_target_pairs={{0,17},{17,0},{1,16},{16,1},{2,19},{19,2},{3,18},{18,3},{4,21},{21... | collective-permute-start | bytes 1572872 | tf_op jit(solution)/shard_map/ppermute | solution.py:148
  15.6 17.3 %collective-permute-start.6 = (bf16[512,512]{1,0:T(8,128)(2,1)S(1)}, bf16[512,512]{1,0:T(8,128)(2,1)S(1)}, u32[]{:S(2)}, u32[]{:S(2)}) collective-permute-start(bf16[512,512]{1,0:T(8,128)(2,1)S(1)} %get-tuple-element.20.refs_0_), channel_id=1, source_target_pairs={{0,12},{4,0},{8,4},{12,8},{1,13},{5,1},{9,5},{13,9},{2,14},{6,2},{... | collective-permute-start | bytes 1572872 | tf_op jit(solution)/shard_map/ppermute | solution.py:145
  18.0 15.4 %collective-permute-start.8 = (bf16[512,512]{1,0:T(8,128)(2,1)S(1)}, bf16[512,512]{1,0:T(8,128)(2,1)}, u32[]{:S(2)}, u32[]{:S(2)}) collective-permute-start(bf16[512,512]{1,0:T(8,128)(2,1)S(1)} %get-tuple-element.20.refs_0_), channel_id=1, source_target_pairs={{0,4},{4,8},{8,12},{12,0},{1,5},{5,9},{9,13},{13,1},{2,6},{6,10},{... | collective-permute-start | bytes 1572872 | tf_op jit(solution)/shard_map/ppermute | solution.py:146
  23.5 15.7 %collective-permute-start = (bf16[512,512]{1,0:T(8,128)(2,1)S(1)}, bf16[512,512]{1,0:T(8,128)(2,1)}, u32[]{:S(2)}, u32[]{:S(2)}) collective-permute-start(bf16[512,512]{1,0:T(8,128)(2,1)S(1)} %shard_map.29), channel_id=1, source_target_pairs={{0,224},{32,0},{64,32},{96,64},{128,96},{160,128},{192,160},{224,1... | collective-permute-start | bytes 1572872 | tf_op jit(solution)/shard_map/ppermute | solution.py:145
  29.1 13.2 %collective-permute-start.3 = (bf16[512,512]{1,0:T(8,128)(2,1)S(1)}, bf16[512,512]{1,0:T(8,128)(2,1)}, u32[]{:S(2)}, u32[]{:S(2)}) collective-permute-start(bf16[512,512]{1,0:T(8,128)(2,1)S(1)} %shard_map.29), channel_id=1, source_target_pairs={{0,32},{32,64},{64,96},{96,128},{128,160},{160,192},{192,224},{224... | collective-permute-start | bytes 1572872 | tf_op jit(solution)/shard_map/ppermute | solution.py:146
  32.8 14.5 %collective-permute-start.15 = (bf16[512,512]{1,0:T(8,128)(2,1)S(1)}, bf16[512,512]{1,0:T(8,128)(2,1)S(1)}, u32[]{:S(2)}, u32[]{:S(2)}) collective-permute-start(bf16[512,512]{1,0:T(8,128)(2,1)S(1)} %get-tuple-element.20.refs_0_), channel_id=1, source_target_pairs={{0,17},{17,0},{1,16},{16,1},{2,19},{19,2},{3,18},{18,3},{4,21},{21... | collective-permute-start | bytes 1572872 | tf_op jit(solution)/shard_map/ppermute | solution.py:148
  32.8 17.0 %collective-permute-start.13 = (bf16[512,512]{1,0:T(8,128)(2,1)S(1)}, bf16[512,512]{1,0:T(8,128)(2,1)S(1)}, u32[]{:S(2)}, u32[]{:S(2)}) collective-permute-start(bf16[512,512]{1,0:T(8,128)(2,1)S(1)} %collective-permute-done.6.refs_1_), channel_id=1, source_target_pairs={{0,1},{1,0},{16,17},{17,16},{2,3},{3,2},{18,19},{19,18},{4,5},{5,4... | collective-permute-start | bytes 1572872 | tf_op jit(solution)/shard_map/ppermute | solution.py:147
  33.4 16.8 %collective-permute-start.7 = (bf16[512,512]{1,0:T(8,128)(2,1)S(1)}, bf16[512,512]{1,0:T(8,128)(2,1)}, u32[]{:S(2)}, u32[]{:S(2)}) collective-permute-start(bf16[512,512]{1,0:T(8,128)(2,1)S(1)} %collective-permute-done.6.refs_1_), channel_id=1, source_target_pairs={{0,12},{4,0},{8,4},{12,8},{1,13},{5,1},{9,5},{13,9},{2,14},{6,2},{... | collective-permute-start | bytes 1572872 | tf_op jit(solution)/shard_map/ppermute | solution.py:145
  39.1 13.4 %collective-permute-start.11 = (bf16[512,512]{1,0:T(8,128)(2,1)S(1)}, bf16[512,512]{1,0:T(8,128)(2,1)}, u32[]{:S(2)}, u32[]{:S(2)}) collective-permute-start(bf16[512,512]{1,0:T(8,128)(2,1)S(1)} %collective-permute-done.9.refs_4_), channel_id=1, source_target_pairs={{0,4},{4,8},{8,12},{12,0},{1,5},{5,9},{9,13},{13,1},{2,6},{6,10},{... | collective-permute-start | bytes 1572872 | tf_op jit(solution)/shard_map/ppermute | solution.py:146
  42.4 11.9 %collective-permute-start.1 = (bf16[512,512]{1,0:T(8,128)(2,1)}, bf16[512,512]{1,0:T(8,128)(2,1)}, u32[]{:S(2)}, u32[]{:S(2)}) collective-permute-start(bf16[512,512]{1,0:T(8,128)(2,1)} %collective-permute-done), channel_id=1, source_target_pairs={{0,224},{32,0},{64,32},{96,64},{128,96},{160,128},{192,160},{224,1... | collective-permute-start | bytes 1572872 | tf_op jit(solution)/shard_map/ppermute | solution.py:145
  47.3 0.8 copy-start.4
  48.1 17.1 %collective-permute-start.4 = (bf16[512,512]{1,0:T(8,128)(2,1)}, bf16[512,512]{1,0:T(8,128)(2,1)}, u32[]{:S(2)}, u32[]{:S(2)}) collective-permute-start(bf16[512,512]{1,0:T(8,128)(2,1)} %collective-permute-done.3), channel_id=1, source_target_pairs={{0,32},{32,64},{64,96},{96,128},{128,160},{160,192},{192,224},{224... | collective-permute-start | bytes 1572872 | tf_op jit(solution)/shard_map/ppermute | solution.py:146
  49.8 16.5 %collective-permute-start.16 = (bf16[512,512]{1,0:T(8,128)(2,1)S(1)}, bf16[512,512]{1,0:T(8,128)(2,1)S(1)}, u32[]{:S(2)}, u32[]{:S(2)}) collective-permute-start(bf16[512,512]{1,0:T(8,128)(2,1)S(1)} %collective-permute-done.6.refs_1_), channel_id=1, source_target_pairs={{0,17},{17,0},{1,16},{16,1},{2,19},{19,2},{3,18},{18,3},{4,21},{21... | collective-permute-start | bytes 1572872 | tf_op jit(solution)/shard_map/ppermute | solution.py:148
  50.2 18.6 %collective-permute-start.14 = (bf16[512,512]{1,0:T(8,128)(2,1)}, bf16[512,512]{1,0:T(8,128)(2,1)S(1)}, u32[]{:S(2)}, u32[]{:S(2)}) collective-permute-start(bf16[512,512]{1,0:T(8,128)(2,1)} %collective-permute-done.8.refs_3_), channel_id=1, source_target_pairs={{0,1},{1,0},{16,17},{17,16},{2,3},{3,2},{18,19},{19,18},{4,5},{5,4... | collective-permute-start | bytes 1572872 | tf_op jit(solution)/shard_map/ppermute | solution.py:147
  52.6 16.2 %collective-permute-start.12 = (bf16[512,512]{1,0:T(8,128)(2,1)}, bf16[512,512]{1,0:T(8,128)(2,1)S(1)}, u32[]{:S(2)}, u32[]{:S(2)}) collective-permute-start(bf16[512,512]{1,0:T(8,128)(2,1)} %collective-permute-done.11.refs_7_), channel_id=1, source_target_pairs={{0,4},{4,8},{8,12},{12,0},{1,5},{5,9},{9,13},{13,1},{2,6},{6,10},{... | collective-permute-start | bytes 1572872 | tf_op jit(solution)/shard_map/ppermute | solution.py:146
  54.3 14.6 %collective-permute-start.2 = (bf16[512,512]{1,0:T(8,128)(2,1)}, bf16[512,512]{1,0:T(8,128)(2,1)S(1)}, u32[]{:S(2)}, u32[]{:S(2)}) collective-permute-start(bf16[512,512]{1,0:T(8,128)(2,1)} %collective-permute-done.1), channel_id=1, source_target_pairs={{0,224},{32,0},{64,32},{96,64},{128,96},{160,128},{192,160},{224,1... | collective-permute-start | bytes 1572872 | tf_op jit(solution)/shard_map/ppermute | solution.py:145
  65.2 13.2 %collective-permute-start.5 = (bf16[512,512]{1,0:T(8,128)(2,1)}, bf16[512,512]{1,0:T(8,128)(2,1)S(1)}, u32[]{:S(2)}, u32[]{:S(2)}) collective-permute-start(bf16[512,512]{1,0:T(8,128)(2,1)} %collective-permute-done.4), channel_id=1, source_target_pairs={{0,32},{32,64},{64,96},{96,128},{128,160},{160,192},{192,224},{224... | collective-permute-start | bytes 1572872 | tf_op jit(solution)/shard_map/ppermute | solution.py:146
  66.3 15.9 %copy-start.5 = (bf16[512,512]{1,0:T(8,128)(2,1)}, bf16[512,512]{1,0:T(8,128)(2,1)S(1)}, u32[]{:S(2)}) copy-start(bf16[512,512]{1,0:T(8,128)(2,1)S(1)} %collective-permute-done.16.refs_12_) | copy-start | bytes 1572868
  66.3 14.3 %collective-permute-start.10 = (bf16[512,512]{1,0:T(8,128)(2,1)S(1)}, bf16[512,512]{1,0:T(8,128)(2,1)S(1)}, u32[]{:S(2)}, u32[]{:S(2)}) collective-permute-start(bf16[512,512]{1,0:T(8,128)(2,1)S(1)} %collective-permute-done.9.refs_4_), channel_id=1, source_target_pairs={{0,12},{4,0},{8,4},{12,8},{1,13},{5,1},{9,5},{13,9},{2,14},{6,2},{... | collective-permute-start | bytes 1572872 | tf_op jit(solution)/shard_map/ppermute | solution.py:145
  68.7 21.5 %copy-start.2 = (bf16[512,512]{1,0:T(8,128)(2,1)}, bf16[512,512]{1,0:T(8,128)(2,1)S(1)}, u32[]{:S(2)}) copy-start(bf16[512,512]{1,0:T(8,128)(2,1)S(1)} %collective-permute-done.14.refs_10_) | copy-start | bytes 1572868
  68.7 21.5 %collective-permute-start.20 = (bf16[512,512]{1,0:T(8,128)(2,1)}, bf16[512,512]{1,0:T(8,128)(2,1)S(1)}, u32[]{:S(2)}, u32[]{:S(2)}) collective-permute-start(bf16[512,512]{1,0:T(8,128)(2,1)} %collective-permute-done.7.refs_2_), channel_id=1, source_target_pairs={{0,17},{17,0},{1,16},{16,1},{2,19},{19,2},{3,18},{18,3},{4,21},{21... | collective-permute-start | bytes 1572872 | tf_op jit(solution)/shard_map/ppermute | solution.py:148
  68.7 21.5 %collective-permute-start.19 = (bf16[512,512]{1,0:T(8,128)(2,1)}, bf16[512,512]{1,0:T(8,128)(2,1)S(1)}, u32[]{:S(2)}, u32[]{:S(2)}) collective-permute-start(bf16[512,512]{1,0:T(8,128)(2,1)} %collective-permute-done.7.refs_2_), channel_id=1, source_target_pairs={{0,1},{1,0},{16,17},{17,16},{2,3},{3,2},{18,19},{19,18},{4,5},{5,4... | collective-permute-start | bytes 1572872 | tf_op jit(solution)/shard_map/ppermute | solution.py:147
  68.8 21.4 %collective-permute-start.21 = (bf16[512,512]{1,0:T(8,128)(2,1)}, bf16[512,512]{1,0:T(8,128)(2,1)S(1)}, u32[]{:S(2)}, u32[]{:S(2)}) collective-permute-start(bf16[512,512]{1,0:T(8,128)(2,1)} %copy-done.4), channel_id=1, source_target_pairs={{0,4},{4,8},{8,12},{12,0},{1,5},{5,9},{9,13},{13,1},{2,6},{6,10},{... | collective-permute-start | bytes 1572872 | tf_op jit(solution)/shard_map/ppermute | solution.py:146
  78.4 11.9 %collective-permute-start.17 = (bf16[256,512]{1,0:T(8,128)(2,1)S(1)}, bf16[256,512]{1,0:T(8,128)(2,1)S(1)}, u32[]{:S(2)}, u32[]{:S(2)}) collective-permute-start(bf16[256,512]{1,0:T(8,128)(2,1)S(1)} %slice.8), channel_id=1, source_target_pairs={{0,224},{32,0},{64,32},{96,64},{128,96},{160,128},{192,160},{224,1... | collective-permute-start | bytes 786440 | tf_op jit(solution)/shard_map/ppermute | solution.py:145
  80.6 2.0 %copy-start.3 = (bf16[8,512,512]{2,1,0:T(8,128)(2,1)}, bf16[8,512,512]{2,1,0:T(8,128)(2,1)S(1)}, u32[]{:S(2)}) copy-start(bf16[8,512,512]{2,1,0:T(8,128)(2,1)S(1)} %bitcast_dynamic-update-slice_fusion.w_ref) | copy-start | bytes 12582916
  80.6 9.6 %collective-permute-start.18 = (bf16[256,512]{1,0:T(8,128)(2,1)S(1)}, bf16[256,512]{1,0:T(8,128)(2,1)S(1)}, u32[]{:S(2)}, u32[]{:S(2)}) collective-permute-start(bf16[256,512]{1,0:T(8,128)(2,1)S(1)} %slice.9), channel_id=1, source_target_pairs={{0,32},{32,64},{64,96},{96,128},{128,160},{160,192},{192,224},{224... | collective-permute-start | bytes 786440 | tf_op jit(solution)/shard_map/ppermute | solution.py:146
  90.2 0.8 copy-start.6
  90.2 1.0 copy-start.7
  90.3 1.1 copy-start.8
  99.4 5.3 %collective-permute-start.22 = (f32[512,512]{1,0:T(8,128)}, f32[512,512]{1,0:T(8,128)S(1)}, u32[]{:S(2)}, u32[]{:S(2)}) collective-permute-start(f32[512,512]{1,0:T(8,128)} %get-tuple-element.28), channel_id=1, source_target_pairs={{0,2},{2,0},{1,3},{3,1},{4,6},{6,4},{5,7},{7,5},{8,10},{10,8},{9,1... | collective-permute-start | bytes 3145736 | tf_op jit(solution)/shard_map/ppermute | solution.py:213
  104.7 1.2 copy-start.1
  107.4 28.6 %all-to-all-start.1 = ((bf16[256,8,128]{2,1,0:T(8,128)(2,1)}), bf16[256,8,128]{2,1,0:T(8,128)(2,1)S(1)}, u32[]{:S(2)}, u32[]{:S(2)}) async-start(bf16[256,8,128]{2,1,0:T(8,128)(2,1)} %bitcast.18), calls=%async_computation.1 | async-start | bytes 1048576 | tf_op jit(solution)/shard_map/all_to_all | solution.py:218
  116.0 14.7 %collective-permute-start.23 = (bf16[512,512]{1,0:T(8,128)(2,1)S(1)}, bf16[512,512]{1,0:T(8,128)(2,1)S(1)}, u32[]{:S(2)}, u32[]{:S(2)}) collective-permute-start(bf16[512,512]{1,0:T(8,128)(2,1)S(1)} %get-tuple-element.29), channel_id=1, source_target_pairs={{0,0},{1,2},{2,1},{3,3},{4,4},{5,6},{6,5},{7,7},{8,8},{9,10},{10,9... | collective-permute-start | bytes 1572872 | tf_op jit(solution)/shard_map/ppermute | solution.py:217

commit v2 on v1

v2 whole, which is shorter than its diff:
```python
import jax
import jax.numpy as jnp
import numpy as np
from jax import lax
from jax.experimental import pallas as pl
from jax.experimental.pallas import tpu as pltpu
from jax.sharding import Mesh, PartitionSpec as P

AXES = ("row", "xh", "y", "core", "rep")
F32, BF16 = jnp.float32, jnp.bfloat16
X_LINE = ("xh", "rep")
PAIR = [(0, 1), (1, 0), (2, 3), (3, 2)]
CROSS = [(0, 3), (3, 0), (1, 2), (2, 1)]
B = 512


def call(body, outs, n_scalar, n_in, flops=0, moved=0, scratch=(), limit=20):
    vmem = pl.BlockSpec(memory_space=pltpu.VMEM)
    smem = pl.BlockSpec(memory_space=pltpu.SMEM)
    return pl.pallas_call(
        body,
        out_shape=outs,
        in_specs=[smem] * n_scalar + [vmem] * n_in,
        out_specs=[vmem] * len(outs),
        scratch_shapes=list(scratch),
        compiler_params=pltpu.CompilerParams(vmem_limit_bytes=limit << 20),
        cost_estimate=pl.CostEstimate(flops=flops, bytes_accessed=moved, transcendentals=0),
    )


def lane_block(shape):
    return lax.broadcasted_iota(jnp.int32, shape, len(shape) - 1) // 32


def turn(parts):
    block = lane_block(parts[0].shape)
    out = []
    for j in range(4):
        rolled = [pltpu.roll(p, ((i - j) * 32) % 128, 1) if i != j else p for i, p in enumerate(parts)]
        out.append(
            jnp.where(
                block < 2, jnp.where(block == 0, rolled[0], rolled[1]), jnp.where(block == 2, rolled[2], rolled[3])
            )
        )
    return out


def w_pack(rep_ref, w_ref, out_ref):
    rep = rep_ref[0]
    for half in range(2):
        for g in range(4):
            parts = []
            for hi in range(4):
                v = w_ref[half * B + hi * 128 : half * B + (hi + 1) * 128, g * 128 : (g + 1) * 128].astype(F32)
                parts.append(jnp.where(rep == 0, v, pltpu.roll(v, 96, 1)))
            turned = turn(parts)
            for j in (0, 2):
                out_ref[g * 2 + j // 2, half] = turned[j].astype(BF16)


def w_unpack(in_ref, out_ref):
    for g in range(4):
        turned = turn([in_ref[4 * g + j].astype(F32) for j in range(4)])
        for hi in range(4):
            out_ref[hi * 128 : (hi + 1) * 128, g * 128 : (g + 1) * 128] = turned[hi].astype(BF16)


def dot(a, b):
    return jnp.dot(a, b, preferred_element_type=F32)


def product_early(pos_ref, w_ref, *refs):
    for half in range(2):
        total = None
        for p in range(8):
            term = dot(refs[half * 8 + p][...], w_ref[pos_ref[p]])
            total = term if total is None else total + term
        refs[16 + half][...] = total


def product_late(pos_ref, keep_ref, first_ref, second_ref, top_ref, bottom_ref, *refs):
    kept_ref, sent_ref, far_ref = refs[16:]
    far_ref[:256] = top_ref[...]
    far_ref[256:] = bottom_ref[...]
    first_kept = keep_ref[0] == 0
    for p in range(8):

        @pl.when(pos_ref[p] == 4)
        def _(p=p):
            first = first_ref[...] + dot(refs[p][...], far_ref[...])
            second = second_ref[...] + dot(refs[8 + p][...], far_ref[...])
            kept_ref[...] = jnp.where(first_kept, first, second)
            sent_ref[...] = jnp.where(first_kept, second, first)


def spread(kept_ref, got_ref, direct_ref, mirror_ref):
    cycle = (kept_ref[...] + got_ref[...]).astype(BF16).astype(F32)
    direct_ref[...] = cycle.T.astype(BF16)
    split = cycle.reshape(16, 4, 8, B)
    for g in range(4):
        parts = [split[:, hi, :, g * 128 : (g + 1) * 128].reshape(128, 128) for hi in range(4)]
        for j, t in enumerate(turn(parts)):
            mirror_ref[2 * g + j // 2, :, j % 2] = t.reshape(16, 8, 128).astype(BF16)


def finish(direct_ref, mirror_ref, out_ref):
    for owner in range(16):
        z, core = owner // 2, owner % 2
        for g in range(4):
            parts = [mirror_ref[z, 2 * g + j // 2, core, j % 2].astype(F32) for j in range(4)]
            for hi, t in enumerate(turn(parts)):
                rows = slice(owner * 32 + hi * 8, owner * 32 + hi * 8 + 8)
                lanes = slice(g * 128, (g + 1) * 128)
                out_ref[rows, lanes] = t + direct_ref[rows, lanes].astype(F32)


def ring(n, step):
    return [(i, (i + step) % n) for i in range(n)]


def lockstep(*groups):
    return lax.optimization_barrier(groups)


def local(amplitudes, intermediate):
    z, xh, y, core, rep = (lax.axis_index(a) for a in AXES)
    shape = jax.ShapeDtypeStruct
    up = lambda v, axis, n: lax.ppermute(v, axis, ring(n, -1))
    down = lambda v, axis, n: lax.ppermute(v, axis, ring(n, 1))
    pair = lambda v: lax.ppermute(v, X_LINE, PAIR)
    cross = lambda v: lax.ppermute(v, X_LINE, CROSS)

    f00 = lax.dynamic_slice_in_dim(amplitudes, rep * B, B, 0)
    g00 = lax.dynamic_slice_in_dim(amplitudes, (1 - rep) * B, B, 0)
    f01, f03, f10 = up(f00, "y", 4), down(f00, "y", 4), cross(g00)

    intermediate, f00, g00 = lax.optimization_barrier((intermediate, f00, g00))
    packed = call(w_pack, [shape((8, 2, 128, 128), BF16)], 1, 1, moved=2 << 20)(
        rep.reshape(1).astype(jnp.int32), intermediate
    )[0]
    arrived = lax.all_to_all(packed.reshape(16, 128, 128), ("xh", "y", "core"), split_axis=0, concat_axis=0, tiled=True)
    w0 = call(w_unpack, [shape((B, B), BF16)], 0, 1, moved=1 << 20)(arrived)[0]

    w0, f00, f01, f03, f10 = lockstep(w0, f00, f01, f03, f10)
    w1, w7 = up(w0, "row", 8), down(w0, "row", 8)
    f02, f13, g01, g10 = up(f01, "y", 4), down(f10, "y", 4), pair(f01), cross(f00)

    w1, w7, f02, f13, g01, g10, f10, f03, f01 = lockstep(w1, w7, f02, f13, g01, g10, f10, f03, f01)
    w2, w6 = up(w1, "row", 8), down(w7, "row", 8)
    f11, f12, g03, g11 = up(f10, "y", 4), down(f13, "y", 4), pair(f03), cross(f01)

    w2, w6, f11, f12, g03, g11, f02, g10 = lockstep(w2, w6, f11, f12, g03, g11, f02, g10)
    w3, w5 = up(w2, "row", 8), down(w6, "row", 8)
    g02, g12, g13 = pair(f02), cross(f02), down(g10, "y", 4)

    w3, w5, g02, g12, g13 = lockstep(w3, w5, g02, g12, g13)
    top, bottom = up(w3[:256], "row", 8), down(w5[256:], "row", 8)

    pieces = (f00, f01, f02, f03, f10, f11, f12, f13, g00, g01, g02, g03, g10, g11, g12, g13)
    position = jnp.stack(
        [(4 * lax.rem(xh + i, 2) + lax.rem(y + j, 4) - z + 8) % 8 for i in range(2) for j in range(4)]
    ).astype(jnp.int32)
    stack = jnp.stack([w0, w1, w2, w3, jnp.zeros((B, B), BF16), w5, w6, w7])
    first, second = call(
        product_early, [shape((B, B), F32)] * 2, 1, 17, flops=32 * B**3, moved=12 << 20
    )(position, stack, *pieces)
    kept, sent = call(
        product_late,
        [shape((B, B), F32)] * 2,
        2,
        4 + 16,
        flops=4 * B**3,
        moved=4 << 20,
        scratch=[pltpu.VMEM((B, B), BF16)],
    )(position, (core ^ rep).reshape(1).astype(jnp.int32), first, second, top, bottom, *pieces)
    got = lax.ppermute(sent, "core", [(0, 1), (1, 0)])
    direct, mirror = call(
        spread, [shape((B, B), BF16), shape((8, 16, 2, 8, 128), BF16)], 0, 2, moved=3 << 20
    )(kept, got)
    direct = lax.ppermute(direct, ("core", "rep"), [(0, 0), (1, 2), (2, 1), (3, 3)])
    mirror = lax.all_to_all(mirror.reshape(256, 8, 128), AXES, split_axis=0, concat_axis=0, tiled=True)
    out = call(finish, [shape((B, B), F32)], 0, 2, moved=2 << 20)(direct, mirror.reshape(8, 8, 2, 2, 8, 128))[0]
    return out.reshape(16, 1, 32, B)


def solution(mesh):
    fine = Mesh(np.asarray(mesh.devices).reshape(8, 2, 4, 2, 2), AXES)
    block = P("row", ("xh", "y", "core"))
    out = P(None, ("xh", "y", "core"), None, ("row", "rep"))
    return jax.shard_map(local, mesh=fine, in_specs=(block, block), out_specs=out, check_vma=False)
```

time: 138 us -> 152 us (1.10)
  blocking collectives: 0 us -> 17.2 us
  Pallas kernels: 20.9 us -> 13.2 us
  waiting for transfers between devices: 56.5 us -> 60.7 us
  starting transfers between devices: 49.2 us -> 51.8 us
  local copies, waits for them, and re-layouts: 10.6 us -> 8.79 us
    all_to_all x0 -> x1, blocking collectives: none -> 17.2 us  [local(): lax.all_to_all(packed.reshape(16, 128, 128), ('xh', 'y', 'core'), split_a...]
    ppermute x7, waiting for transfers between devices: 4.81 us -> 19.4 us  [local(): up = lambda v, axis, n: lax.ppermute(v, axis, ring(n, -1))]
    ppermute x8, waiting for transfers between devices: 20.5 us -> 7.74 us  [local(): down = lambda v, axis, n: lax.ppermute(v, axis, ring(n, 1))]
    ppermute x4, starting transfers between devices: 3.03 us -> 11.7 us  [local(): cross = lambda v: lax.ppermute(v, X_LINE, CROSS)]
    all_to_all x1 -> x0, starting transfers between devices: 8.45 us -> none  [local(): lax.all_to_all(packed.reshape(16, 128, 128), ('xh', 'y', 'core'), split_a...]
    ppermute x4, waiting for transfers between devices: 7.27 us -> 14.8 us  [local(): cross = lambda v: lax.ppermute(v, X_LINE, CROSS)]
    pallas_call x3, Pallas kernels: 16.1 us -> 9.17 us  [the longest x1 6.18 us: local(): call(product_early, [shape((B, B), F32)] * 2, 1, 17, flops=32 * B ** 3, m...]
    ppermute x7, starting transfers between devices: 17.4 us -> 23.6 us  [local(): up = lambda v, axis, n: lax.ppermute(v, axis, ring(n, -1))]
  transfers between devices with their start and end apart: 26 -> 25, of which waited for: 13 -> 13; matrix products, arithmetic and copies ran while one was open for 4% -> 2% of each run, Pallas kernels for 6% -> 5%
where the time goes in v2:
time: 152 us
  waiting for transfers between devices  60.7 us (40%)
  starting transfers between devices  51.8 us (34%)
  blocking collectives  17.2 us (11%)
  Pallas kernels  13.2 us (9%)
  local copies, waits for them, and re-layouts  8.79 us (6%)
    ppermute x7, starting transfers between devices, local(): up = lambda v, axis, n: lax.ppermute(v, axis, ring(n, -1))  23.6 us
    ppermute x7, waiting for transfers between devices, local(): up = lambda v, axis, n: lax.ppermute(v, axis, ring(n, -1))  19.4 us
    all_to_all x1, blocking collectives, local(): lax.all_to_all(packed.reshape(16, 128, 128), ('xh', 'y', 'core'), split_a...  17.2 us
    ppermute x4, waiting for transfers between devices, local(): cross = lambda v: lax.ppermute(v, X_LINE, CROSS)  14.8 us
    ppermute x4, starting transfers between devices, local(): cross = lambda v: lax.ppermute(v, X_LINE, CROSS)  11.7 us
    ppermute x1, waiting for transfers between devices, local(): lax.ppermute(direct, ('core', 'rep'), [(0, 0), (1, 2), (2, 1), (3, 3)])  11.2 us
    ppermute x8, waiting for transfers between devices, local(): down = lambda v, axis, n: lax.ppermute(v, axis, ring(n, 1))  7.74 us
    ppermute x1, starting transfers between devices, local(): got = lax.ppermute(sent, 'core', [(0, 1), (1, 0)])  6.84 us
  transfers between devices with their start and end apart: 25, of which 13 were waited for; matrix products, arithmetic and copies ran while one was open for 2% of the time, Pallas kernels for 5%

profile of v2, /device:TPU:1, one launch (start us, length us, event | category | flops | bytes accessed | tf_op | source)
XLA Modules:
  0.0 151.8 jit_solution(16950089742777720346)
XLA Ops:
  0.0 1.3 constant_dynamic-slice_fusion
  1.3 3.6 %collective-permute-start = (bf16[512,512]{1,0:T(8,128)(2,1)S(1)}, bf16[512,512]{1,0:T(8,128)(2,1)S(1)}, u32[]{:S(2)}, u32[]{:S(2)}) collective-permute-start(bf16[512,512]{1,0:T(8,128)(2,1)S(1)} %get-tuple-element.46.refs_0_), channel_id=1, source_target_pairs={{0,12},{4,0},{8,4},{12,8},{1,13},{5,1},{9,5},{13,9},{2,14},{6,2},{... | collective-permute-start | bytes 1572872 | tf_op jit(solution)/shard_map/ppermute | solution.py:128
  4.9 0.0 collective-permute-start.1
  4.9 2.5 %collective-permute-start.2 = (bf16[512,512]{1,0:T(8,128)(2,1)S(1)}, bf16[512,512]{1,0:T(8,128)(2,1)S(1)}, u32[]{:S(2)}, u32[]{:S(2)}) collective-permute-start(bf16[512,512]{1,0:T(8,128)(2,1)S(1)} %get-tuple-element.64.refs_8_), channel_id=1, source_target_pairs={{0,17},{17,0},{1,16},{16,1},{2,19},{19,2},{3,18},{18,3},{4,21},{21... | collective-permute-start | bytes 1572872 | tf_op jit(solution)/shard_map/ppermute | solution.py:131
  7.4 1.2 copy-done
  8.6 1.1 shard_map.28
  9.7 17.2 %all_to_all.10.in_ref = bf16[16,128,128]{2,1,0:T(8,128)(2,1)S(1)} all-to-all(bf16[16,128,128]{2,1,0:T(8,128)(2,1)S(1)} %bitcast.30), channel_id=1, replica_groups=mesh['row'=8,'xh'=2,'y'=4,'core'=2,'rep'=2] {'xh','y','core'}, dimensions={0} | all-to-all | bytes 1048576 | tf_op jit(solution)/shard_map/all_to_all | solution.py:141
  26.9 0.5 shard_map.29
  27.4 0.0 collective-permute-done.refs_1_
  27.4 0.0 collective-permute-done.1.refs_3_
  27.4 0.0 collective-permute-done.2.refs_4_
  27.4 5.7 %collective-permute-start.3 = (bf16[512,512]{1,0:T(8,128)(2,1)S(1)}, bf16[512,512]{1,0:T(8,128)(2,1)S(1)}, u32[]{:S(2)}, u32[]{:S(2)}) collective-permute-start(bf16[512,512]{1,0:T(8,128)(2,1)S(1)} %shard_map.29), channel_id=1, source_target_pairs={{0,224},{32,0},{64,32},{96,64},{128,96},{160,128},{192,160},{224,1... | collective-permute-start | bytes 1572872 | tf_op jit(solution)/shard_map/ppermute | solution.py:128
  33.1 0.0 collective-permute-start.4
  33.1 1.6 %collective-permute-start.5 = (bf16[512,512]{1,0:T(8,128)(2,1)S(1)}, bf16[512,512]{1,0:T(8,128)(2,1)S(1)}, u32[]{:S(2)}, u32[]{:S(2)}) collective-permute-start(bf16[512,512]{1,0:T(8,128)(2,1)S(1)} %collective-permute-done.refs_1_), channel_id=1, source_target_pairs={{0,12},{4,0},{8,4},{12,8},{1,13},{5,1},{9,5},{13,9},{2,14},{6,2},{... | collective-permute-start | bytes 1572872 | tf_op jit(solution)/shard_map/ppermute | solution.py:128
  34.7 0.3 collective-permute-start.7
  34.9 0.0 collective-permute-start.6
  34.9 8.2 %collective-permute-done.3 = bf16[512,512]{1,0:T(8,128)(2,1)S(1)} collective-permute-done((bf16[512,512]{1,0:T(8,128)(2,1)S(1)}, bf16[512,512]{1,0:T(8,128)(2,1)S(1)}, u32[]{:S(2)}, u32[]{:S(2)}) %collective-permute-start.3) | collective-permute-done | bytes 524320 | tf_op jit(solution)/shard_map/ppermute | solution.py:128
  43.1 2.5 %collective-permute-start.8 = (bf16[512,512]{1,0:T(8,128)(2,1)S(1)}, bf16[512,512]{1,0:T(8,128)(2,1)S(1)}, u32[]{:S(2)}, u32[]{:S(2)}) collective-permute-start(bf16[512,512]{1,0:T(8,128)(2,1)S(1)} %get-tuple-element.46.refs_0_), channel_id=1, source_target_pairs={{0,17},{17,0},{1,16},{16,1},{2,19},{19,2},{3,18},{18,3},{4,21},{21... | collective-permute-start | bytes 1572872 | tf_op jit(solution)/shard_map/ppermute | solution.py:131
  45.7 0.7 collective-permute-done.4
  46.4 0.0 collective-permute-done.5.refs_2_
  46.4 2.2 %collective-permute-done.6.refs_7_ = bf16[512,512]{1,0:T(8,128)(2,1)} collective-permute-done((bf16[512,512]{1,0:T(8,128)(2,1)S(1)}, bf16[512,512]{1,0:T(8,128)(2,1)}, u32[]{:S(2)}, u32[]{:S(2)}) %collective-permute-start.6) | collective-permute-done | bytes 524320 | tf_op jit(solution)/shard_map/ppermute | solution.py:129
  48.6 0.0 collective-permute-done.7.refs_9_
  48.6 0.8 copy-done.3
  49.4 6.7 %collective-permute-done.8.refs_12_ = bf16[512,512]{1,0:T(8,128)(2,1)S(1)} collective-permute-done((bf16[512,512]{1,0:T(8,128)(2,1)S(1)}, bf16[512,512]{1,0:T(8,128)(2,1)S(1)}, u32[]{:S(2)}, u32[]{:S(2)}) %collective-permute-start.8) | collective-permute-done | bytes 524320 | tf_op jit(solution)/shard_map/ppermute | solution.py:131
  56.1 3.6 %collective-permute-start.9 = (bf16[512,512]{1,0:T(8,128)(2,1)S(1)}, bf16[512,512]{1,0:T(8,128)(2,1)S(1)}, u32[]{:S(2)}, u32[]{:S(2)}) collective-permute-start(bf16[512,512]{1,0:T(8,128)(2,1)S(1)} %collective-permute-done.3), channel_id=1, source_target_pairs={{0,224},{32,0},{64,32},{96,64},{128,96},{160,128},{192,160},{224,1... | collective-permute-start | bytes 1572872 | tf_op jit(solution)/shard_map/ppermute | solution.py:128
  59.7 0.0 collective-permute-start.10
  59.7 3.0 %collective-permute-start.11 = (bf16[512,512]{1,0:T(8,128)(2,1)S(1)}, bf16[512,512]{1,0:T(8,128)(2,1)}, u32[]{:S(2)}, u32[]{:S(2)}) collective-permute-start(bf16[512,512]{1,0:T(8,128)(2,1)S(1)} %collective-permute-done.2.refs_4_), channel_id=1, source_target_pairs={{0,12},{4,0},{8,4},{12,8},{1,13},{5,1},{9,5},{13,9},{2,14},{6,2},{... | collective-permute-start | bytes 1572872 | tf_op jit(solution)/shard_map/ppermute | solution.py:128
  62.8 0.0 collective-permute-start.12
  62.8 0.0 collective-permute-start.13
  62.8 5.6 %collective-permute-done.9 = bf16[512,512]{1,0:T(8,128)(2,1)S(1)} collective-permute-done((bf16[512,512]{1,0:T(8,128)(2,1)S(1)}, bf16[512,512]{1,0:T(8,128)(2,1)S(1)}, u32[]{:S(2)}, u32[]{:S(2)}) %collective-permute-start.9) | collective-permute-done | bytes 524320 | tf_op jit(solution)/shard_map/ppermute | solution.py:128
  68.4 0.8 copy-done.8
  69.2 4.3 %collective-permute-start.14 = (bf16[512,512]{1,0:T(8,128)(2,1)S(1)}, bf16[512,512]{1,0:T(8,128)(2,1)}, u32[]{:S(2)}, u32[]{:S(2)}) collective-permute-start(bf16[512,512]{1,0:T(8,128)(2,1)S(1)} %collective-permute-done.refs_1_), channel_id=1, source_target_pairs={{0,17},{17,0},{1,16},{16,1},{2,19},{19,2},{3,18},{18,3},{4,21},{21... | collective-permute-start | bytes 1572872 | tf_op jit(solution)/shard_map/ppermute | solution.py:131
  73.5 0.1 stack.59.pos_ref
  73.6 0.0 collective-permute-done.10
  73.6 0.0 collective-permute-done.11.refs_5_
  73.6 1.5 %collective-permute-done.12.refs_6_ = bf16[512,512]{1,0:T(8,128)(2,1)} collective-permute-done((bf16[512,512]{1,0:T(8,128)(2,1)}, bf16[512,512]{1,0:T(8,128)(2,1)}, u32[]{:S(2)}, u32[]{:S(2)}) %collective-permute-start.12) | collective-permute-done | bytes 524320 | tf_op jit(solution)/shard_map/ppermute | solution.py:129
  75.2 0.0 collective-permute-done.13.refs_11_
  75.2 8.2 %collective-permute-done.14.refs_13_ = bf16[512,512]{1,0:T(8,128)(2,1)} collective-permute-done((bf16[512,512]{1,0:T(8,128)(2,1)S(1)}, bf16[512,512]{1,0:T(8,128)(2,1)}, u32[]{:S(2)}, u32[]{:S(2)}) %collective-permute-start.14) | collective-permute-done | bytes 524320 | tf_op jit(solution)/shard_map/ppermute | solution.py:131
  83.4 0.0 collective-permute-start.17
  83.4 2.4 %collective-permute-start.18 = (bf16[512,512]{1,0:T(8,128)(2,1)}, bf16[512,512]{1,0:T(8,128)(2,1)S(1)}, u32[]{:S(2)}, u32[]{:S(2)}) collective-permute-start(bf16[512,512]{1,0:T(8,128)(2,1)} %copy-done.1), channel_id=1, source_target_pairs={{0,17},{17,0},{1,16},{16,1},{2,19},{19,2},{3,18},{18,3},{4,21},{21... | collective-permute-start | bytes 1572872 | tf_op jit(solution)/shard_map/ppermute | solution.py:131
  85.7 3.6 %collective-permute-start.15 = (bf16[512,512]{1,0:T(8,128)(2,1)}, bf16[512,512]{1,0:T(8,128)(2,1)S(1)}, u32[]{:S(2)}, u32[]{:S(2)}) collective-permute-start(bf16[512,512]{1,0:T(8,128)(2,1)} %copy-done.8), channel_id=1, source_target_pairs={{0,224},{32,0},{64,32},{96,64},{128,96},{160,128},{192,160},{224,1... | collective-permute-start | bytes 1572872 | tf_op jit(solution)/shard_map/ppermute | solution.py:128
  89.4 0.0 collective-permute-start.16
  89.4 0.0 collective-permute-start.19
  89.4 1.2 bitcast_dynamic-update-slice_fusion.5
  90.6 1.1 bitcast_dynamic-update-slice_fusion.4
  91.7 5.6 %collective-permute-done.15 = bf16[512,512]{1,0:T(8,128)(2,1)S(1)} collective-permute-done((bf16[512,512]{1,0:T(8,128)(2,1)}, bf16[512,512]{1,0:T(8,128)(2,1)S(1)}, u32[]{:S(2)}, u32[]{:S(2)}) %collective-permute-start.15) | collective-permute-done | bytes 524320 | tf_op jit(solution)/shard_map/ppermute | solution.py:128
  97.3 3.0 %collective-permute-done.16 = bf16[512,512]{1,0:T(8,128)(2,1)S(1)} collective-permute-done((bf16[512,512]{1,0:T(8,128)(2,1)}, bf16[512,512]{1,0:T(8,128)(2,1)S(1)}, u32[]{:S(2)}, u32[]{:S(2)}) %collective-permute-start.16) | collective-permute-done | bytes 524320 | tf_op jit(solution)/shard_map/ppermute | solution.py:129
  100.3 0.0 collective-permute-done.17.refs_10_
  100.3 0.0 collective-permute-done.18.refs_14_
  100.5 1.1 bitcast_dynamic-update-slice_fusion.1
  101.6 1.1 bitcast_dynamic-update-slice_fusion.w_ref
  102.7 2.5 %collective-permute-start.20 = (bf16[256,512]{1,0:T(8,128)(2,1)S(1)}, bf16[256,512]{1,0:T(8,128)(2,1)S(1)}, u32[]{:S(2)}, u32[]{:S(2)}) collective-permute-start(bf16[256,512]{1,0:T(8,128)(2,1)S(1)} %slice.6), channel_id=1, source_target_pairs={{0,224},{32,0},{64,32},{96,64},{128,96},{160,128},{192,160},{224,1... | collective-permute-start | bytes 786440 | tf_op jit(solution)/shard_map/ppermute | solution.py:128
  105.1 0.0 collective-permute-start.21
  105.1 6.2 %shard_map.30 = (f32[512,512]{1,0:T(8,128)S(1)}, f32[512,512]{1,0:T(8,128)S(1)}) custom-call(s32[8]{0:T(128)S(1)} %stack.59.pos_ref, bf16[8,512,512]{2,1,0:T(8,128)(2,1)S(1)} %bitcast_dynamic-update-slice_fusion.w_ref, bf16[512,512]{1,0:T(8,128)(2,1)S(1)} %get-tuple-element.46.refs_0_, bf16[512,512]{1,0:T(8,128)(2,1)S(1)} %collective-permute-done.refs_1_, ...), custom_call_target="tpu_custom_call" | custom-call | flops 4294967296 | bytes 12582912 | tf_op jit(solution)/shard_map/pallas_call | solution.py:164
  111.3 0.2 collective-permute-done.21.bottom_ref
  111.6 2.5 %shard_map.31 = (f32[512,512]{1,0:T(8,128)S(1)}, f32[512,512]{1,0:T(8,128)S(1)}) custom-call(s32[8]{0:T(128)S(1)} %stack.59.pos_ref, s32[1]{0:T(128)} %bitcast.8.keep_ref, f32[512,512]{1,0:T(8,128)S(1)} %get-tuple-element.71.first_ref, f32[512,512]{1,0:T(8,128)S(1)} %get-tuple-element.72.second_ref, bf16[256,512]{1,0:T(8,128)(2,1)S(1)} %collective-permute-done.20.top_ref, ...), custom_call_target="tpu_custom_call" | custom-call | flops 536870912 | bytes 4194304 | tf_op jit(solution)/shard_map/pallas_call | solution.py:167
  114.1 6.8 %collective-permute-start.22 = (f32[512,512]{1,0:T(8,128)S(1)}, f32[512,512]{1,0:T(8,128)S(1)}, u32[]{:S(2)}, u32[]{:S(2)}) collective-permute-start(f32[512,512]{1,0:T(8,128)S(1)} %get-tuple-element.74), channel_id=1, source_target_pairs={{0,2},{2,0},{1,3},{3,1},{4,6},{6,4},{5,7},{7,5},{8,10},{10,8},{9,1... | collective-permute-start | bytes 3145736 | tf_op jit(solution)/shard_map/ppermute | solution.py:176
  120.9 2.3 %collective-permute-done.22.got_ref = f32[512,512]{1,0:T(8,128)S(1)} collective-permute-done((f32[512,512]{1,0:T(8,128)S(1)}, f32[512,512]{1,0:T(8,128)S(1)}, u32[]{:S(2)}, u32[]{:S(2)}) %collective-permute-start.22) | collective-permute-done | bytes 1048608 | tf_op jit(solution)/shard_map/ppermute | solution.py:176
  123.2 1.4 shard_map.32
  124.6 5.8 %all-to-all-start.1 = ((bf16[256,8,128]{2,1,0:T(8,128)(2,1)}), bf16[256,8,128]{2,1,0:T(8,128)(2,1)S(1)}, u32[]{:S(2)}, u32[]{:S(2)}) async-start(bf16[256,8,128]{2,1,0:T(8,128)(2,1)} %bitcast.18), calls=%async_computation.1 | async-start | bytes 1048576 | tf_op jit(solution)/shard_map/all_to_all | solution.py:181
  130.5 3.5 %collective-permute-start.23 = (bf16[512,512]{1,0:T(8,128)(2,1)S(1)}, bf16[512,512]{1,0:T(8,128)(2,1)S(1)}, u32[]{:S(2)}, u32[]{:S(2)}) collective-permute-start(bf16[512,512]{1,0:T(8,128)(2,1)S(1)} %get-tuple-element.75), channel_id=1, source_target_pairs={{0,0},{1,2},{2,1},{3,3},{4,4},{5,6},{6,5},{7,7},{8,8},{9,10},{10,9... | collective-permute-start | bytes 1572872 | tf_op jit(solution)/shard_map/ppermute | solution.py:180
  134.0 11.2 %collective-permute-done.23.direct_ref = bf16[512,512]{1,0:T(8,128)(2,1)S(1)} collective-permute-done((bf16[512,512]{1,0:T(8,128)(2,1)S(1)}, bf16[512,512]{1,0:T(8,128)(2,1)S(1)}, u32[]{:S(2)}, u32[]{:S(2)}) %collective-permute-start.23) | collective-permute-done | bytes 524320 | tf_op jit(solution)/shard_map/ppermute | solution.py:180
  145.2 5.2 %all-to-all-done.1 = bf16[256,8,128]{2,1,0:T(8,128)(2,1)S(1)} async-done(((bf16[256,8,128]{2,1,0:T(8,128)(2,1)}), bf16[256,8,128]{2,1,0:T(8,128)(2,1)S(1)}, u32[]{:S(2)}, u32[]{:S(2)}) %all-to-all-start.1) | async-done | bytes 524320 | tf_op jit(solution)/shard_map/all_to_all | solution.py:181
  150.4 1.4 shard_map.33
  (23 shorter events, 0.2 us)
Async XLA Ops:
  1.3 26.1 %collective-permute-start = (bf16[512,512]{1,0:T(8,128)(2,1)S(1)}, bf16[512,512]{1,0:T(8,128)(2,1)S(1)}, u32[]{:S(2)}, u32[]{:S(2)}) collective-permute-start(bf16[512,512]{1,0:T(8,128)(2,1)S(1)} %get-tuple-element.46.refs_0_), channel_id=1, source_target_pairs={{0,12},{4,0},{8,4},{12,8},{1,13},{5,1},{9,5},{13,9},{2,14},{6,2},{... | collective-permute-start | bytes 1572872 | tf_op jit(solution)/shard_map/ppermute | solution.py:128
  4.9 22.5 %collective-permute-start.1 = (bf16[512,512]{1,0:T(8,128)(2,1)S(1)}, bf16[512,512]{1,0:T(8,128)(2,1)S(1)}, u32[]{:S(2)}, u32[]{:S(2)}) collective-permute-start(bf16[512,512]{1,0:T(8,128)(2,1)S(1)} %get-tuple-element.46.refs_0_), channel_id=1, source_target_pairs={{0,4},{4,8},{8,12},{12,0},{1,5},{5,9},{9,13},{13,1},{2,6},{6,10},{... | collective-permute-start | bytes 1572872 | tf_op jit(solution)/shard_map/ppermute | solution.py:129
  4.9 22.5 %collective-permute-start.2 = (bf16[512,512]{1,0:T(8,128)(2,1)S(1)}, bf16[512,512]{1,0:T(8,128)(2,1)S(1)}, u32[]{:S(2)}, u32[]{:S(2)}) collective-permute-start(bf16[512,512]{1,0:T(8,128)(2,1)S(1)} %get-tuple-element.64.refs_8_), channel_id=1, source_target_pairs={{0,17},{17,0},{1,16},{16,1},{2,19},{19,2},{3,18},{18,3},{4,21},{21... | collective-permute-start | bytes 1572872 | tf_op jit(solution)/shard_map/ppermute | solution.py:131
  7.4 1.2 copy-start
  27.4 15.7 %collective-permute-start.3 = (bf16[512,512]{1,0:T(8,128)(2,1)S(1)}, bf16[512,512]{1,0:T(8,128)(2,1)S(1)}, u32[]{:S(2)}, u32[]{:S(2)}) collective-permute-start(bf16[512,512]{1,0:T(8,128)(2,1)S(1)} %shard_map.29), channel_id=1, source_target_pairs={{0,224},{32,0},{64,32},{96,64},{128,96},{160,128},{192,160},{224,1... | collective-permute-start | bytes 1572872 | tf_op jit(solution)/shard_map/ppermute | solution.py:128
  33.1 13.3 %collective-permute-start.4 = (bf16[512,512]{1,0:T(8,128)(2,1)S(1)}, bf16[512,512]{1,0:T(8,128)(2,1)}, u32[]{:S(2)}, u32[]{:S(2)}) collective-permute-start(bf16[512,512]{1,0:T(8,128)(2,1)S(1)} %shard_map.29), channel_id=1, source_target_pairs={{0,32},{32,64},{64,96},{96,128},{128,160},{160,192},{192,224},{224... | collective-permute-start | bytes 1572872 | tf_op jit(solution)/shard_map/ppermute | solution.py:129
  33.1 13.3 %collective-permute-start.5 = (bf16[512,512]{1,0:T(8,128)(2,1)S(1)}, bf16[512,512]{1,0:T(8,128)(2,1)S(1)}, u32[]{:S(2)}, u32[]{:S(2)}) collective-permute-start(bf16[512,512]{1,0:T(8,128)(2,1)S(1)} %collective-permute-done.refs_1_), channel_id=1, source_target_pairs={{0,12},{4,0},{8,4},{12,8},{1,13},{5,1},{9,5},{13,9},{2,14},{6,2},{... | collective-permute-start | bytes 1572872 | tf_op jit(solution)/shard_map/ppermute | solution.py:128
  34.7 13.9 %collective-permute-start.7 = (bf16[512,512]{1,0:T(8,128)(2,1)S(1)}, bf16[512,512]{1,0:T(8,128)(2,1)S(1)}, u32[]{:S(2)}, u32[]{:S(2)}) collective-permute-start(bf16[512,512]{1,0:T(8,128)(2,1)S(1)} %collective-permute-done.refs_1_), channel_id=1, source_target_pairs={{0,1},{1,0},{16,17},{17,16},{2,3},{3,2},{18,19},{19,18},{4,5},{5,4... | collective-permute-start | bytes 1572872 | tf_op jit(solution)/shard_map/ppermute | solution.py:130
  34.9 13.7 %collective-permute-start.6 = (bf16[512,512]{1,0:T(8,128)(2,1)S(1)}, bf16[512,512]{1,0:T(8,128)(2,1)}, u32[]{:S(2)}, u32[]{:S(2)}) collective-permute-start(bf16[512,512]{1,0:T(8,128)(2,1)S(1)} %collective-permute-done.2.refs_4_), channel_id=1, source_target_pairs={{0,4},{4,8},{8,12},{12,0},{1,5},{5,9},{9,13},{13,1},{2,6},{6,10},{... | collective-permute-start | bytes 1572872 | tf_op jit(solution)/shard_map/ppermute | solution.py:129
  43.1 25.3 %copy-start.7 = (bf16[512,512]{1,0:T(8,128)(2,1)}, bf16[512,512]{1,0:T(8,128)(2,1)S(1)}, u32[]{:S(2)}) copy-start(bf16[512,512]{1,0:T(8,128)(2,1)S(1)} %collective-permute-done.3) | copy-start | bytes 1572868
  43.1 12.9 %collective-permute-start.8 = (bf16[512,512]{1,0:T(8,128)(2,1)S(1)}, bf16[512,512]{1,0:T(8,128)(2,1)S(1)}, u32[]{:S(2)}, u32[]{:S(2)}) collective-permute-start(bf16[512,512]{1,0:T(8,128)(2,1)S(1)} %get-tuple-element.46.refs_0_), channel_id=1, source_target_pairs={{0,17},{17,0},{1,16},{16,1},{2,19},{19,2},{3,18},{18,3},{4,21},{21... | collective-permute-start | bytes 1572872 | tf_op jit(solution)/shard_map/ppermute | solution.py:131
  46.4 16.4 %copy-start.1 = (bf16[512,512]{1,0:T(8,128)(2,1)}, bf16[512,512]{1,0:T(8,128)(2,1)S(1)}, u32[]{:S(2)}) copy-start(bf16[512,512]{1,0:T(8,128)(2,1)S(1)} %collective-permute-done.5.refs_2_) | copy-start | bytes 1572868
  48.6 0.8 copy-start.3
  56.1 12.4 %copy-start.5 = (bf16[512,512]{1,0:T(8,128)(2,1)}, bf16[512,512]{1,0:T(8,128)(2,1)S(1)}, u32[]{:S(2)}) copy-start(bf16[512,512]{1,0:T(8,128)(2,1)S(1)} %collective-permute-done.8.refs_12_) | copy-start | bytes 1572868
  56.1 12.3 %collective-permute-start.9 = (bf16[512,512]{1,0:T(8,128)(2,1)S(1)}, bf16[512,512]{1,0:T(8,128)(2,1)S(1)}, u32[]{:S(2)}, u32[]{:S(2)}) collective-permute-start(bf16[512,512]{1,0:T(8,128)(2,1)S(1)} %collective-permute-done.3), channel_id=1, source_target_pairs={{0,224},{32,0},{64,32},{96,64},{128,96},{160,128},{192,160},{224,1... | collective-permute-start | bytes 1572872 | tf_op jit(solution)/shard_map/ppermute | solution.py:128
  59.7 13.9 %collective-permute-start.10 = (bf16[512,512]{1,0:T(8,128)(2,1)}, bf16[512,512]{1,0:T(8,128)(2,1)}, u32[]{:S(2)}, u32[]{:S(2)}) collective-permute-start(bf16[512,512]{1,0:T(8,128)(2,1)} %collective-permute-done.4), channel_id=1, source_target_pairs={{0,32},{32,64},{64,96},{96,128},{128,160},{160,192},{192,224},{224... | collective-permute-start | bytes 1572872 | tf_op jit(solution)/shard_map/ppermute | solution.py:129
  59.7 13.9 %collective-permute-start.11 = (bf16[512,512]{1,0:T(8,128)(2,1)S(1)}, bf16[512,512]{1,0:T(8,128)(2,1)}, u32[]{:S(2)}, u32[]{:S(2)}) collective-permute-start(bf16[512,512]{1,0:T(8,128)(2,1)S(1)} %collective-permute-done.2.refs_4_), channel_id=1, source_target_pairs={{0,12},{4,0},{8,4},{12,8},{1,13},{5,1},{9,5},{13,9},{2,14},{6,2},{... | collective-permute-start | bytes 1572872 | tf_op jit(solution)/shard_map/ppermute | solution.py:128
  62.8 12.4 %collective-permute-start.12 = (bf16[512,512]{1,0:T(8,128)(2,1)}, bf16[512,512]{1,0:T(8,128)(2,1)}, u32[]{:S(2)}, u32[]{:S(2)}) collective-permute-start(bf16[512,512]{1,0:T(8,128)(2,1)} %collective-permute-done.6.refs_7_), channel_id=1, source_target_pairs={{0,4},{4,8},{8,12},{12,0},{1,5},{5,9},{9,13},{13,1},{2,6},{6,10},{... | collective-permute-start | bytes 1572872 | tf_op jit(solution)/shard_map/ppermute | solution.py:129
  62.8 12.4 %collective-permute-start.13 = (bf16[512,512]{1,0:T(8,128)(2,1)S(1)}, bf16[512,512]{1,0:T(8,128)(2,1)}, u32[]{:S(2)}, u32[]{:S(2)}) collective-permute-start(bf16[512,512]{1,0:T(8,128)(2,1)S(1)} %collective-permute-done.1.refs_3_), channel_id=1, source_target_pairs={{0,1},{1,0},{16,17},{17,16},{2,3},{3,2},{18,19},{19,18},{4,5},{5,4... | collective-permute-start | bytes 1572872 | tf_op jit(solution)/shard_map/ppermute | solution.py:130
  68.4 0.8 copy-start.8
  69.2 14.1 %collective-permute-start.14 = (bf16[512,512]{1,0:T(8,128)(2,1)S(1)}, bf16[512,512]{1,0:T(8,128)(2,1)}, u32[]{:S(2)}, u32[]{:S(2)}) collective-permute-start(bf16[512,512]{1,0:T(8,128)(2,1)S(1)} %collective-permute-done.refs_1_), channel_id=1, source_target_pairs={{0,17},{17,0},{1,16},{16,1},{2,19},{19,2},{3,18},{18,3},{4,21},{21... | collective-permute-start | bytes 1572872 | tf_op jit(solution)/shard_map/ppermute | solution.py:131
  83.4 17.0 %collective-permute-start.17 = (bf16[512,512]{1,0:T(8,128)(2,1)}, bf16[512,512]{1,0:T(8,128)(2,1)S(1)}, u32[]{:S(2)}, u32[]{:S(2)}) collective-permute-start(bf16[512,512]{1,0:T(8,128)(2,1)} %copy-done.1), channel_id=1, source_target_pairs={{0,1},{1,0},{16,17},{17,16},{2,3},{3,2},{18,19},{19,18},{4,5},{5,4... | collective-permute-start | bytes 1572872 | tf_op jit(solution)/shard_map/ppermute | solution.py:130
  83.4 17.0 %collective-permute-start.18 = (bf16[512,512]{1,0:T(8,128)(2,1)}, bf16[512,512]{1,0:T(8,128)(2,1)S(1)}, u32[]{:S(2)}, u32[]{:S(2)}) collective-permute-start(bf16[512,512]{1,0:T(8,128)(2,1)} %copy-done.1), channel_id=1, source_target_pairs={{0,17},{17,0},{1,16},{16,1},{2,19},{19,2},{3,18},{18,3},{4,21},{21... | collective-permute-start | bytes 1572872 | tf_op jit(solution)/shard_map/ppermute | solution.py:131
  85.7 11.5 %collective-permute-start.15 = (bf16[512,512]{1,0:T(8,128)(2,1)}, bf16[512,512]{1,0:T(8,128)(2,1)S(1)}, u32[]{:S(2)}, u32[]{:S(2)}) collective-permute-start(bf16[512,512]{1,0:T(8,128)(2,1)} %copy-done.8), channel_id=1, source_target_pairs={{0,224},{32,0},{64,32},{96,64},{128,96},{160,128},{192,160},{224,1... | collective-permute-start | bytes 1572872 | tf_op jit(solution)/shard_map/ppermute | solution.py:128
  89.4 10.9 %collective-permute-start.16 = (bf16[512,512]{1,0:T(8,128)(2,1)}, bf16[512,512]{1,0:T(8,128)(2,1)S(1)}, u32[]{:S(2)}, u32[]{:S(2)}) collective-permute-start(bf16[512,512]{1,0:T(8,128)(2,1)} %collective-permute-done.10), channel_id=1, source_target_pairs={{0,32},{32,64},{64,96},{96,128},{128,160},{160,192},{192,224},{224... | collective-permute-start | bytes 1572872 | tf_op jit(solution)/shard_map/ppermute | solution.py:129
  89.4 10.9 %collective-permute-start.19 = (bf16[512,512]{1,0:T(8,128)(2,1)}, bf16[512,512]{1,0:T(8,128)(2,1)S(1)}, u32[]{:S(2)}, u32[]{:S(2)}) collective-permute-start(bf16[512,512]{1,0:T(8,128)(2,1)} %copy-done.5), channel_id=1, source_target_pairs={{0,4},{4,8},{8,12},{12,0},{1,5},{5,9},{9,13},{13,1},{2,6},{6,10},{... | collective-permute-start | bytes 1572872 | tf_op jit(solution)/shard_map/ppermute | solution.py:129
  89.4 15.7 %copy-start.2 = (bf16[512,512]{1,0:T(8,128)(2,1)S(1)}, bf16[512,512]{1,0:T(8,128)(2,1)}, u32[]{:S(2)}) copy-start(bf16[512,512]{1,0:T(8,128)(2,1)} %copy-done.1) | copy-start | bytes 1572868
  89.4 15.7 %copy-start.4 = (bf16[512,512]{1,0:T(8,128)(2,1)S(1)}, bf16[512,512]{1,0:T(8,128)(2,1)}, u32[]{:S(2)}) copy-start(bf16[512,512]{1,0:T(8,128)(2,1)} %copy-done.3) | copy-start | bytes 1572868
  89.4 15.7 %copy-start.6 = (bf16[512,512]{1,0:T(8,128)(2,1)S(1)}, bf16[512,512]{1,0:T(8,128)(2,1)}, u32[]{:S(2)}) copy-start(bf16[512,512]{1,0:T(8,128)(2,1)} %copy-done.5) | copy-start | bytes 1572868
  102.7 8.7 %collective-permute-start.20 = (bf16[256,512]{1,0:T(8,128)(2,1)S(1)}, bf16[256,512]{1,0:T(8,128)(2,1)S(1)}, u32[]{:S(2)}, u32[]{:S(2)}) collective-permute-start(bf16[256,512]{1,0:T(8,128)(2,1)S(1)} %slice.6), channel_id=1, source_target_pairs={{0,224},{32,0},{64,32},{96,64},{128,96},{160,128},{192,160},{224,1... | collective-permute-start | bytes 786440 | tf_op jit(solution)/shard_map/ppermute | solution.py:128
  105.1 6.4 %collective-permute-start.21 = (bf16[256,512]{1,0:T(8,128)(2,1)S(1)}, bf16[256,512]{1,0:T(8,128)(2,1)S(1)}, u32[]{:S(2)}, u32[]{:S(2)}) collective-permute-start(bf16[256,512]{1,0:T(8,128)(2,1)S(1)} %slice.7), channel_id=1, source_target_pairs={{0,32},{32,64},{64,96},{96,128},{128,160},{160,192},{192,224},{224... | collective-permute-start | bytes 786440 | tf_op jit(solution)/shard_map/ppermute | solution.py:129
  114.1 9.1 %collective-permute-start.22 = (f32[512,512]{1,0:T(8,128)S(1)}, f32[512,512]{1,0:T(8,128)S(1)}, u32[]{:S(2)}, u32[]{:S(2)}) collective-permute-start(f32[512,512]{1,0:T(8,128)S(1)} %get-tuple-element.74), channel_id=1, source_target_pairs={{0,2},{2,0},{1,3},{3,1},{4,6},{6,4},{5,7},{7,5},{8,10},{10,8},{9,1... | collective-permute-start | bytes 3145736 | tf_op jit(solution)/shard_map/ppermute | solution.py:176
  124.6 25.7 %all-to-all-start.1 = ((bf16[256,8,128]{2,1,0:T(8,128)(2,1)}), bf16[256,8,128]{2,1,0:T(8,128)(2,1)S(1)}, u32[]{:S(2)}, u32[]{:S(2)}) async-start(bf16[256,8,128]{2,1,0:T(8,128)(2,1)} %bitcast.18), calls=%async_computation.1 | async-start | bytes 1048576 | tf_op jit(solution)/shard_map/all_to_all | solution.py:181
  130.5 14.7 %collective-permute-start.23 = (bf16[512,512]{1,0:T(8,128)(2,1)S(1)}, bf16[512,512]{1,0:T(8,128)(2,1)S(1)}, u32[]{:S(2)}, u32[]{:S(2)}) collective-permute-start(bf16[512,512]{1,0:T(8,128)(2,1)S(1)} %get-tuple-element.75), channel_id=1, source_target_pairs={{0,0},{1,2},{2,1},{3,3},{4,4},{5,6},{6,5},{7,7},{8,8},{9,10},{10,9... | collective-permute-start | bytes 1572872 | tf_op jit(solution)/shard_map/ppermute | solution.py:180

commit v3 on v2

--- a/solution.py
+++ b/solution.py
@@ -69,28 +69,28 @@
     return jnp.dot(a, b, preferred_element_type=F32)
 
 
-def product_early(pos_ref, w_ref, *refs):
-    for half in range(2):
+def product_early(pos_ref, *refs):
+    chunks, pieces, (sum_ref, far_ref, held) = refs[:7], refs[7:15], refs[15:]
+    for j, chunk in zip((0, 1, 2, 3, 5, 6, 7), chunks):
+        held[j] = chunk[...]
+    held[4] = jnp.zeros((B, B), BF16)
+    for rows in (slice(0, B), slice(B, 2 * B)):
         total = None
         for p in range(8):
-            term = dot(refs[half * 8 + p][...], w_ref[pos_ref[p]])
+            term = dot(pieces[p][rows], held[pos_ref[p]])
             total = term if total is None else total + term
-        refs[16 + half][...] = total
-
-
-def product_late(pos_ref, keep_ref, first_ref, second_ref, top_ref, bottom_ref, *refs):
-    kept_ref, sent_ref, far_ref = refs[16:]
-    far_ref[:256] = top_ref[...]
-    far_ref[256:] = bottom_ref[...]
-    first_kept = keep_ref[0] == 0
+        sum_ref[rows] = total
     for p in range(8):
 
         @pl.when(pos_ref[p] == 4)
         def _(p=p):
-            first = first_ref[...] + dot(refs[p][...], far_ref[...])
-            second = second_ref[...] + dot(refs[8 + p][...], far_ref[...])
-            kept_ref[...] = jnp.where(first_kept, first, second)
-            sent_ref[...] = jnp.where(first_kept, second, first)
+            far_ref[...] = pieces[p][...]
+
+
+def product_late(half_ref, sum_ref, far_ref, top_ref, bottom_ref, out_ref):
+    rows = pl.ds(pl.multiple_of(half_ref[0] * B, B), B)
+    block = far_ref[rows, :]
+    out_ref[...] = sum_ref[rows, :] + dot(block[:, : B // 2], top_ref[...]) + dot(block[:, B // 2 :], bottom_ref[...])
 
 
 def spread(kept_ref, got_ref, direct_ref, mirror_ref):
@@ -118,62 +118,71 @@
     return [(i, (i + step) % n) for i in range(n)]
 
 
-def lockstep(*groups):
-    return lax.optimization_barrier(groups)
+def along_y(v):
+    perm = []
+    for y in range(4):
+        for core in range(2):
+            for rep in range(2):
+                to = (y + (1 if core ^ rep else -1)) % 4
+                perm.append(((y * 2 + core) * 2 + rep, (to * 2 + core) * 2 + rep))
+    return lax.ppermute(v, ("y", "core", "rep"), perm)
 
 
 def local(amplitudes, intermediate):
     z, xh, y, core, rep = (lax.axis_index(a) for a in AXES)
     shape = jax.ShapeDtypeStruct
-    up = lambda v, axis, n: lax.ppermute(v, axis, ring(n, -1))
-    down = lambda v, axis, n: lax.ppermute(v, axis, ring(n, 1))
     pair = lambda v: lax.ppermute(v, X_LINE, PAIR)
     cross = lambda v: lax.ppermute(v, X_LINE, CROSS)
+    above = lambda v: lax.ppermute(v, "row", ring(8, -1))
+    below = lambda v: lax.ppermute(v, "row", ring(8, 1))
 
-    f00 = lax.dynamic_slice_in_dim(amplitudes, rep * B, B, 0)
-    g00 = lax.dynamic_slice_in_dim(amplitudes, (1 - rep) * B, B, 0)
-    f01, f03, f10 = up(f00, "y", 4), down(f00, "y", 4), cross(g00)
+    step = 1 - 2 * (core ^ rep)
+    position = jnp.stack(
+        [(4 * ((xh + i) % 2) + (y + j + 4) % 4 - z + 8) % 8 for i in range(2) for j in (0, step, 2, -step)]
+    ).astype(jnp.int32)
+    halves = jnp.stack([core, 1 - core]).astype(jnp.int32)
+    rep = rep.reshape(1).astype(jnp.int32)
+    position, halves, rep, intermediate, own = lax.optimization_barrier(
+        (position, halves, rep, intermediate, amplitudes)
+    )
 
-    intermediate, f00, g00 = lax.optimization_barrier((intermediate, f00, g00))
-    packed = call(w_pack, [shape((8, 2, 128, 128), BF16)], 1, 1, moved=2 << 20)(
-        rep.reshape(1).astype(jnp.int32), intermediate
-    )[0]
+    packed = call(w_pack, [shape((8, 2, 128, 128), BF16)], 1, 1, moved=2 << 20)(rep, intermediate)[0]
     arrived = lax.all_to_all(packed.reshape(16, 128, 128), ("xh", "y", "core"), split_axis=0, concat_axis=0, tiled=True)
     w0 = call(w_unpack, [shape((B, B), BF16)], 0, 1, moved=1 << 20)(arrived)[0]
 
-    w0, f00, f01, f03, f10 = lockstep(w0, f00, f01, f03, f10)
-    w1, w7 = up(w0, "row", 8), down(w0, "row", 8)
-    f02, f13, g01, g10 = up(f01, "y", 4), down(f10, "y", 4), pair(f01), cross(f00)
+    y1, c1_top = along_y(own), cross(own[:B])
+    w0, y1, c1_top = lax.optimization_barrier((w0, y1, c1_top))
+    w1, w7 = above(w0), below(w0)
+    y2, p1, c1_bottom = along_y(y1), pair(y1), cross(own[B:])
 
-    w1, w7, f02, f13, g01, g10, f10, f03, f01 = lockstep(w1, w7, f02, f13, g01, g10, f10, f03, f01)
-    w2, w6 = up(w1, "row", 8), down(w7, "row", 8)
-    f11, f12, g03, g11 = up(f10, "y", 4), down(f13, "y", 4), pair(f03), cross(f01)
+    w1, w7, y2, c1_bottom, y1 = lax.optimization_barrier((w1, w7, y2, c1_bottom, y1))
+    c1 = jnp.concatenate([c1_top, c1_bottom])
+    w2, w6 = above(w1), below(w7)
+    y3, c2 = along_y(c1), cross(y1)
 
-    w2, w6, f11, f12, g03, g11, f02, g10 = lockstep(w2, w6, f11, f12, g03, g11, f02, g10)
-    w3, w5 = up(w2, "row", 8), down(w6, "row", 8)
-    g02, g12, g13 = pair(f02), cross(f02), down(g10, "y", 4)
+    w2, w6, y3, p1 = lax.optimization_barrier((w2, w6, y3, p1))
+    w3, w5 = above(w2), below(w6)
+    y4 = along_y(y3)
 
-    w3, w5, g02, g12, g13 = lockstep(w3, w5, g02, g12, g13)
-    top, bottom = up(w3[:256], "row", 8), down(w5[256:], "row", 8)
+    w3, w5, y4, c2 = lax.optimization_barrier((w3, w5, y4, c2))
+    top, bottom = above(w3[: B // 2]), below(w5[B // 2 :])
 
-    pieces = (f00, f01, f02, f03, f10, f11, f12, f13, g00, g01, g02, g03, g10, g11, g12, g13)
-    position = jnp.stack(
-        [(4 * lax.rem(xh + i, 2) + lax.rem(y + j, 4) - z + 8) % 8 for i in range(2) for j in range(4)]
-    ).astype(jnp.int32)
-    stack = jnp.stack([w0, w1, w2, w3, jnp.zeros((B, B), BF16), w5, w6, w7])
-    first, second = call(
-        product_early, [shape((B, B), F32)] * 2, 1, 17, flops=32 * B**3, moved=12 << 20
-    )(position, stack, *pieces)
-    kept, sent = call(
-        product_late,
-        [shape((B, B), F32)] * 2,
-        2,
-        4 + 16,
-        flops=4 * B**3,
-        moved=4 << 20,
-        scratch=[pltpu.VMEM((B, B), BF16)],
-    )(position, (core ^ rep).reshape(1).astype(jnp.int32), first, second, top, bottom, *pieces)
+    total, far = call(
+        product_early,
+        [shape((2 * B, B), F32), shape((2 * B, B), BF16)],
+        1,
+        15,
+        flops=32 * B**3,
+        moved=16 << 20,
+        scratch=[pltpu.VMEM((8, B, B), BF16)],
+        limit=28,
+    )(position, w0, w1, w2, w3, w5, w6, w7, own, y1, y2, p1, c1, y3, y4, c2)
+    late = lambda half: call(product_late, [shape((B, B), F32)], 1, 4, flops=2 * B**3, moved=4 << 20)(
+        half, total, far, top, bottom
+    )[0]
+    sent = late(halves[1:])
     got = lax.ppermute(sent, "core", [(0, 1), (1, 0)])
+    kept = late(halves[:1])
     direct, mirror = call(
         spread, [shape((B, B), BF16), shape((8, 16, 2, 8, 128), BF16)], 0, 2, moved=3 << 20
     )(kept, got)

time: 152 us -> 123 us (0.81)
  starting transfers between devices: 51.8 us -> 33.1 us
  local copies, waits for them, and re-layouts: 8.79 us -> 2.06 us
  blocking collectives: 17.2 us -> 15.4 us
    ppermute x15 -> x12, starting transfers between devices: 23.6 us -> 15.1 us  [the longest x4 6.13 us: local(): above = lambda v: lax.ppermute(v, 'row', ring(8, -1))]
    ppermute x15 -> x12, waiting for transfers between devices: 27.2 us -> 20.6 us  [the longest x4 13.1 us: local(): above = lambda v: lax.ppermute(v, 'row', ring(8, -1))]
    unnamed x25 -> x5, local copies, waits for them, and re-layouts: 6.32 us -> 0.04 us
    ppermute x3 -> x1, waiting for transfers between devices: 0.01 us -> 5.81 us  [local(): pair = lambda v: lax.ppermute(v, X_LINE, PAIR)]
    ppermute x1, starting transfers between devices: 6.84 us -> 1.63 us  [local(): got = lax.ppermute(sent, 'core', [(0, 1), (1, 0)])]
    ppermute x4 -> x3, starting transfers between devices: 11.7 us -> 7.37 us  [local(): cross = lambda v: lax.ppermute(v, X_LINE, CROSS)]
    slice x2 -> x4, local copies, waits for them, and re-layouts: 0.04 us -> 1.9 us  [the longest x1 1.27 us: local(): y2, p1, c1_bottom = (along_y(y1), pair(y1), cross(own[B:]))]
    all_to_all x1, blocking collectives: 17.2 us -> 15.4 us  [local(): lax.all_to_all(packed.reshape(16, 128, 128), ('xh', 'y', 'core'), split_a...]
  transfers between devices with their start and end apart: 25 -> 19, of which waited for: 13 -> 16; matrix products, arithmetic and copies ran while one was open for 2% -> 2% of each run, Pallas kernels for 5% -> 7%
where the time goes in v3:
time: 123 us
  waiting for transfers between devices  60 us (49%)
  starting transfers between devices  33.1 us (27%)
  blocking collectives  15.4 us (13%)
  Pallas kernels  12.1 us (10%)
  local copies, waits for them, and re-layouts  2.06 us (2%)
    ppermute x3, waiting for transfers between devices, local(): cross = lambda v: lax.ppermute(v, X_LINE, CROSS)  15.9 us
    all_to_all x1, blocking collectives, local(): lax.all_to_all(packed.reshape(16, 128, 128), ('xh', 'y', 'core'), split_a...  15.4 us
    ppermute x4, waiting for transfers between devices, local(): above = lambda v: lax.ppermute(v, 'row', ring(8, -1))  13.1 us
    ppermute x1, waiting for transfers between devices, local(): lax.ppermute(direct, ('core', 'rep'), [(0, 0), (1, 2), (2, 1), (3, 3)])  11.2 us
    ppermute x3, starting transfers between devices, local(): cross = lambda v: lax.ppermute(v, X_LINE, CROSS)  7.37 us
    ppermute x4, waiting for transfers between devices, local(): below = lambda v: lax.ppermute(v, 'row', ring(8, 1))  6.96 us
    ppermute x4, starting transfers between devices, local(): above = lambda v: lax.ppermute(v, 'row', ring(8, -1))  6.13 us
    ppermute x1, waiting for transfers between devices, local(): pair = lambda v: lax.ppermute(v, X_LINE, PAIR)  5.81 us
  transfers between devices with their start and end apart: 19, of which 16 were waited for; matrix products, arithmetic and copies ran while one was open for 2% of the time, Pallas kernels for 7%

profile of v3, /device:TPU:1, one launch (start us, length us, event | category | flops | bytes accessed | tf_op | source)
XLA Modules:
  0.0 122.9 jit_solution(6940422415830279416)
XLA Ops:
  0.0 0.0 copy-start
  0.0 0.1 pad_add_fusion
  0.1 0.1 stack.44.pos_ref
  0.2 2.1 %collective-permute-start = (bf16[1024,512]{1,0:T(8,128)(2,1)}, bf16[1024,512]{1,0:T(8,128)(2,1)S(1)}, u32[]{:S(2)}, u32[]{:S(2)}) collective-permute-start(bf16[1024,512]{1,0:T(8,128)(2,1)} %refs_7_), channel_id=1, source_target_pairs={{0,12},{1,5},{2,6},{3,15},{4,0},{5,9},{6,10},{7,3},{8,4},{9,13},{1... | collective-permute-start | bytes 3145736 | tf_op jit(solution)/shard_map/ppermute | solution.py:128
  2.3 1.3 %fusion = (bf16[512,512]{1,0:T(8,128)(2,1)S(1)}, bf16[512,512]{1,0:T(8,128)(2,1)S(1)}) fusion(bf16[1024,512]{1,0:T(8,128)(2,1)} %refs_7_), kind=kLoop, calls=%fused_computation.3 | loop fusion | bytes 2097152 | tf_op jit(solution)/shard_map/slice | solution.py:156
  3.6 4.0 %collective-permute-start.1 = (bf16[512,512]{1,0:T(8,128)(2,1)S(1)}, bf16[512,512]{1,0:T(8,128)(2,1)S(1)}, u32[]{:S(2)}, u32[]{:S(2)}) collective-permute-start(bf16[512,512]{1,0:T(8,128)(2,1)S(1)} %get-tuple-element.56), channel_id=1, source_target_pairs={{0,17},{17,0},{1,16},{16,1},{2,19},{19,2},{3,18},{18,3},{4,21},{21... | collective-permute-start | bytes 1572872 | tf_op jit(solution)/shard_map/ppermute | solution.py:135
  7.6 0.0 copy-done
  7.6 1.1 shard_map.28
  8.7 15.4 %all_to_all.10.in_ref = bf16[16,128,128]{2,1,0:T(8,128)(2,1)S(1)} all-to-all(bf16[16,128,128]{2,1,0:T(8,128)(2,1)S(1)} %bitcast.17), channel_id=1, replica_groups=mesh['row'=8,'xh'=2,'y'=4,'core'=2,'rep'=2] {'xh','y','core'}, dimensions={0} | all-to-all | bytes 1048576 | tf_op jit(solution)/shard_map/all_to_all | solution.py:150
  24.1 0.0 copy-start.1
  24.1 0.5 shard_map.29.refs_0_
  24.6 0.3 collective-permute-done.1
  24.9 0.0 collective-permute-done.refs_8_
  24.9 0.0 collective-permute-start.4
  24.9 3.4 %collective-permute-start.5 = (bf16[512,512]{1,0:T(8,128)(2,1)S(1)}, bf16[512,512]{1,0:T(8,128)(2,1)S(1)}, u32[]{:S(2)}, u32[]{:S(2)}) collective-permute-start(bf16[512,512]{1,0:T(8,128)(2,1)S(1)} %get-tuple-element.55), channel_id=1, source_target_pairs={{0,17},{17,0},{1,16},{16,1},{2,19},{19,2},{3,18},{18,3},{4,21},{21... | collective-permute-start | bytes 1572872 | tf_op jit(solution)/shard_map/ppermute | solution.py:135
  28.3 5.6 %collective-permute-start.2 = (bf16[512,512]{1,0:T(8,128)(2,1)S(1)}, bf16[512,512]{1,0:T(8,128)(2,1)S(1)}, u32[]{:S(2)}, u32[]{:S(2)}) collective-permute-start(bf16[512,512]{1,0:T(8,128)(2,1)S(1)} %shard_map.29.refs_0_), channel_id=1, source_target_pairs={{0,224},{32,0},{64,32},{96,64},{128,96},{160,128},{192,160},{224,1... | collective-permute-start | bytes 1572872 | tf_op jit(solution)/shard_map/ppermute | solution.py:136
  33.9 0.0 collective-permute-start.3
  33.9 0.0 collective-permute-start.9
  33.9 5.3 %collective-permute-done.5 = bf16[512,512]{1,0:T(8,128)(2,1)S(1)} collective-permute-done((bf16[512,512]{1,0:T(8,128)(2,1)S(1)}, bf16[512,512]{1,0:T(8,128)(2,1)S(1)}, u32[]{:S(2)}, u32[]{:S(2)}) %collective-permute-start.5) | collective-permute-done | bytes 524320 | tf_op jit(solution)/shard_map/ppermute | solution.py:135
  39.2 5.3 %collective-permute-done.2.refs_1_ = bf16[512,512]{1,0:T(8,128)(2,1)S(1)} collective-permute-done((bf16[512,512]{1,0:T(8,128)(2,1)S(1)}, bf16[512,512]{1,0:T(8,128)(2,1)S(1)}, u32[]{:S(2)}, u32[]{:S(2)}) %collective-permute-start.2) | collective-permute-done | bytes 524320 | tf_op jit(solution)/shard_map/ppermute | solution.py:136
  44.5 3.1 %collective-permute-done.3.refs_6_ = bf16[512,512]{1,0:T(8,128)(2,1)S(1)} collective-permute-done((bf16[512,512]{1,0:T(8,128)(2,1)S(1)}, bf16[512,512]{1,0:T(8,128)(2,1)S(1)}, u32[]{:S(2)}, u32[]{:S(2)}) %collective-permute-start.3) | collective-permute-done | bytes 524320 | tf_op jit(solution)/shard_map/ppermute | solution.py:137
  47.6 0.0 collective-permute-done.4.refs_9_
  47.6 2.7 %collective-permute-start.8 = (bf16[1024,512]{1,0:T(8,128)(2,1)S(1)}, bf16[1024,512]{1,0:T(8,128)(2,1)S(1)}, u32[]{:S(2)}, u32[]{:S(2)}) collective-permute-start(bf16[1024,512]{1,0:T(8,128)(2,1)S(1)} %constant_dynamic-update-slice_fusion.refs_11_), channel_id=1, source_target_pairs={{0,12},{1,5},{2,6},{3,15},{4,0},{5,9},{6,10},{7,3},{8,4},{9,13},{1... | collective-permute-start | bytes 3145736 | tf_op jit(solution)/shard_map/ppermute | solution.py:128
  50.3 0.3 collective-permute-start.6
  50.6 1.2 collective-permute-start.7
  51.8 0.0 collective-permute-start.13
  51.8 5.8 %collective-permute-done.9.refs_10_ = bf16[1024,512]{1,0:T(8,128)(2,1)S(1)} collective-permute-done((bf16[1024,512]{1,0:T(8,128)(2,1)S(1)}, bf16[1024,512]{1,0:T(8,128)(2,1)S(1)}, u32[]{:S(2)}, u32[]{:S(2)}) %collective-permute-start.9) | collective-permute-done | bytes 1048608 | tf_op jit(solution)/shard_map/ppermute | solution.py:134
  57.6 6.5 %collective-permute-done.6.refs_2_ = bf16[512,512]{1,0:T(8,128)(2,1)S(1)} collective-permute-done((bf16[512,512]{1,0:T(8,128)(2,1)S(1)}, bf16[512,512]{1,0:T(8,128)(2,1)S(1)}, u32[]{:S(2)}, u32[]{:S(2)}) %collective-permute-start.6) | collective-permute-done | bytes 524320 | tf_op jit(solution)/shard_map/ppermute | solution.py:136
  64.0 1.5 %collective-permute-done.7.refs_5_ = bf16[512,512]{1,0:T(8,128)(2,1)S(1)} collective-permute-done((bf16[512,512]{1,0:T(8,128)(2,1)S(1)}, bf16[512,512]{1,0:T(8,128)(2,1)S(1)}, u32[]{:S(2)}, u32[]{:S(2)}) %collective-permute-start.7) | collective-permute-done | bytes 524320 | tf_op jit(solution)/shard_map/ppermute | solution.py:137
  65.5 0.0 collective-permute-done.8.refs_12_
  65.5 0.0 collective-permute-start.12
  65.5 0.0 collective-permute-start.10
  65.6 1.5 %collective-permute-start.11 = (bf16[512,512]{1,0:T(8,128)(2,1)S(1)}, bf16[512,512]{1,0:T(8,128)(2,1)S(1)}, u32[]{:S(2)}, u32[]{:S(2)}) collective-permute-start(bf16[512,512]{1,0:T(8,128)(2,1)S(1)} %collective-permute-done.7.refs_5_), channel_id=1, source_target_pairs={{0,32},{32,64},{64,96},{96,128},{128,160},{160,192},{192,224},{224... | collective-permute-start | bytes 1572872 | tf_op jit(solution)/shard_map/ppermute | solution.py:137
  67.0 0.6 fusion.1
  67.6 10.3 %collective-permute-done.13.refs_14_ = bf16[1024,512]{1,0:T(8,128)(2,1)S(1)} collective-permute-done((bf16[1024,512]{1,0:T(8,128)(2,1)S(1)}, bf16[1024,512]{1,0:T(8,128)(2,1)S(1)}, u32[]{:S(2)}, u32[]{:S(2)}) %collective-permute-start.13) | collective-permute-done | bytes 1048608 | tf_op jit(solution)/shard_map/ppermute | solution.py:135
  77.9 1.0 collective-permute-done.10.refs_3_
  78.9 1.3 %collective-permute-done.11.refs_4_ = bf16[512,512]{1,0:T(8,128)(2,1)S(1)} collective-permute-done((bf16[512,512]{1,0:T(8,128)(2,1)S(1)}, bf16[512,512]{1,0:T(8,128)(2,1)S(1)}, u32[]{:S(2)}, u32[]{:S(2)}) %collective-permute-start.11) | collective-permute-done | bytes 524320 | tf_op jit(solution)/shard_map/ppermute | solution.py:137
  80.2 0.5 collective-permute-done.12.refs_13_
  80.7 0.3 collective-permute-start.14
  81.0 1.5 %collective-permute-start.15 = (bf16[256,512]{1,0:T(8,128)(2,1)S(1)}, bf16[256,512]{1,0:T(8,128)(2,1)S(1)}, u32[]{:S(2)}, u32[]{:S(2)}) collective-permute-start(bf16[256,512]{1,0:T(8,128)(2,1)S(1)} %slice.22), channel_id=1, source_target_pairs={{0,32},{32,64},{64,96},{96,128},{128,160},{160,192},{192,224},{224... | collective-permute-start | bytes 786440 | tf_op jit(solution)/shard_map/ppermute | solution.py:137
  82.5 0.0 copy-done.1
  82.5 5.4 %shard_map.30 = (f32[1024,512]{1,0:T(8,128)S(1)}, bf16[1024,512]{1,0:T(8,128)(2,1)S(1)}) custom-call(s32[8]{0:T(128)S(1)} %stack.44.pos_ref, bf16[512,512]{1,0:T(8,128)(2,1)S(1)} %shard_map.29.refs_0_, bf16[512,512]{1,0:T(8,128)(2,1)S(1)} %collective-permute-done.2.refs_1_, bf16[512,512]{1,0:T(8,128)(2,1)S(1)} %collective-permute-done.6.refs_2_, ...), custom_call_target="tpu_custom_call" | custom-call | flops 4294967296 | bytes 16777216 | tf_op jit(solution)/shard_map/pallas_call | solution.py:170
  88.0 0.4 collective-permute-done.14.top_ref
  88.4 1.1 collective-permute-done.15.bottom_ref
  89.5 1.1 shard_map.32
  90.6 1.6 %collective-permute-start.16 = (f32[512,512]{1,0:T(8,128)S(1)}, f32[512,512]{1,0:T(8,128)S(1)}, u32[]{:S(2)}, u32[]{:S(2)}) collective-permute-start(f32[512,512]{1,0:T(8,128)S(1)} %shard_map.32), channel_id=1, source_target_pairs={{0,2},{2,0},{1,3},{3,1},{4,6},{6,4},{5,7},{7,5},{8,10},{10,8},{9,1... | collective-permute-start | bytes 3145736 | tf_op jit(solution)/shard_map/ppermute | solution.py:184
  92.2 1.1 shard_map.31.kept_ref
  93.3 1.2 collective-permute-done.16.got_ref
  94.5 1.5 %shard_map.33 = (bf16[512,512]{1,0:T(8,128)(2,1)S(1)}, bf16[8,16,2,8,128]{4,3,2,1,0:T(8,128)(2,1)}) custom-call(f32[512,512]{1,0:T(8,128)S(1)} %shard_map.31.kept_ref, f32[512,512]{1,0:T(8,128)S(1)} %collective-permute-done.16.got_ref), custom_call_target="tpu_custom_call" | custom-call | bytes 3145728 | tf_op jit(solution)/shard_map/pallas_call | solution.py:186
  96.0 5.4 %all-to-all-start.1 = ((bf16[256,8,128]{2,1,0:T(8,128)(2,1)}), bf16[256,8,128]{2,1,0:T(8,128)(2,1)S(1)}, u32[]{:S(2)}, u32[]{:S(2)}) async-start(bf16[256,8,128]{2,1,0:T(8,128)(2,1)} %bitcast.12), calls=%async_computation.1 | async-start | bytes 1048576 | tf_op jit(solution)/shard_map/all_to_all | solution.py:190
  101.4 3.5 %collective-permute-start.17 = (bf16[512,512]{1,0:T(8,128)(2,1)S(1)}, bf16[512,512]{1,0:T(8,128)(2,1)S(1)}, u32[]{:S(2)}, u32[]{:S(2)}) collective-permute-start(bf16[512,512]{1,0:T(8,128)(2,1)S(1)} %get-tuple-element.53), channel_id=1, source_target_pairs={{0,0},{1,2},{2,1},{3,3},{4,4},{5,6},{6,5},{7,7},{8,8},{9,10},{10,9... | collective-permute-start | bytes 1572872 | tf_op jit(solution)/shard_map/ppermute | solution.py:189
  105.0 11.2 %collective-permute-done.17.direct_ref = bf16[512,512]{1,0:T(8,128)(2,1)S(1)} collective-permute-done((bf16[512,512]{1,0:T(8,128)(2,1)S(1)}, bf16[512,512]{1,0:T(8,128)(2,1)S(1)}, u32[]{:S(2)}, u32[]{:S(2)}) %collective-permute-start.17) | collective-permute-done | bytes 524320 | tf_op jit(solution)/shard_map/ppermute | solution.py:189
  116.2 5.3 %all-to-all-done.1 = bf16[256,8,128]{2,1,0:T(8,128)(2,1)S(1)} async-done(((bf16[256,8,128]{2,1,0:T(8,128)(2,1)}), bf16[256,8,128]{2,1,0:T(8,128)(2,1)S(1)}, u32[]{:S(2)}, u32[]{:S(2)}) %all-to-all-start.1) | async-done | bytes 524320 | tf_op jit(solution)/shard_map/all_to_all | solution.py:190
  121.4 1.4 %shard_map.34 = f32[512,512]{1,0:T(8,128)} custom-call(bf16[512,512]{1,0:T(8,128)(2,1)S(1)} %collective-permute-done.17.direct_ref, bf16[8,8,2,2,8,128]{5,4,3,2,1,0:T(8,128)(2,1)S(1)} %bitcast.18), custom_call_target="tpu_custom_call" | custom-call | bytes 2097152 | tf_op jit(solution)/shard_map/pallas_call | solution.py:191
  (4 shorter events, 0.1 us)
Async XLA Ops:
  0.0 7.6 %copy-start = (bf16[1024,512]{1,0:T(8,128)(2,1)S(1)}, bf16[1024,512]{1,0:T(8,128)(2,1)}, u32[]{:S(2)}) copy-start(bf16[1024,512]{1,0:T(8,128)(2,1)} %w_ref) | copy-start | bytes 3145732
  0.2 24.8 %collective-permute-start = (bf16[1024,512]{1,0:T(8,128)(2,1)}, bf16[1024,512]{1,0:T(8,128)(2,1)S(1)}, u32[]{:S(2)}, u32[]{:S(2)}) collective-permute-start(bf16[1024,512]{1,0:T(8,128)(2,1)} %refs_7_), channel_id=1, source_target_pairs={{0,12},{1,5},{2,6},{3,15},{4,0},{5,9},{6,10},{7,3},{8,4},{9,13},{1... | collective-permute-start | bytes 3145736 | tf_op jit(solution)/shard_map/ppermute | solution.py:128
  3.6 21.4 %collective-permute-start.1 = (bf16[512,512]{1,0:T(8,128)(2,1)S(1)}, bf16[512,512]{1,0:T(8,128)(2,1)S(1)}, u32[]{:S(2)}, u32[]{:S(2)}) collective-permute-start(bf16[512,512]{1,0:T(8,128)(2,1)S(1)} %get-tuple-element.56), channel_id=1, source_target_pairs={{0,17},{17,0},{1,16},{16,1},{2,19},{19,2},{3,18},{18,3},{4,21},{21... | collective-permute-start | bytes 1572872 | tf_op jit(solution)/shard_map/ppermute | solution.py:135
  24.1 58.4 %copy-start.1 = (bf16[1024,512]{1,0:T(8,128)(2,1)S(1)}, bf16[1024,512]{1,0:T(8,128)(2,1)}, u32[]{:S(2)}) copy-start(bf16[1024,512]{1,0:T(8,128)(2,1)} %refs_7_) | copy-start | bytes 3145732
  24.9 22.6 %collective-permute-start.4 = (bf16[1024,512]{1,0:T(8,128)(2,1)S(1)}, bf16[1024,512]{1,0:T(8,128)(2,1)S(1)}, u32[]{:S(2)}, u32[]{:S(2)}) collective-permute-start(bf16[1024,512]{1,0:T(8,128)(2,1)S(1)} %collective-permute-done.refs_8_), channel_id=1, source_target_pairs={{0,12},{1,5},{2,6},{3,15},{4,0},{5,9},{6,10},{7,3},{8,4},{9,13},{1... | collective-permute-start | bytes 3145736 | tf_op jit(solution)/shard_map/ppermute | solution.py:128
  24.9 14.3 %collective-permute-start.5 = (bf16[512,512]{1,0:T(8,128)(2,1)S(1)}, bf16[512,512]{1,0:T(8,128)(2,1)S(1)}, u32[]{:S(2)}, u32[]{:S(2)}) collective-permute-start(bf16[512,512]{1,0:T(8,128)(2,1)S(1)} %get-tuple-element.55), channel_id=1, source_target_pairs={{0,17},{17,0},{1,16},{16,1},{2,19},{19,2},{3,18},{18,3},{4,21},{21... | collective-permute-start | bytes 1572872 | tf_op jit(solution)/shard_map/ppermute | solution.py:135
  28.3 16.2 %collective-permute-start.2 = (bf16[512,512]{1,0:T(8,128)(2,1)S(1)}, bf16[512,512]{1,0:T(8,128)(2,1)S(1)}, u32[]{:S(2)}, u32[]{:S(2)}) collective-permute-start(bf16[512,512]{1,0:T(8,128)(2,1)S(1)} %shard_map.29.refs_0_), channel_id=1, source_target_pairs={{0,224},{32,0},{64,32},{96,64},{128,96},{160,128},{192,160},{224,1... | collective-permute-start | bytes 1572872 | tf_op jit(solution)/shard_map/ppermute | solution.py:136
  33.9 13.7 %collective-permute-start.3 = (bf16[512,512]{1,0:T(8,128)(2,1)S(1)}, bf16[512,512]{1,0:T(8,128)(2,1)S(1)}, u32[]{:S(2)}, u32[]{:S(2)}) collective-permute-start(bf16[512,512]{1,0:T(8,128)(2,1)S(1)} %shard_map.29.refs_0_), channel_id=1, source_target_pairs={{0,32},{32,64},{64,96},{96,128},{128,160},{160,192},{192,224},{224... | collective-permute-start | bytes 1572872 | tf_op jit(solution)/shard_map/ppermute | solution.py:137
  33.9 23.7 %collective-permute-start.9 = (bf16[1024,512]{1,0:T(8,128)(2,1)S(1)}, bf16[1024,512]{1,0:T(8,128)(2,1)S(1)}, u32[]{:S(2)}, u32[]{:S(2)}) collective-permute-start(bf16[1024,512]{1,0:T(8,128)(2,1)S(1)} %collective-permute-done.refs_8_), channel_id=1, source_target_pairs={{0,1},{1,0},{16,17},{17,16},{2,3},{3,2},{18,19},{19,18},{4,5},{5,4... | collective-permute-start | bytes 3145736 | tf_op jit(solution)/shard_map/ppermute | solution.py:134
  47.6 17.9 %collective-permute-start.8 = (bf16[1024,512]{1,0:T(8,128)(2,1)S(1)}, bf16[1024,512]{1,0:T(8,128)(2,1)S(1)}, u32[]{:S(2)}, u32[]{:S(2)}) collective-permute-start(bf16[1024,512]{1,0:T(8,128)(2,1)S(1)} %constant_dynamic-update-slice_fusion.refs_11_), channel_id=1, source_target_pairs={{0,12},{1,5},{2,6},{3,15},{4,0},{5,9},{6,10},{7,3},{8,4},{9,13},{1... | collective-permute-start | bytes 3145736 | tf_op jit(solution)/shard_map/ppermute | solution.py:128
  50.3 13.7 %collective-permute-start.6 = (bf16[512,512]{1,0:T(8,128)(2,1)S(1)}, bf16[512,512]{1,0:T(8,128)(2,1)S(1)}, u32[]{:S(2)}, u32[]{:S(2)}) collective-permute-start(bf16[512,512]{1,0:T(8,128)(2,1)S(1)} %collective-permute-done.2.refs_1_), channel_id=1, source_target_pairs={{0,224},{32,0},{64,32},{96,64},{128,96},{160,128},{192,160},{224,1... | collective-permute-start | bytes 1572872 | tf_op jit(solution)/shard_map/ppermute | solution.py:136
  50.6 14.9 %collective-permute-start.7 = (bf16[512,512]{1,0:T(8,128)(2,1)S(1)}, bf16[512,512]{1,0:T(8,128)(2,1)S(1)}, u32[]{:S(2)}, u32[]{:S(2)}) collective-permute-start(bf16[512,512]{1,0:T(8,128)(2,1)S(1)} %collective-permute-done.3.refs_6_), channel_id=1, source_target_pairs={{0,32},{32,64},{64,96},{96,128},{128,160},{160,192},{192,224},{224... | collective-permute-start | bytes 1572872 | tf_op jit(solution)/shard_map/ppermute | solution.py:137
  51.8 26.1 %collective-permute-start.13 = (bf16[1024,512]{1,0:T(8,128)(2,1)S(1)}, bf16[1024,512]{1,0:T(8,128)(2,1)S(1)}, u32[]{:S(2)}, u32[]{:S(2)}) collective-permute-start(bf16[1024,512]{1,0:T(8,128)(2,1)S(1)} %collective-permute-done.refs_8_), channel_id=1, source_target_pairs={{0,17},{17,0},{1,16},{16,1},{2,19},{19,2},{3,18},{18,3},{4,21},{21... | collective-permute-start | bytes 3145736 | tf_op jit(solution)/shard_map/ppermute | solution.py:135
  65.5 15.2 %collective-permute-start.12 = (bf16[1024,512]{1,0:T(8,128)(2,1)S(1)}, bf16[1024,512]{1,0:T(8,128)(2,1)S(1)}, u32[]{:S(2)}, u32[]{:S(2)}) collective-permute-start(bf16[1024,512]{1,0:T(8,128)(2,1)S(1)} %collective-permute-done.8.refs_12_), channel_id=1, source_target_pairs={{0,12},{1,5},{2,6},{3,15},{4,0},{5,9},{6,10},{7,3},{8,4},{9,13},{1... | collective-permute-start | bytes 3145736 | tf_op jit(solution)/shard_map/ppermute | solution.py:128
  65.5 13.4 %collective-permute-start.10 = (bf16[512,512]{1,0:T(8,128)(2,1)S(1)}, bf16[512,512]{1,0:T(8,128)(2,1)S(1)}, u32[]{:S(2)}, u32[]{:S(2)}) collective-permute-start(bf16[512,512]{1,0:T(8,128)(2,1)S(1)} %collective-permute-done.6.refs_2_), channel_id=1, source_target_pairs={{0,224},{32,0},{64,32},{96,64},{128,96},{160,128},{192,160},{224,1... | collective-permute-start | bytes 1572872 | tf_op jit(solution)/shard_map/ppermute | solution.py:136
  65.6 14.6 %collective-permute-start.11 = (bf16[512,512]{1,0:T(8,128)(2,1)S(1)}, bf16[512,512]{1,0:T(8,128)(2,1)S(1)}, u32[]{:S(2)}, u32[]{:S(2)}) collective-permute-start(bf16[512,512]{1,0:T(8,128)(2,1)S(1)} %collective-permute-done.7.refs_5_), channel_id=1, source_target_pairs={{0,32},{32,64},{64,96},{96,128},{128,160},{160,192},{192,224},{224... | collective-permute-start | bytes 1572872 | tf_op jit(solution)/shard_map/ppermute | solution.py:137
  80.7 7.6 %collective-permute-start.14 = (bf16[256,512]{1,0:T(8,128)(2,1)S(1)}, bf16[256,512]{1,0:T(8,128)(2,1)S(1)}, u32[]{:S(2)}, u32[]{:S(2)}) collective-permute-start(bf16[256,512]{1,0:T(8,128)(2,1)S(1)} %slice.21), channel_id=1, source_target_pairs={{0,224},{32,0},{64,32},{96,64},{128,96},{160,128},{192,160},{224,1... | collective-permute-start | bytes 786440 | tf_op jit(solution)/shard_map/ppermute | solution.py:136
  81.0 8.5 %collective-permute-start.15 = (bf16[256,512]{1,0:T(8,128)(2,1)S(1)}, bf16[256,512]{1,0:T(8,128)(2,1)S(1)}, u32[]{:S(2)}, u32[]{:S(2)}) collective-permute-start(bf16[256,512]{1,0:T(8,128)(2,1)S(1)} %slice.22), channel_id=1, source_target_pairs={{0,32},{32,64},{64,96},{96,128},{128,160},{160,192},{192,224},{224... | collective-permute-start | bytes 786440 | tf_op jit(solution)/shard_map/ppermute | solution.py:137
  90.6 3.9 %collective-permute-start.16 = (f32[512,512]{1,0:T(8,128)S(1)}, f32[512,512]{1,0:T(8,128)S(1)}, u32[]{:S(2)}, u32[]{:S(2)}) collective-permute-start(f32[512,512]{1,0:T(8,128)S(1)} %shard_map.32), channel_id=1, source_target_pairs={{0,2},{2,0},{1,3},{3,1},{4,6},{6,4},{5,7},{7,5},{8,10},{10,8},{9,1... | collective-permute-start | bytes 3145736 | tf_op jit(solution)/shard_map/ppermute | solution.py:184
  96.0 25.4 %all-to-all-start.1 = ((bf16[256,8,128]{2,1,0:T(8,128)(2,1)}), bf16[256,8,128]{2,1,0:T(8,128)(2,1)S(1)}, u32[]{:S(2)}, u32[]{:S(2)}) async-start(bf16[256,8,128]{2,1,0:T(8,128)(2,1)} %bitcast.12), calls=%async_computation.1 | async-start | bytes 1048576 | tf_op jit(solution)/shard_map/all_to_all | solution.py:190
  101.4 14.8 %collective-permute-start.17 = (bf16[512,512]{1,0:T(8,128)(2,1)S(1)}, bf16[512,512]{1,0:T(8,128)(2,1)S(1)}, u32[]{:S(2)}, u32[]{:S(2)}) collective-permute-start(bf16[512,512]{1,0:T(8,128)(2,1)S(1)} %get-tuple-element.53), channel_id=1, source_target_pairs={{0,0},{1,2},{2,1},{3,3},{4,4},{5,6},{6,5},{7,7},{8,8},{9,10},{10,9... | collective-permute-start | bytes 1572872 | tf_op jit(solution)/shard_map/ppermute | solution.py:189

commit v4 on v3

--- a/solution.py
+++ b/solution.py
@@ -1,3 +1,5 @@
+import functools
+
 import jax
 import jax.numpy as jnp
 import numpy as np
@@ -11,10 +13,11 @@
 X_LINE = ("xh", "rep")
 PAIR = [(0, 1), (1, 0), (2, 3), (3, 2)]
 CROSS = [(0, 3), (3, 0), (1, 2), (2, 1)]
+COVER = 2**34
 B = 512
 
 
-def call(body, outs, n_scalar, n_in, flops=0, moved=0, scratch=(), limit=20):
+def call(body, outs, n_scalar, n_in, flops=0, moved=0, scratch=(), limit=20, aliases={}):
     vmem = pl.BlockSpec(memory_space=pltpu.VMEM)
     smem = pl.BlockSpec(memory_space=pltpu.SMEM)
     return pl.pallas_call(
@@ -23,6 +26,7 @@
         in_specs=[smem] * n_scalar + [vmem] * n_in,
         out_specs=[vmem] * len(outs),
         scratch_shapes=list(scratch),
+        input_output_aliases=aliases,
         compiler_params=pltpu.CompilerParams(vmem_limit_bytes=limit << 20),
         cost_estimate=pl.CostEstimate(flops=flops, bytes_accessed=moved, transcendentals=0),
     )
@@ -69,11 +73,20 @@
     return jnp.dot(a, b, preferred_element_type=F32)
 
 
+def hold_first(own_ref, up_ref, down_ref, held_ref):
+    held_ref[0] = own_ref[...]
+    held_ref[1] = up_ref[...]
+    held_ref[4] = jnp.zeros((B, B), BF16)
+    held_ref[7] = down_ref[...]
+
+
+def hold_more(step, up_ref, down_ref, _, held_ref):
+    held_ref[step] = up_ref[...]
+    held_ref[8 - step] = down_ref[...]
+
+
 def product_early(pos_ref, *refs):
-    chunks, pieces, (sum_ref, far_ref, held) = refs[:7], refs[7:15], refs[15:]
-    for j, chunk in zip((0, 1, 2, 3, 5, 6, 7), chunks):
-        held[j] = chunk[...]
-    held[4] = jnp.zeros((B, B), BF16)
+    held, pieces, (sum_ref, far_ref) = refs[0], refs[1:9], refs[9:]
     for rows in (slice(0, B), slice(B, 2 * B)):
         total = None
         for p in range(8):
@@ -155,28 +168,32 @@
     w1, w7 = above(w0), below(w0)
     y2, p1, c1_bottom = along_y(y1), pair(y1), cross(own[B:])
 
-    w1, w7, y2, c1_bottom, y1 = lax.optimization_barrier((w1, w7, y2, c1_bottom, y1))
+    stack = call(hold_first, [shape((8, B, B), BF16)], 0, 3, flops=COVER)(w0, w1, w7)[0]
+    y2, c1_bottom, y1, _ = lax.optimization_barrier((y2, c1_bottom, y1, w1))
     c1 = jnp.concatenate([c1_top, c1_bottom])
     w2, w6 = above(w1), below(w7)
     y3, c2 = along_y(c1), cross(y1)
 
-    w2, w6, y3, p1 = lax.optimization_barrier((w2, w6, y3, p1))
+    more = lambda step, cover, *chunks: call(
+        functools.partial(hold_more, step), [shape((8, B, B), BF16)], 0, 3, flops=cover, aliases={2: 0}
+    )(*chunks)[0]
+    stack = more(2, COVER, w2, w6, stack)
+    y3, p1, _ = lax.optimization_barrier((y3, p1, w2))
     w3, w5 = above(w2), below(w6)
     y4 = along_y(y3)
 
-    w3, w5, y4, c2 = lax.optimization_barrier((w3, w5, y4, c2))
+    stack = more(3, 0, w3, w5, stack)
     top, bottom = above(w3[: B // 2]), below(w5[B // 2 :])
 
     total, far = call(
         product_early,
         [shape((2 * B, B), F32), shape((2 * B, B), BF16)],
         1,
-        15,
+        9,
         flops=32 * B**3,
         moved=16 << 20,
-        scratch=[pltpu.VMEM((8, B, B), BF16)],
         limit=28,
-    )(position, w0, w1, w2, w3, w5, w6, w7, own, y1, y2, p1, c1, y3, y4, c2)
+    )(position, stack, own, y1, y2, p1, c1, y3, y4, c2)
     late = lambda half: call(product_late, [shape((B, B), F32)], 1, 4, flops=2 * B**3, moved=4 << 20)(
         half, total, far, top, bottom
     )[0]

time: 123 us -> 119 us (0.967)
  waiting for transfers between devices: 60 us -> 45.1 us
  starting transfers between devices: 33.1 us -> 43.1 us
    ppermute x3, waiting for transfers between devices: 15.9 us -> 4.11 us  [local(): cross = lambda v: lax.ppermute(v, X_LINE, CROSS)]
    ppermute x4, starting transfers between devices: 6.13 us -> 16.1 us  [local(): above = lambda v: lax.ppermute(v, 'row', ring(8, -1))]
    ppermute x4, waiting for transfers between devices: 0.55 us -> 10.5 us  [along_y(): return lax.ppermute(v, ('y', 'core', 'rep'), perm)]
    ppermute x4, waiting for transfers between devices: 6.96 us -> 0.01 us  [local(): below = lambda v: lax.ppermute(v, 'row', ring(8, 1))]
    ppermute x4, starting transfers between devices: 4.17 us -> 0.09 us  [local(): below = lambda v: lax.ppermute(v, 'row', ring(8, 1))]
    all_to_all x1, starting transfers between devices: 5.41 us -> 9.07 us  [local(): lax.all_to_all(mirror.reshape(256, 8, 128), AXES, split_axis=0, concat_ax...]
    ppermute x1, waiting for transfers between devices: 5.81 us -> 2.69 us  [local(): pair = lambda v: lax.ppermute(v, X_LINE, PAIR)]
    ppermute x4, waiting for transfers between devices: 13.1 us -> 10.3 us  [local(): above = lambda v: lax.ppermute(v, 'row', ring(8, -1))]
  transfers between devices with their start and end apart: 19 -> 19, of which waited for: 16 -> 11; matrix products, arithmetic and copies ran while one was open for 2% -> 2% of each run, Pallas kernels for 7% -> 7%
where the time goes in v4:
time: 119 us
  waiting for transfers between devices  45.1 us (38%)
  starting transfers between devices  43.1 us (36%)
  blocking collectives  15.3 us (13%)
  Pallas kernels  12.2 us (10%)
  local copies, waits for them, and re-layouts  3.28 us (3%)
    ppermute x4, starting transfers between devices, local(): above = lambda v: lax.ppermute(v, 'row', ring(8, -1))  16.1 us
    all_to_all x1, blocking collectives, local(): lax.all_to_all(packed.reshape(16, 128, 128), ('xh', 'y', 'core'), split_a...  15.3 us
    ppermute x1, waiting for transfers between devices, local(): lax.ppermute(direct, ('core', 'rep'), [(0, 0), (1, 2), (2, 1), (3, 3)])  11.2 us
    ppermute x4, waiting for transfers between devices, along_y(): return lax.ppermute(v, ('y', 'core', 'rep'), perm)  10.5 us
    ppermute x4, waiting for transfers between devices, local(): above = lambda v: lax.ppermute(v, 'row', ring(8, -1))  10.3 us
    all_to_all x1, starting transfers between devices, local(): lax.all_to_all(mirror.reshape(256, 8, 128), AXES, split_axis=0, concat_ax...  9.07 us
    ppermute x3, starting transfers between devices, local(): cross = lambda v: lax.ppermute(v, X_LINE, CROSS)  7.66 us
    all_to_all x1, waiting for transfers between devices, local(): lax.all_to_all(mirror.reshape(256, 8, 128), AXES, split_axis=0, concat_ax...  5.18 us
  transfers between devices with their start and end apart: 19, of which 11 were waited for; matrix products, arithmetic and copies ran while one was open for 2% of the time, Pallas kernels for 7%

profile of v4, /device:TPU:1, one launch (start us, length us, event | category | flops | bytes accessed | tf_op | source)
XLA Modules:
  0.0 119.1 jit_solution(1622323257922636834)
XLA Ops:
  0.0 0.1 pad_add_fusion
  0.1 0.1 stack.44.pos_ref
  0.2 2.1 %collective-permute-start = (bf16[1024,512]{1,0:T(8,128)(2,1)}, bf16[1024,512]{1,0:T(8,128)(2,1)S(1)}, u32[]{:S(2)}, u32[]{:S(2)}) collective-permute-start(bf16[1024,512]{1,0:T(8,128)(2,1)} %refs_1_), channel_id=1, source_target_pairs={{0,12},{1,5},{2,6},{3,15},{4,0},{5,9},{6,10},{7,3},{8,4},{9,13},{1... | collective-permute-start | bytes 3145736 | tf_op jit(solution)/shard_map/ppermute | solution.py:141
  2.3 1.3 %fusion = (bf16[512,512]{1,0:T(8,128)(2,1)S(1)}, bf16[512,512]{1,0:T(8,128)(2,1)S(1)}) fusion(bf16[1024,512]{1,0:T(8,128)(2,1)} %refs_1_), kind=kLoop, calls=%fused_computation.3 | loop fusion | bytes 2097152 | tf_op jit(solution)/shard_map/slice | solution.py:169
  3.6 4.0 %collective-permute-start.1 = (bf16[512,512]{1,0:T(8,128)(2,1)S(1)}, bf16[512,512]{1,0:T(8,128)(2,1)S(1)}, u32[]{:S(2)}, u32[]{:S(2)}) collective-permute-start(bf16[512,512]{1,0:T(8,128)(2,1)S(1)} %get-tuple-element.40), channel_id=1, source_target_pairs={{0,17},{17,0},{1,16},{16,1},{2,19},{19,2},{3,18},{18,3},{4,21},{21... | collective-permute-start | bytes 1572872 | tf_op jit(solution)/shard_map/ppermute | solution.py:148
  7.6 0.0 copy-start
  7.6 1.2 %copy-done = bf16[1024,512]{1,0:T(8,128)(2,1)S(1)} copy-done((bf16[1024,512]{1,0:T(8,128)(2,1)S(1)}, bf16[1024,512]{1,0:T(8,128)(2,1)}, u32[]{:S(2)}) %copy-start) | copy-done | bytes 1048600
  8.8 1.1 shard_map.28
  9.9 15.3 %all_to_all.10.in_ref = bf16[16,128,128]{2,1,0:T(8,128)(2,1)S(1)} all-to-all(bf16[16,128,128]{2,1,0:T(8,128)(2,1)S(1)} %bitcast.17), channel_id=1, replica_groups=mesh['row'=8,'xh'=2,'y'=4,'core'=2,'rep'=2] {'xh','y','core'}, dimensions={0} | all-to-all | bytes 1048576 | tf_op jit(solution)/shard_map/all_to_all | solution.py:163
  25.2 0.5 shard_map.29.own_ref
  25.7 0.0 collective-permute-done.1
  25.7 0.0 collective-permute-done.refs_2_
  25.7 0.1 collective-permute-start.8
  25.8 5.7 %collective-permute-start.2 = (bf16[512,512]{1,0:T(8,128)(2,1)S(1)}, bf16[512,512]{1,0:T(8,128)(2,1)S(1)}, u32[]{:S(2)}, u32[]{:S(2)}) collective-permute-start(bf16[512,512]{1,0:T(8,128)(2,1)S(1)} %shard_map.29.own_ref), channel_id=1, source_target_pairs={{0,224},{32,0},{64,32},{96,64},{128,96},{160,128},{192,160},{224,1... | collective-permute-start | bytes 1572872 | tf_op jit(solution)/shard_map/ppermute | solution.py:149
  31.5 0.0 collective-permute-start.5
  31.5 2.4 %collective-permute-start.9 = (bf16[512,512]{1,0:T(8,128)(2,1)S(1)}, bf16[512,512]{1,0:T(8,128)(2,1)S(1)}, u32[]{:S(2)}, u32[]{:S(2)}) collective-permute-start(bf16[512,512]{1,0:T(8,128)(2,1)S(1)} %get-tuple-element.39), channel_id=1, source_target_pairs={{0,17},{17,0},{1,16},{16,1},{2,19},{19,2},{3,18},{18,3},{4,21},{21... | collective-permute-start | bytes 1572872 | tf_op jit(solution)/shard_map/ppermute | solution.py:148
  33.9 0.6 fusion.1
  34.5 0.0 collective-permute-start.11
  34.5 6.0 %collective-permute-done.2.up_ref = bf16[512,512]{1,0:T(8,128)(2,1)S(1)} collective-permute-done((bf16[512,512]{1,0:T(8,128)(2,1)S(1)}, bf16[512,512]{1,0:T(8,128)(2,1)S(1)}, u32[]{:S(2)}, u32[]{:S(2)}) %collective-permute-start.2) | collective-permute-done | bytes 524320 | tf_op jit(solution)/shard_map/ppermute | solution.py:149
  40.5 3.4 %collective-permute-start.3 = (bf16[512,512]{1,0:T(8,128)(2,1)S(1)}, bf16[512,512]{1,0:T(8,128)(2,1)S(1)}, u32[]{:S(2)}, u32[]{:S(2)}) collective-permute-start(bf16[512,512]{1,0:T(8,128)(2,1)S(1)} %collective-permute-done.2.up_ref), channel_id=1, source_target_pairs={{0,224},{32,0},{64,32},{96,64},{128,96},{160,128},{192,160},{224,1... | collective-permute-start | bytes 1572872 | tf_op jit(solution)/shard_map/ppermute | solution.py:149
  43.9 0.0 collective-permute-done.5.down_ref
  44.0 0.0 collective-permute-start.6
  44.0 0.5 collective-permute-done.9
  44.5 0.0 collective-permute-done.8.refs_3_
  44.5 2.7 %collective-permute-start.10 = (bf16[1024,512]{1,0:T(8,128)(2,1)S(1)}, bf16[1024,512]{1,0:T(8,128)(2,1)S(1)}, u32[]{:S(2)}, u32[]{:S(2)}) collective-permute-start(bf16[1024,512]{1,0:T(8,128)(2,1)S(1)} %constant_dynamic-update-slice_fusion.refs_5_), channel_id=1, source_target_pairs={{0,12},{1,5},{2,6},{3,15},{4,0},{5,9},{6,10},{7,3},{8,4},{9,13},{1... | collective-permute-start | bytes 3145736 | tf_op jit(solution)/shard_map/ppermute | solution.py:141
  47.2 0.1 shard_map.30._
  47.3 1.3 %collective-permute-start.13 = (bf16[1024,512]{1,0:T(8,128)(2,1)S(1)}, bf16[1024,512]{1,0:T(8,128)(2,1)S(1)}, u32[]{:S(2)}, u32[]{:S(2)}) collective-permute-start(bf16[1024,512]{1,0:T(8,128)(2,1)S(1)} %collective-permute-done.refs_2_), channel_id=1, source_target_pairs={{0,17},{17,0},{1,16},{16,1},{2,19},{19,2},{3,18},{18,3},{4,21},{21... | collective-permute-start | bytes 3145736 | tf_op jit(solution)/shard_map/ppermute | solution.py:148
  48.6 3.5 %collective-permute-done.3.up_ref = bf16[512,512]{1,0:T(8,128)(2,1)S(1)} collective-permute-done((bf16[512,512]{1,0:T(8,128)(2,1)S(1)}, bf16[512,512]{1,0:T(8,128)(2,1)S(1)}, u32[]{:S(2)}, u32[]{:S(2)}) %collective-permute-start.3) | collective-permute-done | bytes 524320 | tf_op jit(solution)/shard_map/ppermute | solution.py:149
  52.1 3.4 %collective-permute-start.4 = (bf16[512,512]{1,0:T(8,128)(2,1)S(1)}, bf16[512,512]{1,0:T(8,128)(2,1)S(1)}, u32[]{:S(2)}, u32[]{:S(2)}) collective-permute-start(bf16[512,512]{1,0:T(8,128)(2,1)S(1)} %collective-permute-done.3.up_ref), channel_id=1, source_target_pairs={{0,224},{32,0},{64,32},{96,64},{128,96},{160,128},{192,160},{224,1... | collective-permute-start | bytes 1572872 | tf_op jit(solution)/shard_map/ppermute | solution.py:149
  55.5 0.0 collective-permute-done.6.down_ref
  55.5 0.0 collective-permute-start.7
  55.5 2.7 %collective-permute-done.11.refs_4_ = bf16[1024,512]{1,0:T(8,128)(2,1)S(1)} collective-permute-done((bf16[1024,512]{1,0:T(8,128)(2,1)S(1)}, bf16[1024,512]{1,0:T(8,128)(2,1)S(1)}, u32[]{:S(2)}, u32[]{:S(2)}) %collective-permute-start.11) | collective-permute-done | bytes 1048608 | tf_op jit(solution)/shard_map/ppermute | solution.py:147
  58.2 3.6 %collective-permute-done.10.refs_6_ = bf16[1024,512]{1,0:T(8,128)(2,1)S(1)} collective-permute-done((bf16[1024,512]{1,0:T(8,128)(2,1)S(1)}, bf16[1024,512]{1,0:T(8,128)(2,1)S(1)}, u32[]{:S(2)}, u32[]{:S(2)}) %collective-permute-start.10) | collective-permute-done | bytes 1048608 | tf_op jit(solution)/shard_map/ppermute | solution.py:141
  61.8 0.0 collective-permute-start.12
  61.8 0.1 shard_map.31._
  61.9 0.8 collective-permute-done.4.up_ref
  62.7 3.7 %collective-permute-start.14 = (bf16[256,512]{1,0:T(8,128)(2,1)S(1)}, bf16[256,512]{1,0:T(8,128)(2,1)S(1)}, u32[]{:S(2)}, u32[]{:S(2)}) collective-permute-start(bf16[256,512]{1,0:T(8,128)(2,1)S(1)} %slice.24), channel_id=1, source_target_pairs={{0,224},{32,0},{64,32},{96,64},{128,96},{160,128},{192,160},{224,1... | collective-permute-start | bytes 786440 | tf_op jit(solution)/shard_map/ppermute | solution.py:149
  66.4 0.0 collective-permute-done.7.down_ref
  66.4 0.0 copy-start.1
  66.4 0.1 collective-permute-start.15
  66.5 0.1 shard_map.32.refs_0_
  66.6 3.6 %collective-permute-done.13.refs_8_ = bf16[1024,512]{1,0:T(8,128)(2,1)S(1)} collective-permute-done((bf16[1024,512]{1,0:T(8,128)(2,1)S(1)}, bf16[1024,512]{1,0:T(8,128)(2,1)S(1)}, u32[]{:S(2)}, u32[]{:S(2)}) %collective-permute-start.13) | collective-permute-done | bytes 1048608 | tf_op jit(solution)/shard_map/ppermute | solution.py:148
  70.2 6.8 %collective-permute-done.12.refs_7_ = bf16[1024,512]{1,0:T(8,128)(2,1)S(1)} collective-permute-done((bf16[1024,512]{1,0:T(8,128)(2,1)S(1)}, bf16[1024,512]{1,0:T(8,128)(2,1)S(1)}, u32[]{:S(2)}, u32[]{:S(2)}) %collective-permute-start.12) | collective-permute-done | bytes 1048608 | tf_op jit(solution)/shard_map/ppermute | solution.py:141
  77.0 0.0 copy-done.1
  77.0 5.1 %shard_map.33 = (f32[1024,512]{1,0:T(8,128)S(1)}, bf16[1024,512]{1,0:T(8,128)(2,1)S(1)}) custom-call(s32[8]{0:T(128)S(1)} %stack.44.pos_ref, bf16[8,512,512]{2,1,0:T(8,128)(2,1)S(1)} %shard_map.32.refs_0_, bf16[1024,512]{1,0:T(8,128)(2,1)S(1)} %copy-done.1, bf16[1024,512]{1,0:T(8,128)(2,1)S(1)} %collective-permute-done.refs_2_, ...), custom_call_target="tpu_custom_call" | custom-call | flops 4294967296 | bytes 16777216 | tf_op jit(solution)/shard_map/pallas_call | solution.py:188
  82.1 0.0 collective-permute-done.14.top_ref
  82.1 0.0 collective-permute-done.15.bottom_ref
  82.2 1.1 shard_map.35
  83.2 1.7 %collective-permute-start.16 = (f32[512,512]{1,0:T(8,128)S(1)}, f32[512,512]{1,0:T(8,128)S(1)}, u32[]{:S(2)}, u32[]{:S(2)}) collective-permute-start(f32[512,512]{1,0:T(8,128)S(1)} %shard_map.35), channel_id=1, source_target_pairs={{0,2},{2,0},{1,3},{3,1},{4,6},{6,4},{5,7},{7,5},{8,10},{10,8},{9,1... | collective-permute-start | bytes 3145736 | tf_op jit(solution)/shard_map/ppermute | solution.py:201
  85.0 1.1 shard_map.34.kept_ref
  86.1 1.2 collective-permute-done.16.got_ref
  87.2 1.5 %shard_map.36 = (bf16[512,512]{1,0:T(8,128)(2,1)S(1)}, bf16[8,16,2,8,128]{4,3,2,1,0:T(8,128)(2,1)}) custom-call(f32[512,512]{1,0:T(8,128)S(1)} %shard_map.34.kept_ref, f32[512,512]{1,0:T(8,128)S(1)} %collective-permute-done.16.got_ref), custom_call_target="tpu_custom_call" | custom-call | bytes 3145728 | tf_op jit(solution)/shard_map/pallas_call | solution.py:203
  88.7 9.1 %all-to-all-start.1 = ((bf16[256,8,128]{2,1,0:T(8,128)(2,1)}), bf16[256,8,128]{2,1,0:T(8,128)(2,1)S(1)}, u32[]{:S(2)}, u32[]{:S(2)}) async-start(bf16[256,8,128]{2,1,0:T(8,128)(2,1)} %bitcast.12), calls=%async_computation.1 | async-start | bytes 1048576 | tf_op jit(solution)/shard_map/all_to_all | solution.py:207
  97.8 3.5 %collective-permute-start.17 = (bf16[512,512]{1,0:T(8,128)(2,1)S(1)}, bf16[512,512]{1,0:T(8,128)(2,1)S(1)}, u32[]{:S(2)}, u32[]{:S(2)}) collective-permute-start(bf16[512,512]{1,0:T(8,128)(2,1)S(1)} %get-tuple-element.37), channel_id=1, source_target_pairs={{0,0},{1,2},{2,1},{3,3},{4,4},{5,6},{6,5},{7,7},{8,8},{9,10},{10,9... | collective-permute-start | bytes 1572872 | tf_op jit(solution)/shard_map/ppermute | solution.py:206
  101.4 11.2 %collective-permute-done.17.direct_ref = bf16[512,512]{1,0:T(8,128)(2,1)S(1)} collective-permute-done((bf16[512,512]{1,0:T(8,128)(2,1)S(1)}, bf16[512,512]{1,0:T(8,128)(2,1)S(1)}, u32[]{:S(2)}, u32[]{:S(2)}) %collective-permute-start.17) | collective-permute-done | bytes 524320 | tf_op jit(solution)/shard_map/ppermute | solution.py:206
  112.5 5.2 %all-to-all-done.1 = bf16[256,8,128]{2,1,0:T(8,128)(2,1)S(1)} async-done(((bf16[256,8,128]{2,1,0:T(8,128)(2,1)}), bf16[256,8,128]{2,1,0:T(8,128)(2,1)S(1)}, u32[]{:S(2)}, u32[]{:S(2)}) %all-to-all-start.1) | async-done | bytes 524320 | tf_op jit(solution)/shard_map/all_to_all | solution.py:207
  117.7 1.4 %shard_map.37 = f32[512,512]{1,0:T(8,128)} custom-call(bf16[512,512]{1,0:T(8,128)(2,1)S(1)} %collective-permute-done.17.direct_ref, bf16[8,8,2,2,8,128]{5,4,3,2,1,0:T(8,128)(2,1)S(1)} %bitcast.18), custom_call_target="tpu_custom_call" | custom-call | bytes 2097152 | tf_op jit(solution)/shard_map/pallas_call | solution.py:208
  (4 shorter events, 0.1 us)
Async XLA Ops:
  0.2 25.6 %collective-permute-start = (bf16[1024,512]{1,0:T(8,128)(2,1)}, bf16[1024,512]{1,0:T(8,128)(2,1)S(1)}, u32[]{:S(2)}, u32[]{:S(2)}) collective-permute-start(bf16[1024,512]{1,0:T(8,128)(2,1)} %refs_1_), channel_id=1, source_target_pairs={{0,12},{1,5},{2,6},{3,15},{4,0},{5,9},{6,10},{7,3},{8,4},{9,13},{1... | collective-permute-start | bytes 3145736 | tf_op jit(solution)/shard_map/ppermute | solution.py:141
  3.6 22.2 %collective-permute-start.1 = (bf16[512,512]{1,0:T(8,128)(2,1)S(1)}, bf16[512,512]{1,0:T(8,128)(2,1)S(1)}, u32[]{:S(2)}, u32[]{:S(2)}) collective-permute-start(bf16[512,512]{1,0:T(8,128)(2,1)S(1)} %get-tuple-element.40), channel_id=1, source_target_pairs={{0,17},{17,0},{1,16},{16,1},{2,19},{19,2},{3,18},{18,3},{4,21},{21... | collective-permute-start | bytes 1572872 | tf_op jit(solution)/shard_map/ppermute | solution.py:148
  7.6 1.2 %copy-start = (bf16[1024,512]{1,0:T(8,128)(2,1)S(1)}, bf16[1024,512]{1,0:T(8,128)(2,1)}, u32[]{:S(2)}) copy-start(bf16[1024,512]{1,0:T(8,128)(2,1)} %w_ref) | copy-start | bytes 3145732
  25.7 18.7 %collective-permute-start.8 = (bf16[1024,512]{1,0:T(8,128)(2,1)S(1)}, bf16[1024,512]{1,0:T(8,128)(2,1)S(1)}, u32[]{:S(2)}, u32[]{:S(2)}) collective-permute-start(bf16[1024,512]{1,0:T(8,128)(2,1)S(1)} %collective-permute-done.refs_2_), channel_id=1, source_target_pairs={{0,12},{1,5},{2,6},{3,15},{4,0},{5,9},{6,10},{7,3},{8,4},{9,13},{1... | collective-permute-start | bytes 3145736 | tf_op jit(solution)/shard_map/ppermute | solution.py:141
  25.8 14.7 %collective-permute-start.2 = (bf16[512,512]{1,0:T(8,128)(2,1)S(1)}, bf16[512,512]{1,0:T(8,128)(2,1)S(1)}, u32[]{:S(2)}, u32[]{:S(2)}) collective-permute-start(bf16[512,512]{1,0:T(8,128)(2,1)S(1)} %shard_map.29.own_ref), channel_id=1, source_target_pairs={{0,224},{32,0},{64,32},{96,64},{128,96},{160,128},{192,160},{224,1... | collective-permute-start | bytes 1572872 | tf_op jit(solution)/shard_map/ppermute | solution.py:149
  31.5 12.5 %collective-permute-start.5 = (bf16[512,512]{1,0:T(8,128)(2,1)S(1)}, bf16[512,512]{1,0:T(8,128)(2,1)S(1)}, u32[]{:S(2)}, u32[]{:S(2)}) collective-permute-start(bf16[512,512]{1,0:T(8,128)(2,1)S(1)} %shard_map.29.own_ref), channel_id=1, source_target_pairs={{0,32},{32,64},{64,96},{96,128},{128,160},{160,192},{192,224},{224... | collective-permute-start | bytes 1572872 | tf_op jit(solution)/shard_map/ppermute | solution.py:150
  31.5 13.0 %collective-permute-start.9 = (bf16[512,512]{1,0:T(8,128)(2,1)S(1)}, bf16[512,512]{1,0:T(8,128)(2,1)S(1)}, u32[]{:S(2)}, u32[]{:S(2)}) collective-permute-start(bf16[512,512]{1,0:T(8,128)(2,1)S(1)} %get-tuple-element.39), channel_id=1, source_target_pairs={{0,17},{17,0},{1,16},{16,1},{2,19},{19,2},{3,18},{18,3},{4,21},{21... | collective-permute-start | bytes 1572872 | tf_op jit(solution)/shard_map/ppermute | solution.py:148
  34.5 23.7 %collective-permute-start.11 = (bf16[1024,512]{1,0:T(8,128)(2,1)S(1)}, bf16[1024,512]{1,0:T(8,128)(2,1)S(1)}, u32[]{:S(2)}, u32[]{:S(2)}) collective-permute-start(bf16[1024,512]{1,0:T(8,128)(2,1)S(1)} %collective-permute-done.refs_2_), channel_id=1, source_target_pairs={{0,1},{1,0},{16,17},{17,16},{2,3},{3,2},{18,19},{19,18},{4,5},{5,4... | collective-permute-start | bytes 3145736 | tf_op jit(solution)/shard_map/ppermute | solution.py:147
  40.5 11.5 %collective-permute-start.3 = (bf16[512,512]{1,0:T(8,128)(2,1)S(1)}, bf16[512,512]{1,0:T(8,128)(2,1)S(1)}, u32[]{:S(2)}, u32[]{:S(2)}) collective-permute-start(bf16[512,512]{1,0:T(8,128)(2,1)S(1)} %collective-permute-done.2.up_ref), channel_id=1, source_target_pairs={{0,224},{32,0},{64,32},{96,64},{128,96},{160,128},{192,160},{224,1... | collective-permute-start | bytes 1572872 | tf_op jit(solution)/shard_map/ppermute | solution.py:149
  44.0 11.5 %collective-permute-start.6 = (bf16[512,512]{1,0:T(8,128)(2,1)S(1)}, bf16[512,512]{1,0:T(8,128)(2,1)S(1)}, u32[]{:S(2)}, u32[]{:S(2)}) collective-permute-start(bf16[512,512]{1,0:T(8,128)(2,1)S(1)} %collective-permute-done.5.down_ref), channel_id=1, source_target_pairs={{0,32},{32,64},{64,96},{96,128},{128,160},{160,192},{192,224},{224... | collective-permute-start | bytes 1572872 | tf_op jit(solution)/shard_map/ppermute | solution.py:150
  44.5 17.3 %collective-permute-start.10 = (bf16[1024,512]{1,0:T(8,128)(2,1)S(1)}, bf16[1024,512]{1,0:T(8,128)(2,1)S(1)}, u32[]{:S(2)}, u32[]{:S(2)}) collective-permute-start(bf16[1024,512]{1,0:T(8,128)(2,1)S(1)} %constant_dynamic-update-slice_fusion.refs_5_), channel_id=1, source_target_pairs={{0,12},{1,5},{2,6},{3,15},{4,0},{5,9},{6,10},{7,3},{8,4},{9,13},{1... | collective-permute-start | bytes 3145736 | tf_op jit(solution)/shard_map/ppermute | solution.py:141
  47.3 22.9 %collective-permute-start.13 = (bf16[1024,512]{1,0:T(8,128)(2,1)S(1)}, bf16[1024,512]{1,0:T(8,128)(2,1)S(1)}, u32[]{:S(2)}, u32[]{:S(2)}) collective-permute-start(bf16[1024,512]{1,0:T(8,128)(2,1)S(1)} %collective-permute-done.refs_2_), channel_id=1, source_target_pairs={{0,17},{17,0},{1,16},{16,1},{2,19},{19,2},{3,18},{18,3},{4,21},{21... | collective-permute-start | bytes 3145736 | tf_op jit(solution)/shard_map/ppermute | solution.py:148
  52.1 10.6 %collective-permute-start.4 = (bf16[512,512]{1,0:T(8,128)(2,1)S(1)}, bf16[512,512]{1,0:T(8,128)(2,1)S(1)}, u32[]{:S(2)}, u32[]{:S(2)}) collective-permute-start(bf16[512,512]{1,0:T(8,128)(2,1)S(1)} %collective-permute-done.3.up_ref), channel_id=1, source_target_pairs={{0,224},{32,0},{64,32},{96,64},{128,96},{160,128},{192,160},{224,1... | collective-permute-start | bytes 1572872 | tf_op jit(solution)/shard_map/ppermute | solution.py:149
  55.5 10.9 %collective-permute-start.7 = (bf16[512,512]{1,0:T(8,128)(2,1)S(1)}, bf16[512,512]{1,0:T(8,128)(2,1)S(1)}, u32[]{:S(2)}, u32[]{:S(2)}) collective-permute-start(bf16[512,512]{1,0:T(8,128)(2,1)S(1)} %collective-permute-done.6.down_ref), channel_id=1, source_target_pairs={{0,32},{32,64},{64,96},{96,128},{128,160},{160,192},{192,224},{224... | collective-permute-start | bytes 1572872 | tf_op jit(solution)/shard_map/ppermute | solution.py:150
  61.8 15.2 %collective-permute-start.12 = (bf16[1024,512]{1,0:T(8,128)(2,1)S(1)}, bf16[1024,512]{1,0:T(8,128)(2,1)S(1)}, u32[]{:S(2)}, u32[]{:S(2)}) collective-permute-start(bf16[1024,512]{1,0:T(8,128)(2,1)S(1)} %collective-permute-done.10.refs_6_), channel_id=1, source_target_pairs={{0,12},{1,5},{2,6},{3,15},{4,0},{5,9},{6,10},{7,3},{8,4},{9,13},{1... | collective-permute-start | bytes 3145736 | tf_op jit(solution)/shard_map/ppermute | solution.py:141
  62.7 19.4 %collective-permute-start.14 = (bf16[256,512]{1,0:T(8,128)(2,1)S(1)}, bf16[256,512]{1,0:T(8,128)(2,1)S(1)}, u32[]{:S(2)}, u32[]{:S(2)}) collective-permute-start(bf16[256,512]{1,0:T(8,128)(2,1)S(1)} %slice.24), channel_id=1, source_target_pairs={{0,224},{32,0},{64,32},{96,64},{128,96},{160,128},{192,160},{224,1... | collective-permute-start | bytes 786440 | tf_op jit(solution)/shard_map/ppermute | solution.py:149
  66.4 10.6 %copy-start.1 = (bf16[1024,512]{1,0:T(8,128)(2,1)S(1)}, bf16[1024,512]{1,0:T(8,128)(2,1)}, u32[]{:S(2)}) copy-start(bf16[1024,512]{1,0:T(8,128)(2,1)} %refs_1_) | copy-start | bytes 3145732
  66.4 15.7 %collective-permute-start.15 = (bf16[256,512]{1,0:T(8,128)(2,1)S(1)}, bf16[256,512]{1,0:T(8,128)(2,1)S(1)}, u32[]{:S(2)}, u32[]{:S(2)}) collective-permute-start(bf16[256,512]{1,0:T(8,128)(2,1)S(1)} %slice.25), channel_id=1, source_target_pairs={{0,32},{32,64},{64,96},{96,128},{128,160},{160,192},{192,224},{224... | collective-permute-start | bytes 786440 | tf_op jit(solution)/shard_map/ppermute | solution.py:150
  83.2 4.0 %collective-permute-start.16 = (f32[512,512]{1,0:T(8,128)S(1)}, f32[512,512]{1,0:T(8,128)S(1)}, u32[]{:S(2)}, u32[]{:S(2)}) collective-permute-start(f32[512,512]{1,0:T(8,128)S(1)} %shard_map.35), channel_id=1, source_target_pairs={{0,2},{2,0},{1,3},{3,1},{4,6},{6,4},{5,7},{7,5},{8,10},{10,8},{9,1... | collective-permute-start | bytes 3145736 | tf_op jit(solution)/shard_map/ppermute | solution.py:201
  88.7 29.0 %all-to-all-start.1 = ((bf16[256,8,128]{2,1,0:T(8,128)(2,1)}), bf16[256,8,128]{2,1,0:T(8,128)(2,1)S(1)}, u32[]{:S(2)}, u32[]{:S(2)}) async-start(bf16[256,8,128]{2,1,0:T(8,128)(2,1)} %bitcast.12), calls=%async_computation.1 | async-start | bytes 1048576 | tf_op jit(solution)/shard_map/all_to_all | solution.py:207
  97.8 14.7 %collective-permute-start.17 = (bf16[512,512]{1,0:T(8,128)(2,1)S(1)}, bf16[512,512]{1,0:T(8,128)(2,1)S(1)}, u32[]{:S(2)}, u32[]{:S(2)}) collective-permute-start(bf16[512,512]{1,0:T(8,128)(2,1)S(1)} %get-tuple-element.37), channel_id=1, source_target_pairs={{0,0},{1,2},{2,1},{3,3},{4,4},{5,6},{6,5},{7,7},{8,8},{9,10},{10,9... | collective-permute-start | bytes 1572872 | tf_op jit(solution)/shard_map/ppermute | solution.py:206

commit v5 on v4

--- a/solution.py
+++ b/solution.py
@@ -106,14 +106,18 @@
     out_ref[...] = sum_ref[rows, :] + dot(block[:, : B // 2], top_ref[...]) + dot(block[:, B // 2 :], bottom_ref[...])
 
 
-def spread(kept_ref, got_ref, direct_ref, mirror_ref):
+def mirrored(kept_ref, got_ref, mirror_ref):
     cycle = (kept_ref[...] + got_ref[...]).astype(BF16).astype(F32)
-    direct_ref[...] = cycle.T.astype(BF16)
     split = cycle.reshape(16, 4, 8, B)
     for g in range(4):
         parts = [split[:, hi, :, g * 128 : (g + 1) * 128].reshape(128, 128) for hi in range(4)]
         for j, t in enumerate(turn(parts)):
             mirror_ref[2 * g + j // 2, :, j % 2] = t.reshape(16, 8, 128).astype(BF16)
+
+
+def transposed(kept_ref, got_ref, _, direct_ref):
+    cycle = (kept_ref[...] + got_ref[...]).astype(BF16).astype(F32)
+    direct_ref[...] = cycle.T.astype(BF16)
 
 
 def finish(direct_ref, mirror_ref, out_ref):
@@ -200,9 +204,15 @@
     sent = late(halves[1:])
     got = lax.ppermute(sent, "core", [(0, 1), (1, 0)])
     kept = late(halves[:1])
-    direct, mirror = call(
-        spread, [shape((B, B), BF16), shape((8, 16, 2, 8, 128), BF16)], 0, 2, moved=3 << 20
-    )(kept, got)
+    mirror = call(mirrored, [shape((8, 16, 2, 8, 128), BF16)], 0, 2, moved=3 << 20)(kept, got)[0]
+    direct = pl.pallas_call(
+        transposed,
+        out_shape=shape((B, B), BF16),
+        in_specs=[pl.BlockSpec(memory_space=pltpu.VMEM)] * 2 + [pl.BlockSpec(memory_space=pl.ANY)],
+        out_specs=pl.BlockSpec(memory_space=pltpu.VMEM),
+        compiler_params=pltpu.CompilerParams(vmem_limit_bytes=20 << 20),
+        cost_estimate=pl.CostEstimate(flops=0, bytes_accessed=3 << 20, transcendentals=0),
+    )(kept, got, mirror)
     direct = lax.ppermute(direct, ("core", "rep"), [(0, 0), (1, 2), (2, 1), (3, 3)])
     mirror = lax.all_to_all(mirror.reshape(256, 8, 128), AXES, split_axis=0, concat_axis=0, tiled=True)
     out = call(finish, [shape((B, B), F32)], 0, 2, moved=2 << 20)(direct, mirror.reshape(8, 8, 2, 2, 8, 128))[0]

time: 119 us -> 119 us (level)
  no operation moved by 1% of the time
where the time goes in v5:
time: 119 us
  waiting for transfers between devices  44.9 us (38%)
  starting transfers between devices  43.1 us (36%)
  blocking collectives  15.3 us (13%)
  Pallas kernels  12.2 us (10%)
  local copies, waits for them, and re-layouts  3.27 us (3%)
    ppermute x4, starting transfers between devices, local(): above = lambda v: lax.ppermute(v, 'row', ring(8, -1))  16.1 us
    all_to_all x1, blocking collectives, local(): lax.all_to_all(packed.reshape(16, 128, 128), ('xh', 'y', 'core'), split_a...  15.3 us
    ppermute x1, waiting for transfers between devices, local(): lax.ppermute(direct, ('core', 'rep'), [(0, 0), (1, 2), (2, 1), (3, 3)])  11 us
    ppermute x4, waiting for transfers between devices, along_y(): return lax.ppermute(v, ('y', 'core', 'rep'), perm)  10.5 us
    ppermute x4, waiting for transfers between devices, local(): above = lambda v: lax.ppermute(v, 'row', ring(8, -1))  10.3 us
    all_to_all x1, starting transfers between devices, local(): lax.all_to_all(mirror.reshape(256, 8, 128), AXES, split_axis=0, concat_ax...  9.07 us
    ppermute x3, starting transfers between devices, local(): cross = lambda v: lax.ppermute(v, X_LINE, CROSS)  7.66 us
    pallas_call x1, Pallas kernels, local(): call(product_early, [shape((2 * B, B), F32), shape((2 * B, B), BF16)], 1,...  5.14 us
  transfers between devices with their start and end apart: 19, of which 11 were waited for; matrix products, arithmetic and copies ran while one was open for 2% of the time, Pallas kernels for 7%

profile of v5, /device:TPU:1, one launch (start us, length us, event | category | flops | bytes accessed | tf_op | source)
XLA Modules:
  0.0 119.1 jit_solution(13390174448641467756)
XLA Ops:
  0.0 0.1 pad_add_fusion
  0.1 0.1 stack.44.pos_ref
  0.2 2.1 %collective-permute-start = (bf16[1024,512]{1,0:T(8,128)(2,1)}, bf16[1024,512]{1,0:T(8,128)(2,1)S(1)}, u32[]{:S(2)}, u32[]{:S(2)}) collective-permute-start(bf16[1024,512]{1,0:T(8,128)(2,1)} %refs_1_), channel_id=1, source_target_pairs={{0,12},{1,5},{2,6},{3,15},{4,0},{5,9},{6,10},{7,3},{8,4},{9,13},{1... | collective-permute-start | bytes 3145736 | tf_op jit(solution)/shard_map/ppermute | solution.py:145
  2.3 1.3 %fusion = (bf16[512,512]{1,0:T(8,128)(2,1)S(1)}, bf16[512,512]{1,0:T(8,128)(2,1)S(1)}) fusion(bf16[1024,512]{1,0:T(8,128)(2,1)} %refs_1_), kind=kLoop, calls=%fused_computation.3 | loop fusion | bytes 2097152 | tf_op jit(solution)/shard_map/slice | solution.py:173
  3.6 4.0 %collective-permute-start.1 = (bf16[512,512]{1,0:T(8,128)(2,1)S(1)}, bf16[512,512]{1,0:T(8,128)(2,1)S(1)}, u32[]{:S(2)}, u32[]{:S(2)}) collective-permute-start(bf16[512,512]{1,0:T(8,128)(2,1)S(1)} %get-tuple-element.36), channel_id=1, source_target_pairs={{0,17},{17,0},{1,16},{16,1},{2,19},{19,2},{3,18},{18,3},{4,21},{21... | collective-permute-start | bytes 1572872 | tf_op jit(solution)/shard_map/ppermute | solution.py:152
  7.6 0.0 copy-start
  7.6 1.2 %copy-done = bf16[1024,512]{1,0:T(8,128)(2,1)S(1)} copy-done((bf16[1024,512]{1,0:T(8,128)(2,1)S(1)}, bf16[1024,512]{1,0:T(8,128)(2,1)}, u32[]{:S(2)}) %copy-start) | copy-done | bytes 1048600
  8.8 1.1 shard_map.28
  9.9 15.3 %all_to_all.10.in_ref = bf16[16,128,128]{2,1,0:T(8,128)(2,1)S(1)} all-to-all(bf16[16,128,128]{2,1,0:T(8,128)(2,1)S(1)} %bitcast.17), channel_id=1, replica_groups=mesh['row'=8,'xh'=2,'y'=4,'core'=2,'rep'=2] {'xh','y','core'}, dimensions={0} | all-to-all | bytes 1048576 | tf_op jit(solution)/shard_map/all_to_all | solution.py:167
  25.2 0.5 shard_map.29.own_ref
  25.7 0.0 collective-permute-done.1
  25.7 0.0 collective-permute-done.refs_2_
  25.7 0.1 collective-permute-start.8
  25.8 5.7 %collective-permute-start.2 = (bf16[512,512]{1,0:T(8,128)(2,1)S(1)}, bf16[512,512]{1,0:T(8,128)(2,1)S(1)}, u32[]{:S(2)}, u32[]{:S(2)}) collective-permute-start(bf16[512,512]{1,0:T(8,128)(2,1)S(1)} %shard_map.29.own_ref), channel_id=1, source_target_pairs={{0,224},{32,0},{64,32},{96,64},{128,96},{160,128},{192,160},{224,1... | collective-permute-start | bytes 1572872 | tf_op jit(solution)/shard_map/ppermute | solution.py:153
  31.5 0.0 collective-permute-start.5
  31.5 2.4 %collective-permute-start.9 = (bf16[512,512]{1,0:T(8,128)(2,1)S(1)}, bf16[512,512]{1,0:T(8,128)(2,1)S(1)}, u32[]{:S(2)}, u32[]{:S(2)}) collective-permute-start(bf16[512,512]{1,0:T(8,128)(2,1)S(1)} %get-tuple-element.35), channel_id=1, source_target_pairs={{0,17},{17,0},{1,16},{16,1},{2,19},{19,2},{3,18},{18,3},{4,21},{21... | collective-permute-start | bytes 1572872 | tf_op jit(solution)/shard_map/ppermute | solution.py:152
  33.9 0.6 fusion.1
  34.5 0.0 collective-permute-start.11
  34.5 6.0 %collective-permute-done.2.up_ref = bf16[512,512]{1,0:T(8,128)(2,1)S(1)} collective-permute-done((bf16[512,512]{1,0:T(8,128)(2,1)S(1)}, bf16[512,512]{1,0:T(8,128)(2,1)S(1)}, u32[]{:S(2)}, u32[]{:S(2)}) %collective-permute-start.2) | collective-permute-done | bytes 524320 | tf_op jit(solution)/shard_map/ppermute | solution.py:153
  40.5 3.4 %collective-permute-start.3 = (bf16[512,512]{1,0:T(8,128)(2,1)S(1)}, bf16[512,512]{1,0:T(8,128)(2,1)S(1)}, u32[]{:S(2)}, u32[]{:S(2)}) collective-permute-start(bf16[512,512]{1,0:T(8,128)(2,1)S(1)} %collective-permute-done.2.up_ref), channel_id=1, source_target_pairs={{0,224},{32,0},{64,32},{96,64},{128,96},{160,128},{192,160},{224,1... | collective-permute-start | bytes 1572872 | tf_op jit(solution)/shard_map/ppermute | solution.py:153
  43.9 0.0 collective-permute-done.5.down_ref
  44.0 0.0 collective-permute-start.6
  44.0 0.5 collective-permute-done.9
  44.5 0.0 collective-permute-done.8.refs_3_
  44.5 2.7 %collective-permute-start.10 = (bf16[1024,512]{1,0:T(8,128)(2,1)S(1)}, bf16[1024,512]{1,0:T(8,128)(2,1)S(1)}, u32[]{:S(2)}, u32[]{:S(2)}) collective-permute-start(bf16[1024,512]{1,0:T(8,128)(2,1)S(1)} %constant_dynamic-update-slice_fusion.refs_5_), channel_id=1, source_target_pairs={{0,12},{1,5},{2,6},{3,15},{4,0},{5,9},{6,10},{7,3},{8,4},{9,13},{1... | collective-permute-start | bytes 3145736 | tf_op jit(solution)/shard_map/ppermute | solution.py:145
  47.2 0.1 shard_map.30._
  47.3 1.3 %collective-permute-start.13 = (bf16[1024,512]{1,0:T(8,128)(2,1)S(1)}, bf16[1024,512]{1,0:T(8,128)(2,1)S(1)}, u32[]{:S(2)}, u32[]{:S(2)}) collective-permute-start(bf16[1024,512]{1,0:T(8,128)(2,1)S(1)} %collective-permute-done.refs_2_), channel_id=1, source_target_pairs={{0,17},{17,0},{1,16},{16,1},{2,19},{19,2},{3,18},{18,3},{4,21},{21... | collective-permute-start | bytes 3145736 | tf_op jit(solution)/shard_map/ppermute | solution.py:152
  48.6 3.5 %collective-permute-done.3.up_ref = bf16[512,512]{1,0:T(8,128)(2,1)S(1)} collective-permute-done((bf16[512,512]{1,0:T(8,128)(2,1)S(1)}, bf16[512,512]{1,0:T(8,128)(2,1)S(1)}, u32[]{:S(2)}, u32[]{:S(2)}) %collective-permute-start.3) | collective-permute-done | bytes 524320 | tf_op jit(solution)/shard_map/ppermute | solution.py:153
  52.1 3.4 %collective-permute-start.4 = (bf16[512,512]{1,0:T(8,128)(2,1)S(1)}, bf16[512,512]{1,0:T(8,128)(2,1)S(1)}, u32[]{:S(2)}, u32[]{:S(2)}) collective-permute-start(bf16[512,512]{1,0:T(8,128)(2,1)S(1)} %collective-permute-done.3.up_ref), channel_id=1, source_target_pairs={{0,224},{32,0},{64,32},{96,64},{128,96},{160,128},{192,160},{224,1... | collective-permute-start | bytes 1572872 | tf_op jit(solution)/shard_map/ppermute | solution.py:153
  55.5 0.0 collective-permute-done.6.down_ref
  55.5 0.0 collective-permute-start.7
  55.5 2.7 %collective-permute-done.11.refs_4_ = bf16[1024,512]{1,0:T(8,128)(2,1)S(1)} collective-permute-done((bf16[1024,512]{1,0:T(8,128)(2,1)S(1)}, bf16[1024,512]{1,0:T(8,128)(2,1)S(1)}, u32[]{:S(2)}, u32[]{:S(2)}) %collective-permute-start.11) | collective-permute-done | bytes 1048608 | tf_op jit(solution)/shard_map/ppermute | solution.py:151
  58.2 3.7 %collective-permute-done.10.refs_6_ = bf16[1024,512]{1,0:T(8,128)(2,1)S(1)} collective-permute-done((bf16[1024,512]{1,0:T(8,128)(2,1)S(1)}, bf16[1024,512]{1,0:T(8,128)(2,1)S(1)}, u32[]{:S(2)}, u32[]{:S(2)}) %collective-permute-start.10) | collective-permute-done | bytes 1048608 | tf_op jit(solution)/shard_map/ppermute | solution.py:145
  61.8 0.0 collective-permute-start.12
  61.8 0.1 shard_map.31._
  61.9 0.8 collective-permute-done.4.up_ref
  62.7 3.7 %collective-permute-start.14 = (bf16[256,512]{1,0:T(8,128)(2,1)S(1)}, bf16[256,512]{1,0:T(8,128)(2,1)S(1)}, u32[]{:S(2)}, u32[]{:S(2)}) collective-permute-start(bf16[256,512]{1,0:T(8,128)(2,1)S(1)} %slice.24), channel_id=1, source_target_pairs={{0,224},{32,0},{64,32},{96,64},{128,96},{160,128},{192,160},{224,1... | collective-permute-start | bytes 786440 | tf_op jit(solution)/shard_map/ppermute | solution.py:153
  66.4 0.0 collective-permute-done.7.down_ref
  66.4 0.0 copy-start.1
  66.4 0.1 collective-permute-start.15
  66.5 0.1 shard_map.32.refs_0_
  66.6 3.6 %collective-permute-done.13.refs_8_ = bf16[1024,512]{1,0:T(8,128)(2,1)S(1)} collective-permute-done((bf16[1024,512]{1,0:T(8,128)(2,1)S(1)}, bf16[1024,512]{1,0:T(8,128)(2,1)S(1)}, u32[]{:S(2)}, u32[]{:S(2)}) %collective-permute-start.13) | collective-permute-done | bytes 1048608 | tf_op jit(solution)/shard_map/ppermute | solution.py:152
  70.2 6.8 %collective-permute-done.12.refs_7_ = bf16[1024,512]{1,0:T(8,128)(2,1)S(1)} collective-permute-done((bf16[1024,512]{1,0:T(8,128)(2,1)S(1)}, bf16[1024,512]{1,0:T(8,128)(2,1)S(1)}, u32[]{:S(2)}, u32[]{:S(2)}) %collective-permute-start.12) | collective-permute-done | bytes 1048608 | tf_op jit(solution)/shard_map/ppermute | solution.py:145
  77.0 0.0 copy-done.1
  77.0 5.1 %shard_map.33 = (f32[1024,512]{1,0:T(8,128)S(1)}, bf16[1024,512]{1,0:T(8,128)(2,1)S(1)}) custom-call(s32[8]{0:T(128)S(1)} %stack.44.pos_ref, bf16[8,512,512]{2,1,0:T(8,128)(2,1)S(1)} %shard_map.32.refs_0_, bf16[1024,512]{1,0:T(8,128)(2,1)S(1)} %copy-done.1, bf16[1024,512]{1,0:T(8,128)(2,1)S(1)} %collective-permute-done.refs_2_, ...), custom_call_target="tpu_custom_call" | custom-call | flops 4294967296 | bytes 16777216 | tf_op jit(solution)/shard_map/pallas_call | solution.py:192
  82.1 0.0 collective-permute-done.14.top_ref
  82.1 0.0 collective-permute-done.15.bottom_ref
  82.2 1.1 shard_map.35
  83.2 1.7 %collective-permute-start.16 = (f32[512,512]{1,0:T(8,128)S(1)}, f32[512,512]{1,0:T(8,128)S(1)}, u32[]{:S(2)}, u32[]{:S(2)}) collective-permute-start(f32[512,512]{1,0:T(8,128)S(1)} %shard_map.35), channel_id=1, source_target_pairs={{0,2},{2,0},{1,3},{3,1},{4,6},{6,4},{5,7},{7,5},{8,10},{10,8},{9,1... | collective-permute-start | bytes 3145736 | tf_op jit(solution)/shard_map/ppermute | solution.py:205
  85.0 1.1 shard_map.34.kept_ref
  86.0 1.2 %collective-permute-done.16.got_ref = f32[512,512]{1,0:T(8,128)S(1)} collective-permute-done((f32[512,512]{1,0:T(8,128)S(1)}, f32[512,512]{1,0:T(8,128)S(1)}, u32[]{:S(2)}, u32[]{:S(2)}) %collective-permute-start.16) | collective-permute-done | bytes 1048608 | tf_op jit(solution)/shard_map/ppermute | solution.py:205
  87.2 1.4 %shard_map.36._ = bf16[8,16,2,8,128]{4,3,2,1,0:T(8,128)(2,1)} custom-call(f32[512,512]{1,0:T(8,128)S(1)} %shard_map.34.kept_ref, f32[512,512]{1,0:T(8,128)S(1)} %collective-permute-done.16.got_ref), custom_call_target="tpu_custom_call" | custom-call | bytes 3145728 | tf_op jit(solution)/shard_map/pallas_call | solution.py:207
  88.7 9.1 %all-to-all-start.1 = ((bf16[256,8,128]{2,1,0:T(8,128)(2,1)}), bf16[256,8,128]{2,1,0:T(8,128)(2,1)S(1)}, u32[]{:S(2)}, u32[]{:S(2)}) async-start(bf16[256,8,128]{2,1,0:T(8,128)(2,1)} %bitcast.12), calls=%async_computation.1 | async-start | bytes 1048576 | tf_op jit(solution)/shard_map/all_to_all | solution.py:217
  97.7 0.2 shard_map.37
  97.9 3.5 %collective-permute-start.17 = (bf16[512,512]{1,0:T(8,128)(2,1)S(1)}, bf16[512,512]{1,0:T(8,128)(2,1)S(1)}, u32[]{:S(2)}, u32[]{:S(2)}) collective-permute-start(bf16[512,512]{1,0:T(8,128)(2,1)S(1)} %shard_map.37), channel_id=1, source_target_pairs={{0,0},{1,2},{2,1},{3,3},{4,4},{5,6},{6,5},{7,7},{8,8},{9,10},{10,9... | collective-permute-start | bytes 1572872 | tf_op jit(solution)/shard_map/ppermute | solution.py:216
  101.5 11.0 %collective-permute-done.17.direct_ref = bf16[512,512]{1,0:T(8,128)(2,1)S(1)} collective-permute-done((bf16[512,512]{1,0:T(8,128)(2,1)S(1)}, bf16[512,512]{1,0:T(8,128)(2,1)S(1)}, u32[]{:S(2)}, u32[]{:S(2)}) %collective-permute-start.17) | collective-permute-done | bytes 524320 | tf_op jit(solution)/shard_map/ppermute | solution.py:216
  112.5 5.1 %all-to-all-done.1 = bf16[256,8,128]{2,1,0:T(8,128)(2,1)S(1)} async-done(((bf16[256,8,128]{2,1,0:T(8,128)(2,1)}), bf16[256,8,128]{2,1,0:T(8,128)(2,1)S(1)}, u32[]{:S(2)}, u32[]{:S(2)}) %all-to-all-start.1) | async-done | bytes 524320 | tf_op jit(solution)/shard_map/all_to_all | solution.py:217
  117.6 1.4 %shard_map.38 = f32[512,512]{1,0:T(8,128)} custom-call(bf16[512,512]{1,0:T(8,128)(2,1)S(1)} %collective-permute-done.17.direct_ref, bf16[8,8,2,2,8,128]{5,4,3,2,1,0:T(8,128)(2,1)S(1)} %bitcast.18), custom_call_target="tpu_custom_call" | custom-call | bytes 2097152 | tf_op jit(solution)/shard_map/pallas_call | solution.py:218
  (4 shorter events, 0.1 us)
Async XLA Ops:
  0.2 25.6 %collective-permute-start = (bf16[1024,512]{1,0:T(8,128)(2,1)}, bf16[1024,512]{1,0:T(8,128)(2,1)S(1)}, u32[]{:S(2)}, u32[]{:S(2)}) collective-permute-start(bf16[1024,512]{1,0:T(8,128)(2,1)} %refs_1_), channel_id=1, source_target_pairs={{0,12},{1,5},{2,6},{3,15},{4,0},{5,9},{6,10},{7,3},{8,4},{9,13},{1... | collective-permute-start | bytes 3145736 | tf_op jit(solution)/shard_map/ppermute | solution.py:145
  3.6 22.2 %collective-permute-start.1 = (bf16[512,512]{1,0:T(8,128)(2,1)S(1)}, bf16[512,512]{1,0:T(8,128)(2,1)S(1)}, u32[]{:S(2)}, u32[]{:S(2)}) collective-permute-start(bf16[512,512]{1,0:T(8,128)(2,1)S(1)} %get-tuple-element.36), channel_id=1, source_target_pairs={{0,17},{17,0},{1,16},{16,1},{2,19},{19,2},{3,18},{18,3},{4,21},{21... | collective-permute-start | bytes 1572872 | tf_op jit(solution)/shard_map/ppermute | solution.py:152
  7.6 1.2 %copy-start = (bf16[1024,512]{1,0:T(8,128)(2,1)S(1)}, bf16[1024,512]{1,0:T(8,128)(2,1)}, u32[]{:S(2)}) copy-start(bf16[1024,512]{1,0:T(8,128)(2,1)} %w_ref) | copy-start | bytes 3145732
  25.7 18.7 %collective-permute-start.8 = (bf16[1024,512]{1,0:T(8,128)(2,1)S(1)}, bf16[1024,512]{1,0:T(8,128)(2,1)S(1)}, u32[]{:S(2)}, u32[]{:S(2)}) collective-permute-start(bf16[1024,512]{1,0:T(8,128)(2,1)S(1)} %collective-permute-done.refs_2_), channel_id=1, source_target_pairs={{0,12},{1,5},{2,6},{3,15},{4,0},{5,9},{6,10},{7,3},{8,4},{9,13},{1... | collective-permute-start | bytes 3145736 | tf_op jit(solution)/shard_map/ppermute | solution.py:145
  25.8 14.7 %collective-permute-start.2 = (bf16[512,512]{1,0:T(8,128)(2,1)S(1)}, bf16[512,512]{1,0:T(8,128)(2,1)S(1)}, u32[]{:S(2)}, u32[]{:S(2)}) collective-permute-start(bf16[512,512]{1,0:T(8,128)(2,1)S(1)} %shard_map.29.own_ref), channel_id=1, source_target_pairs={{0,224},{32,0},{64,32},{96,64},{128,96},{160,128},{192,160},{224,1... | collective-permute-start | bytes 1572872 | tf_op jit(solution)/shard_map/ppermute | solution.py:153
  31.5 12.5 %collective-permute-start.5 = (bf16[512,512]{1,0:T(8,128)(2,1)S(1)}, bf16[512,512]{1,0:T(8,128)(2,1)S(1)}, u32[]{:S(2)}, u32[]{:S(2)}) collective-permute-start(bf16[512,512]{1,0:T(8,128)(2,1)S(1)} %shard_map.29.own_ref), channel_id=1, source_target_pairs={{0,32},{32,64},{64,96},{96,128},{128,160},{160,192},{192,224},{224... | collective-permute-start | bytes 1572872 | tf_op jit(solution)/shard_map/ppermute | solution.py:154
  31.5 13.0 %collective-permute-start.9 = (bf16[512,512]{1,0:T(8,128)(2,1)S(1)}, bf16[512,512]{1,0:T(8,128)(2,1)S(1)}, u32[]{:S(2)}, u32[]{:S(2)}) collective-permute-start(bf16[512,512]{1,0:T(8,128)(2,1)S(1)} %get-tuple-element.35), channel_id=1, source_target_pairs={{0,17},{17,0},{1,16},{16,1},{2,19},{19,2},{3,18},{18,3},{4,21},{21... | collective-permute-start | bytes 1572872 | tf_op jit(solution)/shard_map/ppermute | solution.py:152
  34.5 23.7 %collective-permute-start.11 = (bf16[1024,512]{1,0:T(8,128)(2,1)S(1)}, bf16[1024,512]{1,0:T(8,128)(2,1)S(1)}, u32[]{:S(2)}, u32[]{:S(2)}) collective-permute-start(bf16[1024,512]{1,0:T(8,128)(2,1)S(1)} %collective-permute-done.refs_2_), channel_id=1, source_target_pairs={{0,1},{1,0},{16,17},{17,16},{2,3},{3,2},{18,19},{19,18},{4,5},{5,4... | collective-permute-start | bytes 3145736 | tf_op jit(solution)/shard_map/ppermute | solution.py:151
  40.5 11.5 %collective-permute-start.3 = (bf16[512,512]{1,0:T(8,128)(2,1)S(1)}, bf16[512,512]{1,0:T(8,128)(2,1)S(1)}, u32[]{:S(2)}, u32[]{:S(2)}) collective-permute-start(bf16[512,512]{1,0:T(8,128)(2,1)S(1)} %collective-permute-done.2.up_ref), channel_id=1, source_target_pairs={{0,224},{32,0},{64,32},{96,64},{128,96},{160,128},{192,160},{224,1... | collective-permute-start | bytes 1572872 | tf_op jit(solution)/shard_map/ppermute | solution.py:153
  44.0 11.5 %collective-permute-start.6 = (bf16[512,512]{1,0:T(8,128)(2,1)S(1)}, bf16[512,512]{1,0:T(8,128)(2,1)S(1)}, u32[]{:S(2)}, u32[]{:S(2)}) collective-permute-start(bf16[512,512]{1,0:T(8,128)(2,1)S(1)} %collective-permute-done.5.down_ref), channel_id=1, source_target_pairs={{0,32},{32,64},{64,96},{96,128},{128,160},{160,192},{192,224},{224... | collective-permute-start | bytes 1572872 | tf_op jit(solution)/shard_map/ppermute | solution.py:154
  44.5 17.3 %collective-permute-start.10 = (bf16[1024,512]{1,0:T(8,128)(2,1)S(1)}, bf16[1024,512]{1,0:T(8,128)(2,1)S(1)}, u32[]{:S(2)}, u32[]{:S(2)}) collective-permute-start(bf16[1024,512]{1,0:T(8,128)(2,1)S(1)} %constant_dynamic-update-slice_fusion.refs_5_), channel_id=1, source_target_pairs={{0,12},{1,5},{2,6},{3,15},{4,0},{5,9},{6,10},{7,3},{8,4},{9,13},{1... | collective-permute-start | bytes 3145736 | tf_op jit(solution)/shard_map/ppermute | solution.py:145
  47.3 22.9 %collective-permute-start.13 = (bf16[1024,512]{1,0:T(8,128)(2,1)S(1)}, bf16[1024,512]{1,0:T(8,128)(2,1)S(1)}, u32[]{:S(2)}, u32[]{:S(2)}) collective-permute-start(bf16[1024,512]{1,0:T(8,128)(2,1)S(1)} %collective-permute-done.refs_2_), channel_id=1, source_target_pairs={{0,17},{17,0},{1,16},{16,1},{2,19},{19,2},{3,18},{18,3},{4,21},{21... | collective-permute-start | bytes 3145736 | tf_op jit(solution)/shard_map/ppermute | solution.py:152
  52.1 10.6 %collective-permute-start.4 = (bf16[512,512]{1,0:T(8,128)(2,1)S(1)}, bf16[512,512]{1,0:T(8,128)(2,1)S(1)}, u32[]{:S(2)}, u32[]{:S(2)}) collective-permute-start(bf16[512,512]{1,0:T(8,128)(2,1)S(1)} %collective-permute-done.3.up_ref), channel_id=1, source_target_pairs={{0,224},{32,0},{64,32},{96,64},{128,96},{160,128},{192,160},{224,1... | collective-permute-start | bytes 1572872 | tf_op jit(solution)/shard_map/ppermute | solution.py:153
  55.5 10.9 %collective-permute-start.7 = (bf16[512,512]{1,0:T(8,128)(2,1)S(1)}, bf16[512,512]{1,0:T(8,128)(2,1)S(1)}, u32[]{:S(2)}, u32[]{:S(2)}) collective-permute-start(bf16[512,512]{1,0:T(8,128)(2,1)S(1)} %collective-permute-done.6.down_ref), channel_id=1, source_target_pairs={{0,32},{32,64},{64,96},{96,128},{128,160},{160,192},{192,224},{224... | collective-permute-start | bytes 1572872 | tf_op jit(solution)/shard_map/ppermute | solution.py:154
  61.8 15.2 %collective-permute-start.12 = (bf16[1024,512]{1,0:T(8,128)(2,1)S(1)}, bf16[1024,512]{1,0:T(8,128)(2,1)S(1)}, u32[]{:S(2)}, u32[]{:S(2)}) collective-permute-start(bf16[1024,512]{1,0:T(8,128)(2,1)S(1)} %collective-permute-done.10.refs_6_), channel_id=1, source_target_pairs={{0,12},{1,5},{2,6},{3,15},{4,0},{5,9},{6,10},{7,3},{8,4},{9,13},{1... | collective-permute-start | bytes 3145736 | tf_op jit(solution)/shard_map/ppermute | solution.py:145
  62.7 19.4 %collective-permute-start.14 = (bf16[256,512]{1,0:T(8,128)(2,1)S(1)}, bf16[256,512]{1,0:T(8,128)(2,1)S(1)}, u32[]{:S(2)}, u32[]{:S(2)}) collective-permute-start(bf16[256,512]{1,0:T(8,128)(2,1)S(1)} %slice.24), channel_id=1, source_target_pairs={{0,224},{32,0},{64,32},{96,64},{128,96},{160,128},{192,160},{224,1... | collective-permute-start | bytes 786440 | tf_op jit(solution)/shard_map/ppermute | solution.py:153
  66.4 10.6 %copy-start.1 = (bf16[1024,512]{1,0:T(8,128)(2,1)S(1)}, bf16[1024,512]{1,0:T(8,128)(2,1)}, u32[]{:S(2)}) copy-start(bf16[1024,512]{1,0:T(8,128)(2,1)} %refs_1_) | copy-start | bytes 3145732
  66.4 15.7 %collective-permute-start.15 = (bf16[256,512]{1,0:T(8,128)(2,1)S(1)}, bf16[256,512]{1,0:T(8,128)(2,1)S(1)}, u32[]{:S(2)}, u32[]{:S(2)}) collective-permute-start(bf16[256,512]{1,0:T(8,128)(2,1)S(1)} %slice.25), channel_id=1, source_target_pairs={{0,32},{32,64},{64,96},{96,128},{128,160},{160,192},{192,224},{224... | collective-permute-start | bytes 786440 | tf_op jit(solution)/shard_map/ppermute | solution.py:154
  83.2 4.0 %collective-permute-start.16 = (f32[512,512]{1,0:T(8,128)S(1)}, f32[512,512]{1,0:T(8,128)S(1)}, u32[]{:S(2)}, u32[]{:S(2)}) collective-permute-start(f32[512,512]{1,0:T(8,128)S(1)} %shard_map.35), channel_id=1, source_target_pairs={{0,2},{2,0},{1,3},{3,1},{4,6},{6,4},{5,7},{7,5},{8,10},{10,8},{9,1... | collective-permute-start | bytes 3145736 | tf_op jit(solution)/shard_map/ppermute | solution.py:205
  88.7 29.0 %all-to-all-start.1 = ((bf16[256,8,128]{2,1,0:T(8,128)(2,1)}), bf16[256,8,128]{2,1,0:T(8,128)(2,1)S(1)}, u32[]{:S(2)}, u32[]{:S(2)}) async-start(bf16[256,8,128]{2,1,0:T(8,128)(2,1)} %bitcast.12), calls=%async_computation.1 | async-start | bytes 1048576 | tf_op jit(solution)/shard_map/all_to_all | solution.py:217
  97.9 14.6 %collective-permute-start.17 = (bf16[512,512]{1,0:T(8,128)(2,1)S(1)}, bf16[512,512]{1,0:T(8,128)(2,1)S(1)}, u32[]{:S(2)}, u32[]{:S(2)}) collective-permute-start(bf16[512,512]{1,0:T(8,128)(2,1)S(1)} %shard_map.37), channel_id=1, source_target_pairs={{0,0},{1,2},{2,1},{3,3},{4,4},{5,6},{6,5},{7,7},{8,8},{9,10},{10,9... | collective-permute-start | bytes 1572872 | tf_op jit(solution)/shard_map/ppermute | solution.py:216

commit v6 on v5

--- a/solution.py
+++ b/solution.py
@@ -51,15 +51,14 @@
 
 def w_pack(rep_ref, w_ref, out_ref):
     rep = rep_ref[0]
-    for half in range(2):
-        for g in range(4):
-            parts = []
-            for hi in range(4):
-                v = w_ref[half * B + hi * 128 : half * B + (hi + 1) * 128, g * 128 : (g + 1) * 128].astype(F32)
-                parts.append(jnp.where(rep == 0, v, pltpu.roll(v, 96, 1)))
-            turned = turn(parts)
-            for j in (0, 2):
-                out_ref[g * 2 + j // 2, half] = turned[j].astype(BF16)
+    for g in range(4):
+        parts = []
+        for hi in range(4):
+            v = w_ref[hi * 128 : (hi + 1) * 128, g * 128 : (g + 1) * 128].astype(F32)
+            parts.append(jnp.where(rep == 0, v, pltpu.roll(v, 96, 1)))
+        turned = turn(parts)
+        for j in (0, 2):
+            out_ref[g * 2 + j // 2, 0] = turned[j].astype(BF16)
 
 
 def w_unpack(in_ref, out_ref):
@@ -163,7 +162,15 @@
         (position, halves, rep, intermediate, amplitudes)
     )
 
-    packed = call(w_pack, [shape((8, 2, 128, 128), BF16)], 1, 1, moved=2 << 20)(rep, intermediate)[0]
+    packed = pl.pallas_call(
+        w_pack,
+        out_shape=shape((8, 2, 128, 128), BF16),
+        grid=(2,),
+        in_specs=[pl.BlockSpec(memory_space=pltpu.SMEM), pl.BlockSpec((B, B), lambda i: (i, 0))],
+        out_specs=pl.BlockSpec((8, 1, 128, 128), lambda i: (0, i, 0, 0)),
+        compiler_params=pltpu.CompilerParams(vmem_limit_bytes=20 << 20),
+        cost_estimate=pl.CostEstimate(flops=0, bytes_accessed=2 << 20, transcendentals=0),
+    )(rep, intermediate)
     arrived = lax.all_to_all(packed.reshape(16, 128, 128), ("xh", "y", "core"), split_axis=0, concat_axis=0, tiled=True)
     w0 = call(w_unpack, [shape((B, B), BF16)], 0, 1, moved=1 << 20)(arrived)[0]
 

time: 119 us -> 119 us (level)
  no operation moved by 1% of the time
where the time goes in v6:
time: 119 us
  waiting for transfers between devices  44.9 us (38%)
  starting transfers between devices  43.1 us (36%)
  blocking collectives  15.3 us (13%)
  Pallas kernels  12.3 us (10%)
  local copies, waits for them, and re-layouts  3.27 us (3%)
    ppermute x4, starting transfers between devices, local(): above = lambda v: lax.ppermute(v, 'row', ring(8, -1))  16.1 us
    all_to_all x1, blocking collectives, local(): lax.all_to_all(packed.reshape(16, 128, 128), ('xh', 'y', 'core'), split_a...  15.3 us
    ppermute x1, waiting for transfers between devices, local(): lax.ppermute(direct, ('core', 'rep'), [(0, 0), (1, 2), (2, 1), (3, 3)])  11 us
    ppermute x4, waiting for transfers between devices, local(): above = lambda v: lax.ppermute(v, 'row', ring(8, -1))  10.7 us
    ppermute x4, waiting for transfers between devices, along_y(): return lax.ppermute(v, ('y', 'core', 'rep'), perm)  10.4 us
    all_to_all x1, starting transfers between devices, local(): lax.all_to_all(mirror.reshape(256, 8, 128), AXES, split_axis=0, concat_ax...  9.31 us
    ppermute x3, starting transfers between devices, local(): cross = lambda v: lax.ppermute(v, X_LINE, CROSS)  7.54 us
    pallas_call x1, Pallas kernels, local(): call(product_early, [shape((2 * B, B), F32), shape((2 * B, B), BF16)], 1,...  5.14 us
  transfers between devices with their start and end apart: 19, of which 11 were waited for; matrix products, arithmetic and copies ran while one was open for 2% of the time, Pallas kernels for 7%

profile of v6, /device:TPU:1, one launch (start us, length us, event | category | flops | bytes accessed | tf_op | source)
XLA Modules:
  0.0 119.2 jit_solution(2062670638063530727)
XLA Ops:
  0.0 0.1 pad_add_fusion
  0.1 0.1 stack.44.pos_ref
  0.2 2.1 %collective-permute-start = (bf16[1024,512]{1,0:T(8,128)(2,1)}, bf16[1024,512]{1,0:T(8,128)(2,1)S(1)}, u32[]{:S(2)}, u32[]{:S(2)}) collective-permute-start(bf16[1024,512]{1,0:T(8,128)(2,1)} %refs_1_), channel_id=1, source_target_pairs={{0,12},{1,5},{2,6},{3,15},{4,0},{5,9},{6,10},{7,3},{8,4},{9,13},{1... | collective-permute-start | bytes 3145736 | tf_op jit(solution)/shard_map/ppermute | solution.py:144
  2.3 1.3 %fusion = (bf16[512,512]{1,0:T(8,128)(2,1)S(1)}, bf16[512,512]{1,0:T(8,128)(2,1)S(1)}) fusion(bf16[1024,512]{1,0:T(8,128)(2,1)} %refs_1_), kind=kLoop, calls=%fused_computation.3 | loop fusion | bytes 2097152 | tf_op jit(solution)/shard_map/slice | solution.py:180
  3.6 4.0 %collective-permute-start.1 = (bf16[512,512]{1,0:T(8,128)(2,1)S(1)}, bf16[512,512]{1,0:T(8,128)(2,1)S(1)}, u32[]{:S(2)}, u32[]{:S(2)}) collective-permute-start(bf16[512,512]{1,0:T(8,128)(2,1)S(1)} %get-tuple-element.36), channel_id=1, source_target_pairs={{0,17},{17,0},{1,16},{16,1},{2,19},{19,2},{3,18},{18,3},{4,21},{21... | collective-permute-start | bytes 1572872 | tf_op jit(solution)/shard_map/ppermute | solution.py:151
  7.6 0.0 copy-start
  7.6 1.2 %copy-done = bf16[1024,512]{1,0:T(8,128)(2,1)S(1)} copy-done((bf16[1024,512]{1,0:T(8,128)(2,1)S(1)}, bf16[1024,512]{1,0:T(8,128)(2,1)}, u32[]{:S(2)}) %copy-start) | copy-done | bytes 1048600
  8.8 1.2 %shard_map.28 = bf16[8,2,128,128]{3,2,1,0:T(8,128)(2,1)S(1)} custom-call(s32[1]{0:T(128)} %bitcast.10.rep_ref, bf16[1024,512]{1,0:T(8,128)(2,1)S(1)} %copy-done), custom_call_target="tpu_custom_call" | custom-call | bytes 2097152 | tf_op jit(solution)/shard_map/pallas_call | solution.py:165
  10.0 15.3 %all_to_all.10.in_ref = bf16[16,128,128]{2,1,0:T(8,128)(2,1)S(1)} all-to-all(bf16[16,128,128]{2,1,0:T(8,128)(2,1)S(1)} %bitcast.17), channel_id=1, replica_groups=mesh['row'=8,'xh'=2,'y'=4,'core'=2,'rep'=2] {'xh','y','core'}, dimensions={0} | all-to-all | bytes 1048576 | tf_op jit(solution)/shard_map/all_to_all | solution.py:174
  25.4 0.5 shard_map.29.own_ref
  25.8 0.0 collective-permute-done.1
  25.9 0.0 collective-permute-done.refs_2_
  25.9 0.1 collective-permute-start.8
  26.0 5.7 %collective-permute-start.2 = (bf16[512,512]{1,0:T(8,128)(2,1)S(1)}, bf16[512,512]{1,0:T(8,128)(2,1)S(1)}, u32[]{:S(2)}, u32[]{:S(2)}) collective-permute-start(bf16[512,512]{1,0:T(8,128)(2,1)S(1)} %shard_map.29.own_ref), channel_id=1, source_target_pairs={{0,224},{32,0},{64,32},{96,64},{128,96},{160,128},{192,160},{224,1... | collective-permute-start | bytes 1572872 | tf_op jit(solution)/shard_map/ppermute | solution.py:152
  31.6 0.0 collective-permute-start.5
  31.6 2.3 %collective-permute-start.9 = (bf16[512,512]{1,0:T(8,128)(2,1)S(1)}, bf16[512,512]{1,0:T(8,128)(2,1)S(1)}, u32[]{:S(2)}, u32[]{:S(2)}) collective-permute-start(bf16[512,512]{1,0:T(8,128)(2,1)S(1)} %get-tuple-element.35), channel_id=1, source_target_pairs={{0,17},{17,0},{1,16},{16,1},{2,19},{19,2},{3,18},{18,3},{4,21},{21... | collective-permute-start | bytes 1572872 | tf_op jit(solution)/shard_map/ppermute | solution.py:151
  33.9 0.6 fusion.1
  34.5 0.0 collective-permute-start.11
  34.5 6.2 %collective-permute-done.2.up_ref = bf16[512,512]{1,0:T(8,128)(2,1)S(1)} collective-permute-done((bf16[512,512]{1,0:T(8,128)(2,1)S(1)}, bf16[512,512]{1,0:T(8,128)(2,1)S(1)}, u32[]{:S(2)}, u32[]{:S(2)}) %collective-permute-start.2) | collective-permute-done | bytes 524320 | tf_op jit(solution)/shard_map/ppermute | solution.py:152
  40.7 3.4 %collective-permute-start.3 = (bf16[512,512]{1,0:T(8,128)(2,1)S(1)}, bf16[512,512]{1,0:T(8,128)(2,1)S(1)}, u32[]{:S(2)}, u32[]{:S(2)}) collective-permute-start(bf16[512,512]{1,0:T(8,128)(2,1)S(1)} %collective-permute-done.2.up_ref), channel_id=1, source_target_pairs={{0,224},{32,0},{64,32},{96,64},{128,96},{160,128},{192,160},{224,1... | collective-permute-start | bytes 1572872 | tf_op jit(solution)/shard_map/ppermute | solution.py:152
  44.1 0.0 collective-permute-done.5.down_ref
  44.1 0.0 collective-permute-start.6
  44.1 0.4 collective-permute-done.9
  44.5 0.0 collective-permute-done.8.refs_3_
  44.5 2.7 %collective-permute-start.10 = (bf16[1024,512]{1,0:T(8,128)(2,1)S(1)}, bf16[1024,512]{1,0:T(8,128)(2,1)S(1)}, u32[]{:S(2)}, u32[]{:S(2)}) collective-permute-start(bf16[1024,512]{1,0:T(8,128)(2,1)S(1)} %constant_dynamic-update-slice_fusion.refs_5_), channel_id=1, source_target_pairs={{0,12},{1,5},{2,6},{3,15},{4,0},{5,9},{6,10},{7,3},{8,4},{9,13},{1... | collective-permute-start | bytes 3145736 | tf_op jit(solution)/shard_map/ppermute | solution.py:144
  47.2 0.1 shard_map.30._
  47.3 1.3 %collective-permute-start.13 = (bf16[1024,512]{1,0:T(8,128)(2,1)S(1)}, bf16[1024,512]{1,0:T(8,128)(2,1)S(1)}, u32[]{:S(2)}, u32[]{:S(2)}) collective-permute-start(bf16[1024,512]{1,0:T(8,128)(2,1)S(1)} %collective-permute-done.refs_2_), channel_id=1, source_target_pairs={{0,17},{17,0},{1,16},{16,1},{2,19},{19,2},{3,18},{18,3},{4,21},{21... | collective-permute-start | bytes 3145736 | tf_op jit(solution)/shard_map/ppermute | solution.py:151
  48.6 3.6 %collective-permute-done.3.up_ref = bf16[512,512]{1,0:T(8,128)(2,1)S(1)} collective-permute-done((bf16[512,512]{1,0:T(8,128)(2,1)S(1)}, bf16[512,512]{1,0:T(8,128)(2,1)S(1)}, u32[]{:S(2)}, u32[]{:S(2)}) %collective-permute-start.3) | collective-permute-done | bytes 524320 | tf_op jit(solution)/shard_map/ppermute | solution.py:152
  52.2 3.4 %collective-permute-start.4 = (bf16[512,512]{1,0:T(8,128)(2,1)S(1)}, bf16[512,512]{1,0:T(8,128)(2,1)S(1)}, u32[]{:S(2)}, u32[]{:S(2)}) collective-permute-start(bf16[512,512]{1,0:T(8,128)(2,1)S(1)} %collective-permute-done.3.up_ref), channel_id=1, source_target_pairs={{0,224},{32,0},{64,32},{96,64},{128,96},{160,128},{192,160},{224,1... | collective-permute-start | bytes 1572872 | tf_op jit(solution)/shard_map/ppermute | solution.py:152
  55.6 0.0 collective-permute-done.6.down_ref
  55.6 0.0 collective-permute-start.7
  55.6 2.6 %collective-permute-done.11.refs_4_ = bf16[1024,512]{1,0:T(8,128)(2,1)S(1)} collective-permute-done((bf16[1024,512]{1,0:T(8,128)(2,1)S(1)}, bf16[1024,512]{1,0:T(8,128)(2,1)S(1)}, u32[]{:S(2)}, u32[]{:S(2)}) %collective-permute-start.11) | collective-permute-done | bytes 1048608 | tf_op jit(solution)/shard_map/ppermute | solution.py:150
  58.2 3.7 %collective-permute-done.10.refs_6_ = bf16[1024,512]{1,0:T(8,128)(2,1)S(1)} collective-permute-done((bf16[1024,512]{1,0:T(8,128)(2,1)S(1)}, bf16[1024,512]{1,0:T(8,128)(2,1)S(1)}, u32[]{:S(2)}, u32[]{:S(2)}) %collective-permute-start.10) | collective-permute-done | bytes 1048608 | tf_op jit(solution)/shard_map/ppermute | solution.py:144
  61.8 0.0 collective-permute-start.12
  61.8 0.1 shard_map.31._
  61.9 0.9 collective-permute-done.4.up_ref
  62.8 3.7 %collective-permute-start.14 = (bf16[256,512]{1,0:T(8,128)(2,1)S(1)}, bf16[256,512]{1,0:T(8,128)(2,1)S(1)}, u32[]{:S(2)}, u32[]{:S(2)}) collective-permute-start(bf16[256,512]{1,0:T(8,128)(2,1)S(1)} %slice.24), channel_id=1, source_target_pairs={{0,224},{32,0},{64,32},{96,64},{128,96},{160,128},{192,160},{224,1... | collective-permute-start | bytes 786440 | tf_op jit(solution)/shard_map/ppermute | solution.py:152
  66.5 0.0 collective-permute-done.7.down_ref
  66.5 0.0 copy-start.1
  66.5 0.1 collective-permute-start.15
  66.6 0.1 shard_map.32.refs_0_
  66.7 3.6 %collective-permute-done.13.refs_8_ = bf16[1024,512]{1,0:T(8,128)(2,1)S(1)} collective-permute-done((bf16[1024,512]{1,0:T(8,128)(2,1)S(1)}, bf16[1024,512]{1,0:T(8,128)(2,1)S(1)}, u32[]{:S(2)}, u32[]{:S(2)}) %collective-permute-start.13) | collective-permute-done | bytes 1048608 | tf_op jit(solution)/shard_map/ppermute | solution.py:151
  70.3 6.7 %collective-permute-done.12.refs_7_ = bf16[1024,512]{1,0:T(8,128)(2,1)S(1)} collective-permute-done((bf16[1024,512]{1,0:T(8,128)(2,1)S(1)}, bf16[1024,512]{1,0:T(8,128)(2,1)S(1)}, u32[]{:S(2)}, u32[]{:S(2)}) %collective-permute-start.12) | collective-permute-done | bytes 1048608 | tf_op jit(solution)/shard_map/ppermute | solution.py:144
  77.0 0.0 copy-done.1
  77.0 5.1 %shard_map.33 = (f32[1024,512]{1,0:T(8,128)S(1)}, bf16[1024,512]{1,0:T(8,128)(2,1)S(1)}) custom-call(s32[8]{0:T(128)S(1)} %stack.44.pos_ref, bf16[8,512,512]{2,1,0:T(8,128)(2,1)S(1)} %shard_map.32.refs_0_, bf16[1024,512]{1,0:T(8,128)(2,1)S(1)} %copy-done.1, bf16[1024,512]{1,0:T(8,128)(2,1)S(1)} %collective-permute-done.refs_2_, ...), custom_call_target="tpu_custom_call" | custom-call | flops 4294967296 | bytes 16777216 | tf_op jit(solution)/shard_map/pallas_call | solution.py:199
  82.1 0.0 collective-permute-done.14.top_ref
  82.2 0.0 collective-permute-done.15.bottom_ref
  82.2 1.1 shard_map.35
  83.3 1.6 %collective-permute-start.16 = (f32[512,512]{1,0:T(8,128)S(1)}, f32[512,512]{1,0:T(8,128)S(1)}, u32[]{:S(2)}, u32[]{:S(2)}) collective-permute-start(f32[512,512]{1,0:T(8,128)S(1)} %shard_map.35), channel_id=1, source_target_pairs={{0,2},{2,0},{1,3},{3,1},{4,6},{6,4},{5,7},{7,5},{8,10},{10,8},{9,1... | collective-permute-start | bytes 3145736 | tf_op jit(solution)/shard_map/ppermute | solution.py:212
  84.8 1.1 shard_map.34.kept_ref
  85.9 1.2 %collective-permute-done.16.got_ref = f32[512,512]{1,0:T(8,128)S(1)} collective-permute-done((f32[512,512]{1,0:T(8,128)S(1)}, f32[512,512]{1,0:T(8,128)S(1)}, u32[]{:S(2)}, u32[]{:S(2)}) %collective-permute-start.16) | collective-permute-done | bytes 1048608 | tf_op jit(solution)/shard_map/ppermute | solution.py:212
  87.1 1.4 %shard_map.36._ = bf16[8,16,2,8,128]{4,3,2,1,0:T(8,128)(2,1)} custom-call(f32[512,512]{1,0:T(8,128)S(1)} %shard_map.34.kept_ref, f32[512,512]{1,0:T(8,128)S(1)} %collective-permute-done.16.got_ref), custom_call_target="tpu_custom_call" | custom-call | bytes 3145728 | tf_op jit(solution)/shard_map/pallas_call | solution.py:214
  88.5 9.3 %all-to-all-start.1 = ((bf16[256,8,128]{2,1,0:T(8,128)(2,1)}), bf16[256,8,128]{2,1,0:T(8,128)(2,1)S(1)}, u32[]{:S(2)}, u32[]{:S(2)}) async-start(bf16[256,8,128]{2,1,0:T(8,128)(2,1)} %bitcast.12), calls=%async_computation.1 | async-start | bytes 1048576 | tf_op jit(solution)/shard_map/all_to_all | solution.py:224
  97.9 0.2 shard_map.37
  98.1 3.5 %collective-permute-start.17 = (bf16[512,512]{1,0:T(8,128)(2,1)S(1)}, bf16[512,512]{1,0:T(8,128)(2,1)S(1)}, u32[]{:S(2)}, u32[]{:S(2)}) collective-permute-start(bf16[512,512]{1,0:T(8,128)(2,1)S(1)} %shard_map.37), channel_id=1, source_target_pairs={{0,0},{1,2},{2,1},{3,3},{4,4},{5,6},{6,5},{7,7},{8,8},{9,10},{10,9... | collective-permute-start | bytes 1572872 | tf_op jit(solution)/shard_map/ppermute | solution.py:223
  101.6 11.0 %collective-permute-done.17.direct_ref = bf16[512,512]{1,0:T(8,128)(2,1)S(1)} collective-permute-done((bf16[512,512]{1,0:T(8,128)(2,1)S(1)}, bf16[512,512]{1,0:T(8,128)(2,1)S(1)}, u32[]{:S(2)}, u32[]{:S(2)}) %collective-permute-start.17) | collective-permute-done | bytes 524320 | tf_op jit(solution)/shard_map/ppermute | solution.py:223
  112.7 5.1 %all-to-all-done.1 = bf16[256,8,128]{2,1,0:T(8,128)(2,1)S(1)} async-done(((bf16[256,8,128]{2,1,0:T(8,128)(2,1)}), bf16[256,8,128]{2,1,0:T(8,128)(2,1)S(1)}, u32[]{:S(2)}, u32[]{:S(2)}) %all-to-all-start.1) | async-done | bytes 524320 | tf_op jit(solution)/shard_map/all_to_all | solution.py:224
  117.7 1.4 %shard_map.38 = f32[512,512]{1,0:T(8,128)} custom-call(bf16[512,512]{1,0:T(8,128)(2,1)S(1)} %collective-permute-done.17.direct_ref, bf16[8,8,2,2,8,128]{5,4,3,2,1,0:T(8,128)(2,1)S(1)} %bitcast.18), custom_call_target="tpu_custom_call" | custom-call | bytes 2097152 | tf_op jit(solution)/shard_map/pallas_call | solution.py:225
  (4 shorter events, 0.1 us)
Async XLA Ops:
  0.2 25.7 %collective-permute-start = (bf16[1024,512]{1,0:T(8,128)(2,1)}, bf16[1024,512]{1,0:T(8,128)(2,1)S(1)}, u32[]{:S(2)}, u32[]{:S(2)}) collective-permute-start(bf16[1024,512]{1,0:T(8,128)(2,1)} %refs_1_), channel_id=1, source_target_pairs={{0,12},{1,5},{2,6},{3,15},{4,0},{5,9},{6,10},{7,3},{8,4},{9,13},{1... | collective-permute-start | bytes 3145736 | tf_op jit(solution)/shard_map/ppermute | solution.py:144
  3.6 22.3 %collective-permute-start.1 = (bf16[512,512]{1,0:T(8,128)(2,1)S(1)}, bf16[512,512]{1,0:T(8,128)(2,1)S(1)}, u32[]{:S(2)}, u32[]{:S(2)}) collective-permute-start(bf16[512,512]{1,0:T(8,128)(2,1)S(1)} %get-tuple-element.36), channel_id=1, source_target_pairs={{0,17},{17,0},{1,16},{16,1},{2,19},{19,2},{3,18},{18,3},{4,21},{21... | collective-permute-start | bytes 1572872 | tf_op jit(solution)/shard_map/ppermute | solution.py:151
  7.6 1.2 %copy-start = (bf16[1024,512]{1,0:T(8,128)(2,1)S(1)}, bf16[1024,512]{1,0:T(8,128)(2,1)}, u32[]{:S(2)}) copy-start(bf16[1024,512]{1,0:T(8,128)(2,1)} %w_ref) | copy-start | bytes 3145732
  25.9 18.6 %collective-permute-start.8 = (bf16[1024,512]{1,0:T(8,128)(2,1)S(1)}, bf16[1024,512]{1,0:T(8,128)(2,1)S(1)}, u32[]{:S(2)}, u32[]{:S(2)}) collective-permute-start(bf16[1024,512]{1,0:T(8,128)(2,1)S(1)} %collective-permute-done.refs_2_), channel_id=1, source_target_pairs={{0,12},{1,5},{2,6},{3,15},{4,0},{5,9},{6,10},{7,3},{8,4},{9,13},{1... | collective-permute-start | bytes 3145736 | tf_op jit(solution)/shard_map/ppermute | solution.py:144
  26.0 14.7 %collective-permute-start.2 = (bf16[512,512]{1,0:T(8,128)(2,1)S(1)}, bf16[512,512]{1,0:T(8,128)(2,1)S(1)}, u32[]{:S(2)}, u32[]{:S(2)}) collective-permute-start(bf16[512,512]{1,0:T(8,128)(2,1)S(1)} %shard_map.29.own_ref), channel_id=1, source_target_pairs={{0,224},{32,0},{64,32},{96,64},{128,96},{160,128},{192,160},{224,1... | collective-permute-start | bytes 1572872 | tf_op jit(solution)/shard_map/ppermute | solution.py:152
  31.6 12.5 %collective-permute-start.5 = (bf16[512,512]{1,0:T(8,128)(2,1)S(1)}, bf16[512,512]{1,0:T(8,128)(2,1)S(1)}, u32[]{:S(2)}, u32[]{:S(2)}) collective-permute-start(bf16[512,512]{1,0:T(8,128)(2,1)S(1)} %shard_map.29.own_ref), channel_id=1, source_target_pairs={{0,32},{32,64},{64,96},{96,128},{128,160},{160,192},{192,224},{224... | collective-permute-start | bytes 1572872 | tf_op jit(solution)/shard_map/ppermute | solution.py:153
  31.6 12.9 %collective-permute-start.9 = (bf16[512,512]{1,0:T(8,128)(2,1)S(1)}, bf16[512,512]{1,0:T(8,128)(2,1)S(1)}, u32[]{:S(2)}, u32[]{:S(2)}) collective-permute-start(bf16[512,512]{1,0:T(8,128)(2,1)S(1)} %get-tuple-element.35), channel_id=1, source_target_pairs={{0,17},{17,0},{1,16},{16,1},{2,19},{19,2},{3,18},{18,3},{4,21},{21... | collective-permute-start | bytes 1572872 | tf_op jit(solution)/shard_map/ppermute | solution.py:151
  34.5 23.7 %collective-permute-start.11 = (bf16[1024,512]{1,0:T(8,128)(2,1)S(1)}, bf16[1024,512]{1,0:T(8,128)(2,1)S(1)}, u32[]{:S(2)}, u32[]{:S(2)}) collective-permute-start(bf16[1024,512]{1,0:T(8,128)(2,1)S(1)} %collective-permute-done.refs_2_), channel_id=1, source_target_pairs={{0,1},{1,0},{16,17},{17,16},{2,3},{3,2},{18,19},{19,18},{4,5},{5,4... | collective-permute-start | bytes 3145736 | tf_op jit(solution)/shard_map/ppermute | solution.py:150
  40.7 11.5 %collective-permute-start.3 = (bf16[512,512]{1,0:T(8,128)(2,1)S(1)}, bf16[512,512]{1,0:T(8,128)(2,1)S(1)}, u32[]{:S(2)}, u32[]{:S(2)}) collective-permute-start(bf16[512,512]{1,0:T(8,128)(2,1)S(1)} %collective-permute-done.2.up_ref), channel_id=1, source_target_pairs={{0,224},{32,0},{64,32},{96,64},{128,96},{160,128},{192,160},{224,1... | collective-permute-start | bytes 1572872 | tf_op jit(solution)/shard_map/ppermute | solution.py:152
  44.1 11.5 %collective-permute-start.6 = (bf16[512,512]{1,0:T(8,128)(2,1)S(1)}, bf16[512,512]{1,0:T(8,128)(2,1)S(1)}, u32[]{:S(2)}, u32[]{:S(2)}) collective-permute-start(bf16[512,512]{1,0:T(8,128)(2,1)S(1)} %collective-permute-done.5.down_ref), channel_id=1, source_target_pairs={{0,32},{32,64},{64,96},{96,128},{128,160},{160,192},{192,224},{224... | collective-permute-start | bytes 1572872 | tf_op jit(solution)/shard_map/ppermute | solution.py:153
  44.5 17.3 %collective-permute-start.10 = (bf16[1024,512]{1,0:T(8,128)(2,1)S(1)}, bf16[1024,512]{1,0:T(8,128)(2,1)S(1)}, u32[]{:S(2)}, u32[]{:S(2)}) collective-permute-start(bf16[1024,512]{1,0:T(8,128)(2,1)S(1)} %constant_dynamic-update-slice_fusion.refs_5_), channel_id=1, source_target_pairs={{0,12},{1,5},{2,6},{3,15},{4,0},{5,9},{6,10},{7,3},{8,4},{9,13},{1... | collective-permute-start | bytes 3145736 | tf_op jit(solution)/shard_map/ppermute | solution.py:144
  47.3 23.0 %collective-permute-start.13 = (bf16[1024,512]{1,0:T(8,128)(2,1)S(1)}, bf16[1024,512]{1,0:T(8,128)(2,1)S(1)}, u32[]{:S(2)}, u32[]{:S(2)}) collective-permute-start(bf16[1024,512]{1,0:T(8,128)(2,1)S(1)} %collective-permute-done.refs_2_), channel_id=1, source_target_pairs={{0,17},{17,0},{1,16},{16,1},{2,19},{19,2},{3,18},{18,3},{4,21},{21... | collective-permute-start | bytes 3145736 | tf_op jit(solution)/shard_map/ppermute | solution.py:151
  52.2 10.6 %collective-permute-start.4 = (bf16[512,512]{1,0:T(8,128)(2,1)S(1)}, bf16[512,512]{1,0:T(8,128)(2,1)S(1)}, u32[]{:S(2)}, u32[]{:S(2)}) collective-permute-start(bf16[512,512]{1,0:T(8,128)(2,1)S(1)} %collective-permute-done.3.up_ref), channel_id=1, source_target_pairs={{0,224},{32,0},{64,32},{96,64},{128,96},{160,128},{192,160},{224,1... | collective-permute-start | bytes 1572872 | tf_op jit(solution)/shard_map/ppermute | solution.py:152
  55.6 10.9 %collective-permute-start.7 = (bf16[512,512]{1,0:T(8,128)(2,1)S(1)}, bf16[512,512]{1,0:T(8,128)(2,1)S(1)}, u32[]{:S(2)}, u32[]{:S(2)}) collective-permute-start(bf16[512,512]{1,0:T(8,128)(2,1)S(1)} %collective-permute-done.6.down_ref), channel_id=1, source_target_pairs={{0,32},{32,64},{64,96},{96,128},{128,160},{160,192},{192,224},{224... | collective-permute-start | bytes 1572872 | tf_op jit(solution)/shard_map/ppermute | solution.py:153
  61.8 15.2 %collective-permute-start.12 = (bf16[1024,512]{1,0:T(8,128)(2,1)S(1)}, bf16[1024,512]{1,0:T(8,128)(2,1)S(1)}, u32[]{:S(2)}, u32[]{:S(2)}) collective-permute-start(bf16[1024,512]{1,0:T(8,128)(2,1)S(1)} %collective-permute-done.10.refs_6_), channel_id=1, source_target_pairs={{0,12},{1,5},{2,6},{3,15},{4,0},{5,9},{6,10},{7,3},{8,4},{9,13},{1... | collective-permute-start | bytes 3145736 | tf_op jit(solution)/shard_map/ppermute | solution.py:144
  62.8 19.3 %collective-permute-start.14 = (bf16[256,512]{1,0:T(8,128)(2,1)S(1)}, bf16[256,512]{1,0:T(8,128)(2,1)S(1)}, u32[]{:S(2)}, u32[]{:S(2)}) collective-permute-start(bf16[256,512]{1,0:T(8,128)(2,1)S(1)} %slice.24), channel_id=1, source_target_pairs={{0,224},{32,0},{64,32},{96,64},{128,96},{160,128},{192,160},{224,1... | collective-permute-start | bytes 786440 | tf_op jit(solution)/shard_map/ppermute | solution.py:152
  66.5 10.5 %copy-start.1 = (bf16[1024,512]{1,0:T(8,128)(2,1)S(1)}, bf16[1024,512]{1,0:T(8,128)(2,1)}, u32[]{:S(2)}) copy-start(bf16[1024,512]{1,0:T(8,128)(2,1)} %refs_1_) | copy-start | bytes 3145732
  66.5 15.6 %collective-permute-start.15 = (bf16[256,512]{1,0:T(8,128)(2,1)S(1)}, bf16[256,512]{1,0:T(8,128)(2,1)S(1)}, u32[]{:S(2)}, u32[]{:S(2)}) collective-permute-start(bf16[256,512]{1,0:T(8,128)(2,1)S(1)} %slice.25), channel_id=1, source_target_pairs={{0,32},{32,64},{64,96},{96,128},{128,160},{160,192},{192,224},{224... | collective-permute-start | bytes 786440 | tf_op jit(solution)/shard_map/ppermute | solution.py:153
  83.3 3.9 %collective-permute-start.16 = (f32[512,512]{1,0:T(8,128)S(1)}, f32[512,512]{1,0:T(8,128)S(1)}, u32[]{:S(2)}, u32[]{:S(2)}) collective-permute-start(f32[512,512]{1,0:T(8,128)S(1)} %shard_map.35), channel_id=1, source_target_pairs={{0,2},{2,0},{1,3},{3,1},{4,6},{6,4},{5,7},{7,5},{8,10},{10,8},{9,1... | collective-permute-start | bytes 3145736 | tf_op jit(solution)/shard_map/ppermute | solution.py:212
  88.5 29.2 %all-to-all-start.1 = ((bf16[256,8,128]{2,1,0:T(8,128)(2,1)}), bf16[256,8,128]{2,1,0:T(8,128)(2,1)S(1)}, u32[]{:S(2)}, u32[]{:S(2)}) async-start(bf16[256,8,128]{2,1,0:T(8,128)(2,1)} %bitcast.12), calls=%async_computation.1 | async-start | bytes 1048576 | tf_op jit(solution)/shard_map/all_to_all | solution.py:224
  98.1 14.6 %collective-permute-start.17 = (bf16[512,512]{1,0:T(8,128)(2,1)S(1)}, bf16[512,512]{1,0:T(8,128)(2,1)S(1)}, u32[]{:S(2)}, u32[]{:S(2)}) collective-permute-start(bf16[512,512]{1,0:T(8,128)(2,1)S(1)} %shard_map.37), channel_id=1, source_target_pairs={{0,0},{1,2},{2,1},{3,3},{4,4},{5,6},{6,5},{7,7},{8,8},{9,10},{10,9... | collective-permute-start | bytes 1572872 | tf_op jit(solution)/shard_map/ppermute | solution.py:223
